TPU v7x, 128 devices: a whole 4x4x4 slice. The times are simulated.
128 devices in a mesh: row: 16 (over x_hi, y, core), col: 8 (over x_lo, z).
Axes of the slice: x: 4 (x_hi: 2, x_lo: 2; x = x_hi * 2 + x_lo), y: 4, z: 4, core: 2. Of those that a mesh axis runs over, the one named last changes fastest.
Arguments:
- pair: bfloat16 [384, 384, 128], P('row', 'col'), may hold values from -6 to 6
- gain: float32 [128], replicated, may hold values from 0.1 to 1.9
- projections: bfloat16 [5, 128, 128], replicated, may hold values from -0.5 to 0.5
- bias_weight: bfloat16 [128, 4], replicated, as said below
- valid_len: int32 [1], replicated, may hold values from 192 to 384
- out_cotangent: bfloat16 [384, 384, 128], P('row', 'col'), may hold values from -6 to 6
Outputs:
- attended: bfloat16 [384, 384, 128], P('row', 'col')
- pair_gradient: float32 [384, 384, 128], P('row', 'col')
- projection_grad: float32 [5, 128, 128], replicated
- bias_weight_grad: float32 [128, 4], replicated
- gain_gradient: float32 [128], replicated
Inputs may be any that keep to these rules, and one draw needn't show every extreme that they name: `bias_weight`: scale of the bias projection entries is free; rows are drawn independently.
All inputs are finite; a program needn't handle non-finite values.
Results may differ from a plain program's by a relative error of at most 0.0045.
The roundings to bfloat16 on the way count: a program that leaves them out, or rounds other values in their place, can miss the bound.
Values may be sent and summed in bfloat16 or wider, within the bound.
No kernel may reach another device: no remote copies, remote signals or barrier semaphores. Data moves between devices by JAX's collectives and lax.ppermute only.
A program may use at most 64 MiB of HBM per device.

v0:
```python
import jax
import jax.numpy as jnp
from jax import lax
from jax.sharding import Mesh
from jax.sharding import PartitionSpec as P

QB = 384
ROW = ("row_0", "row_1", "row_2")
COL = ("col_0", "col_1")
ROW_COL = ("row_0", "row_1", "row_2", "col_0", "col_1")


EPS = 1e-05


def piece_ends(length, count):
    unit = 8 if length >= 8 * count else 1
    return [length // unit * k // count * unit for k in range(1, count)]


def stacked_from(value, axes, sequence):
    parts = value[None]
    for k in sequence:
        parts = lax.all_gather(parts, axes[k], axis=0, tiled=True)
    current = [lax.axis_size(axes[k]) for k in reversed(sequence)]
    parts = parts.reshape(*current, *value.shape)
    turned = sorted(range(len(sequence)), key=lambda place: sequence[len(sequence) - 1 - place])
    return parts.transpose(*turned, *range(len(sequence), parts.ndim)).reshape(-1, *value.shape)


def in_order(parts, dim):
    parts = jnp.moveaxis(parts, 0, dim)
    shape = parts.shape
    return parts.reshape(*shape[:dim], shape[dim] * shape[dim + 1], *shape[dim + 2 :])


def gather_all_axes(value, axes, dim):
    widest = max(range(max(1, value.ndim - 1)), key=lambda d: value.shape[d])
    count, gathered = (len(axes), [])
    for leading, piece in enumerate(
        jnp.split(value, piece_ends(value.shape[widest], count), axis=widest)
    ):
        if piece.size:
            sequence = [(leading - k) % count for k in range(count)]
            gathered.append(stacked_from(piece, axes, sequence))
    return in_order(jnp.concatenate(gathered, axis=widest + 1), dim)


def in_one_piece(arrays, axis, split_dim, concat_dim, along):
    ends, at = ([], 0)
    for a in arrays[:-1]:
        at += a.shape[along]
        ends.append(at)
    both = jnp.concatenate(arrays, axis=along)
    return tuple(
        jnp.split(
            lax.all_to_all(both, axis, split_axis=split_dim, concat_axis=concat_dim, tiled=True),
            ends,
            axis=along,
        )
    )


def split_up(value, dim, devices):
    shape = value.shape
    parts = value.reshape(*shape[:dim], devices, shape[dim] // devices, *shape[dim + 1 :])
    return jnp.moveaxis(parts, dim, 0)


def summed_on_arrival(value, axis, dim):
    parts = split_up(value, dim, lax.axis_size(axis))
    arrived = lax.all_to_all(parts, axis, split_axis=0, concat_axis=0, tiled=True)
    return arrived.sum(axis=0)


def dense(left, right):
    return jnp.einsum("abc,cd->abd", left, right, preferred_element_type=jnp.float32)


def outer_sum(left, right):
    return jnp.einsum("abc,abd->cd", left, right, preferred_element_type=jnp.float32)


def attend_forward(query, key, value, bias_blocks, keep):
    ncols, rows, heads, width = query.shape
    nblocks = bias_blocks.shape[0]
    scale = width ** (-0.5)

    def per_column(cols):
        qcol, kcol, vcol = cols

        def per_block(blk):
            qblk, bblk = blk
            scores = (
                jnp.einsum("qhd,khd->hqk", qblk, kcol, preferred_element_type=jnp.float32) * scale
                + bblk
            )
            scores = jnp.where(keep[None, None, :], scores, -1000000000.0)
            probs = jax.nn.softmax(scores, axis=-1)
            out = jnp.einsum(
                "hqk,khd->qhd", probs.astype(jnp.bfloat16), vcol, preferred_element_type=jnp.float32
            )
            return out.astype(jnp.bfloat16)

        return lax.map(
            per_block, (qcol.reshape(nblocks, rows // nblocks, heads, width), bias_blocks)
        ).reshape(rows, heads, width)

    return lax.map(per_column, (query, key, value))


def attend_backward(query, key, value, d_context, bias_blocks, keep):
    ncols, rows, heads, width = query.shape
    nblocks = bias_blocks.shape[0]
    qsize = rows // nblocks
    scale = width ** (-0.5)

    def per_column(total, cols):
        qcol, kcol, vcol, dcol = cols

        def per_block(carry, blk):
            dk_acc, dv_acc = carry
            qblk, dblk, bblk = blk
            scores = (
                jnp.einsum("qhd,khd->hqk", qblk, kcol, preferred_element_type=jnp.float32) * scale
                + bblk
            )
            scores = jnp.where(keep[None, None, :], scores, -1000000000.0)
            probs = jax.nn.softmax(scores, axis=-1)
            weights_b = probs.astype(jnp.bfloat16)
            d_probs = jnp.einsum("qhd,khd->hqk", dblk, vcol, preferred_element_type=jnp.float32)
            d_scores = probs * (d_probs - jnp.sum(probs * d_probs, axis=-1, keepdims=True))
            dsb = d_scores.astype(jnp.bfloat16)
            dq = (
                jnp.einsum("hqk,khd->qhd", dsb, kcol, preferred_element_type=jnp.float32) * scale
            ).astype(jnp.bfloat16)
            dk_acc = (
                dk_acc
                + jnp.einsum("hqk,qhd->khd", dsb, qblk, preferred_element_type=jnp.float32) * scale
            )
            dv_acc = dv_acc + jnp.einsum(
                "hqk,qhd->khd", weights_b, dblk, preferred_element_type=jnp.float32
            )
            return ((dk_acc, dv_acc), (dq, d_scores))

        zeros = jnp.zeros((rows, heads, width), jnp.float32)
        (dk, dv), (dq, dscores) = lax.scan(
            per_block,
            (zeros, zeros),
            (
                qcol.reshape(nblocks, qsize, heads, width),
                dcol.reshape(nblocks, qsize, heads, width),
                bias_blocks,
            ),
        )
        return (
            total + dscores,
            (dq.reshape(rows, heads, width), dk.astype(jnp.bfloat16), dv.astype(jnp.bfloat16)),
        )

    start = jnp.zeros(bias_blocks.shape, jnp.float32)
    total, (dq, dk, dv) = lax.scan(per_column, start, (query, key, value, d_context))
    return (dq, dk, dv, total)


def arrange_bias(gathered, n_row, n_col, rows):
    heads, tile_rows, tile_cols = (gathered.shape[1], gathered.shape[2], gathered.shape[3])
    grid = gathered.reshape(n_row, n_col, heads, tile_rows, tile_cols)
    bias_t = jnp.transpose(grid, (2, 1, 4, 0, 3)).reshape(heads, rows, rows)
    return bias_t.reshape(heads, rows // QB, QB, rows).transpose(1, 0, 2, 3)


def shards(pair, gain, projections, bias_weight, valid_len, out_cotangent):
    n_row = lax.axis_size(ROW)
    n_col = lax.axis_size(COL)
    tile_rows, tile_cols, channels = pair.shape
    rows = tile_rows * n_row
    heads = bias_weight.shape[1]
    width = channels // heads
    ncols = tile_cols // n_row
    pair_float = pair.astype(jnp.float32)
    average_value = jnp.mean(pair_float, axis=-1, keepdims=True)
    var = jnp.mean((pair_float - average_value) ** 2, axis=-1, keepdims=True)
    inverse_deviation = lax.rsqrt(var + EPS)
    centered_scaled = (pair_float - average_value) * inverse_deviation
    normalized_pair = (centered_scaled * gain).astype(jnp.bfloat16)
    bias_tile = jnp.einsum(
        "abc,ch->hab", normalized_pair, bias_weight, preferred_element_type=jnp.float32
    )
    gathered = gather_all_axes(bias_tile[None], ROW_COL, 0)
    bias_blocks = arrange_bias(gathered, n_row, n_col, rows)
    keep = jnp.arange(rows, dtype=jnp.int32) < valid_len[0]

    def split(tensor):
        return jnp.moveaxis(tensor, 1, 0).reshape(ncols, rows, heads, width)

    def join(tensor):
        return jnp.moveaxis(tensor.reshape(ncols, rows, channels), 0, 1)

    normed_cols, cot_cols = in_one_piece((normalized_pair, out_cotangent), ROW, 1, 0, 2)
    query = dense(normed_cols, projections[0]).astype(jnp.bfloat16)
    key = dense(normed_cols, projections[1]).astype(jnp.bfloat16)
    value = dense(normed_cols, projections[2]).astype(jnp.bfloat16)
    gate = jax.nn.sigmoid(dense(normed_cols, projections[3]))
    qcols, kcols, vcols = (split(query), split(key), split(value))
    context = join(attend_forward(qcols, kcols, vcols, bias_blocks, keep))
    gated = (gate * context.astype(jnp.float32)).astype(jnp.bfloat16)
    attended_cols = dense(gated, projections[4]).astype(jnp.bfloat16)
    attended = lax.all_to_all(attended_cols, ROW, split_axis=0, concat_axis=1, tiled=True)
    d_gated = dense(cot_cols, projections[4].T)
    d_context_cols = (d_gated * gate).astype(jnp.bfloat16)
    d_gate_pre = (d_gated * context.astype(jnp.float32) * gate * (1.0 - gate)).astype(jnp.bfloat16)
    dq, dk, dv, total = attend_backward(
        qcols, kcols, vcols, split(d_context_cols), bias_blocks, keep
    )
    dq, dk, dv = (join(dq), join(dk), join(dv))
    grid = total.transpose(1, 0, 2, 3).reshape(heads, n_col, tile_cols, n_row, tile_rows)
    grid = jnp.transpose(grid, (3, 1, 0, 4, 2))
    column_part = summed_on_arrival(grid, COL, 1)
    d_bias = summed_on_arrival(column_part, ROW, 0)[0, 0].astype(jnp.bfloat16)
    bias_term = jnp.einsum("hab,ch->abc", d_bias, bias_weight, preferred_element_type=jnp.float32)
    bias_weight_part = jnp.einsum(
        "abc,hab->ch", normalized_pair, d_bias, preferred_element_type=jnp.float32
    )
    d_cols = dense(dq, projections[0].T) + dense(dk, projections[1].T) + dense(dv, projections[2].T)
    d_cols = d_cols + dense(d_gate_pre, projections[3].T)
    parts = jnp.stack(
        [
            outer_sum(normed_cols, dq),
            outer_sum(normed_cols, dk),
            outer_sum(normed_cols, dv),
            outer_sum(normed_cols, d_gate_pre),
            outer_sum(gated, cot_cols),
        ]
    )
    normalized_gradient = (
        lax.all_to_all(d_cols, ROW, split_axis=0, concat_axis=1, tiled=True) + bias_term
    )
    gain_partial_sum = jnp.sum(normalized_gradient * centered_scaled, axis=(0, 1))
    projection_grad, bias_weight_grad, gain_gradient = lax.psum(
        (parts, bias_weight_part, gain_partial_sum), ROW_COL
    )
    scaled_output = normalized_gradient * gain
    pair_gradient = inverse_deviation * (
        scaled_output
        - jnp.mean(scaled_output, axis=-1, keepdims=True)
        - centered_scaled * jnp.mean(scaled_output * centered_scaled, axis=-1, keepdims=True)
    )
    return (attended, pair_gradient, projection_grad, bias_weight_grad, gain_gradient)


def solution(mesh):
    torus = Mesh(mesh.devices.reshape(2, 4, 2, 2, 4), ("row_0", "row_1", "row_2", "col_0", "col_1"))
    in_specs = (P(ROW, COL, None), P(), P(), P(), P(), P(ROW, COL, None))
    out_specs = (P(ROW, COL, None), P(ROW, COL, None), P(), P(), P())
    return jax.shard_map(
        shards, mesh=torus, in_specs=in_specs, out_specs=out_specs, check_vma=False
    )
```

profile of v0, /device:TPU:1, one launch (start us, length us, event | category | flops | bytes accessed | tf_op | source)
XLA Modules:
  0.0 610.2 jit_solution(14113767609708172437)
XLA Ops:
  22.8 11.9 %all-gather.5 = f32[4,4,5,48]{3,1,2,0:T(4,128)S(1)} all-gather(f32[1,4,5,48]{3,1,2,0:T(4,128)S(1)} %get-tuple-element.293), channel_id=7, replica_groups=mesh['row_0'=2,'row_1'=4,'row_2'=2,'col_0'=2,'col_1'=4] {'row_1'}, dimensions={0}, use_global_device_ids=true | all-gather | bytes 19200 | tf_op jit(solution)/shard_map/all_gather | solution.py:24
  41.4 10.7 %all-gather.7 = f32[32,4,5,48]{3,1,2,0:T(4,128)S(1)} all-gather(f32[8,4,5,48]{3,1,2,0:T(4,128)S(1)} %all-gather.6), channel_id=9, replica_groups=mesh['row_0'=2,'row_1'=4,'row_2'=2,'col_0'=2,'col_1'=4] {'col_1'}, dimensions={0}, use_global_device_ids=true | all-gather | bytes 153600 | tf_op jit(solution)/shard_map/all_gather | solution.py:24
  58.7 10.4 %all-gather.9 = f32[128,4,5,48]{3,1,2,0:T(4,128)S(1)} all-gather(f32[64,4,5,48]{3,1,2,0:T(4,128)S(1)} %all-gather.8), channel_id=11, replica_groups=mesh['row_0'=2,'row_1'=4,'row_2'=2,'col_0'=2,'col_1'=4] {'row_2'}, dimensions={0}, use_global_device_ids=true | all-gather | bytes 737280 | tf_op jit(solution)/shard_map/all_gather | solution.py:24
  75.1 9.0 %all-gather.1 = f32[8,4,4,48]{3,2,1,0:T(4,128)S(1)} all-gather(f32[2,4,4,48]{3,2,1,0:T(4,128)S(1)} %all-gather), channel_id=3, replica_groups=mesh['row_0'=2,'row_1'=4,'row_2'=2,'col_0'=2,'col_1'=4] {'col_1'}, dimensions={0}, use_global_device_ids=true | all-gather | bytes 30720 | tf_op jit(solution)/shard_map/all_gather | solution.py:24
  94.8 12.4 %all-gather.4 = f32[128,4,4,48]{3,2,1,0:T(4,128)S(1)} all-gather(f32[32,4,4,48]{3,2,1,0:T(4,128)S(1)} %all-gather.3), channel_id=6, replica_groups=mesh['row_0'=2,'row_1'=4,'row_2'=2,'col_0'=2,'col_1'=4] {'row_1'}, dimensions={0}, use_global_device_ids=true | all-gather | bytes 491520 | tf_op jit(solution)/shard_map/all_gather | solution.py:24
  112.9 9.0 %all-gather.11 = f32[8,4,5,48]{3,1,2,0:T(4,128)S(1)} all-gather(f32[2,4,5,48]{3,1,2,0:T(4,128)S(1)} %all-gather.10), channel_id=13, replica_groups=mesh['row_0'=2,'row_1'=4,'row_2'=2,'col_0'=2,'col_1'=4] {'row_1'}, dimensions={0}, use_global_device_ids=true | all-gather | bytes 38400 | tf_op jit(solution)/shard_map/all_gather | solution.py:24
  127.7 10.6 %all-gather.13 = f32[64,4,5,48]{3,1,2,0:T(4,128)S(1)} all-gather(f32[16,4,5,48]{3,1,2,0:T(4,128)S(1)} %all-gather.12), channel_id=15, replica_groups=mesh['row_0'=2,'row_1'=4,'row_2'=2,'col_0'=2,'col_1'=4] {'col_1'}, dimensions={0}, use_global_device_ids=true | all-gather | bytes 307200 | tf_op jit(solution)/shard_map/all_gather | solution.py:24
  138.3 10.1 %all-gather.14 = f32[128,4,5,48]{3,1,2,0:T(4,128)S(1)} all-gather(f32[64,4,5,48]{3,1,2,0:T(4,128)S(1)} %all-gather.13), channel_id=16, replica_groups=mesh['row_0'=2,'row_1'=4,'row_2'=2,'col_0'=2,'col_1'=4] {'col_0'}, dimensions={0}, use_global_device_ids=true | all-gather | bytes 737280 | tf_op jit(solution)/shard_map/all_gather | solution.py:24
  152.9 10.6 %all-gather.16 = f32[4,4,5,48]{3,1,2,0:T(4,128)S(1)} all-gather(f32[2,4,5,48]{3,1,2,0:T(4,128)S(1)} %all-gather.15), channel_id=18, replica_groups=mesh['row_0'=2,'row_1'=4,'row_2'=2,'col_0'=2,'col_1'=4] {'row_2'}, dimensions={0}, use_global_device_ids=true | all-gather | bytes 23040 | tf_op jit(solution)/shard_map/all_gather | solution.py:24
  163.5 9.2 %all-gather.17 = f32[16,4,5,48]{3,1,2,0:T(4,128)S(1)} all-gather(f32[4,4,5,48]{3,1,2,0:T(4,128)S(1)} %all-gather.16), channel_id=19, replica_groups=mesh['row_0'=2,'row_1'=4,'row_2'=2,'col_0'=2,'col_1'=4] {'row_1'}, dimensions={0}, use_global_device_ids=true | all-gather | bytes 76800 | tf_op jit(solution)/shard_map/all_gather | solution.py:24
  179.4 13.5 %all-gather.19 = f32[128,4,5,48]{3,1,2,0:T(4,128)S(1)} all-gather(f32[32,4,5,48]{3,1,2,0:T(4,128)S(1)} %all-gather.18), channel_id=21, replica_groups=mesh['row_0'=2,'row_1'=4,'row_2'=2,'col_0'=2,'col_1'=4] {'col_1'}, dimensions={0}, use_global_device_ids=true | all-gather | bytes 614400 | tf_op jit(solution)/shard_map/all_gather | solution.py:24
  193.7 9.3 %all-gather.20 = f32[4,4,5,48]{3,1,2,0:T(4,128)S(1)} all-gather(f32[1,4,5,48]{3,1,2,0:T(4,128)S(1)} %get-tuple-element.290), channel_id=22, replica_groups=mesh['row_0'=2,'row_1'=4,'row_2'=2,'col_0'=2,'col_1'=4] {'col_1'}, dimensions={0}, use_global_device_ids=true | all-gather | bytes 19200 | tf_op jit(solution)/shard_map/all_gather | solution.py:24
  206.5 12.1 %all-gather.22 = f32[16,4,5,48]{3,1,2,0:T(4,128)S(1)} all-gather(f32[8,4,5,48]{3,1,2,0:T(4,128)S(1)} %all-gather.21), channel_id=24, replica_groups=mesh['row_0'=2,'row_1'=4,'row_2'=2,'col_0'=2,'col_1'=4] {'row_2'}, dimensions={0}, use_global_device_ids=true | all-gather | bytes 92160 | tf_op jit(solution)/shard_map/all_gather | solution.py:24
  218.5 10.5 %all-gather.23 = f32[64,4,5,48]{3,1,2,0:T(4,128)S(1)} all-gather(f32[16,4,5,48]{3,1,2,0:T(4,128)S(1)} %all-gather.22), channel_id=25, replica_groups=mesh['row_0'=2,'row_1'=4,'row_2'=2,'col_0'=2,'col_1'=4] {'row_1'}, dimensions={0}, use_global_device_ids=true | all-gather | bytes 307200 | tf_op jit(solution)/shard_map/all_gather | solution.py:24
  229.4 15.6 %all-gather.24 = f32[128,4,5,48]{3,1,2,0:T(4,128)S(1)} all-gather(f32[64,4,5,48]{3,1,2,0:T(4,128)S(1)} %all-gather.23), channel_id=26, replica_groups=mesh['row_0'=2,'row_1'=4,'row_2'=2,'col_0'=2,'col_1'=4] {'row_0'}, dimensions={0}, use_global_device_ids=true | all-gather | bytes 737280 | tf_op jit(solution)/shard_map/all_gather | solution.py:24
  259.7 22.7 %while.28 = (s32[]{:T(128)}, bf16[3,384,4,32]{1,3,2,0:T(8,128)(2,1)}, bf16[3,384,4,32]{1,3,2,0:T(8,128)(2,1)}, bf16[3,384,4,32]{1,3,2,0:T(8,128)(2,1)S(1)}, bf16...) while((s32[]{:T(128)}, ...), condition=%wide.region_5.6_spmd.clone, body=%wide.region_2.5_spmd.clone.sunk | while | flops 119786112 | bytes 12403161 | solution.py:109
  287.6 9.9 %all-to-all-start.1 = ((bf16[384,3,128]{2,1,0:T(4,128)(2,1)}), bf16[384,3,128]{2,1,0:T(4,128)(2,1)}, u32[]{:S(2)}, u32[]{:S(2)}) async-start(bf16[384,3,128]{2,1,0:T(4,128)(2,1)} %copy.209), calls=%async_computation.1 | async-start | bytes 786432 | tf_op jit(solution)/shard_map/all_to_all | solution.py:209
  299.8 50.9 %while.29 = (s32[]{:T(128)}, f32[1,4,384,384]{2,3,1,0:T(8,128)}, bf16[3,384,4,32]{1,3,2,0:T(8,128)(2,1)}, bf16[3,384,4,32]{1,3,2,0:T(8,128)(2,1)}, bf16[3,384,4,...) while((s32[]{:T(128)}, f32[1,4,384,384]{2,3,1,0:T(8,128)}, ...), condition=%wide.region_10.11_spmd.clone, body=%wide.region_6.10_spmd.clone.sunk | while | flops 240305280 | bytes 59063928 | solution.py:162
  363.2 9.5 %reshape.162 = f32[8,1,73728]{2,1,0:T(1,128)} reshape(f32[8,1,4,16,24,48]{5,4,3,2,1,0:T(8,128)} %bitcast.347) | data formatting | bytes 4718592
  372.7 13.2 %all-to-all-start.3 = ((f32[8,1,73728]{2,1,0:T(1,128)}), f32[8,1,73728]{2,1,0:T(1,128)S(1)}, u32[]{:S(2)}, u32[]{:S(2)}) async-start(f32[8,1,73728]{2,1,0:T(1,128)} %reshape.162), calls=%async_computation.3 | async-start | bytes 4718592 | tf_op jit(solution)/shard_map/all_to_all | solution.py:72
  397.6 17.1 %all-to-all-done.3 = f32[8,1,73728]{2,1,0:T(1,128)S(1)} async-done(((f32[8,1,73728]{2,1,0:T(1,128)}), f32[8,1,73728]{2,1,0:T(1,128)S(1)}, u32[]{:S(2)}, u32[]{:S(2)}) %all-to-all-start.3) | async-done | bytes 2359328 | tf_op jit(solution)/shard_map/all_to_all | solution.py:72
  424.1 8.7 %reduce.2 = f32[8,73728]{1,0:T(8,128)} reduce(f32[8,1,73728]{2,1,0:T(1,128)S(1)} %all-to-all-done.3, f32[]{:T(128)} %broadcast.112), dimensions={1}, to_apply=%all_to_all.57.reduce_sub_computation | reduce | bytes 4718596 | tf_op jit(solution)/shard_map/all_to_all | solution.py:72
  463.6 64.0 %all-reduce = (f32[128,4]{0,1:T(4,128)}, f32[128]{0:T(128)}) all-reduce(f32[128,4]{0,1:T(4,128)S(1)} %convolution_bitcast_fusion.6, f32[128]{0:T(128)S(1)} %get-tuple-element.242), channel_id=1, replica_groups=mesh['row_0'=2,'row_1'=4,'row_2'=2,'col_0'=2,'col_1'=4] {'row_0','row_1'..., use_global_device_ids=true, to_apply=%region_16.17 | all-reduce | flops 640 | bytes 5120 | tf_op jit(solution)/shard_map/psum | solution.py:240
  529.1 72.3 %all-reduce.3.cloned.1.call-done = f32[5,128,128]{2,1,0:T(8,128)} async-done(((f32[5,128,128]{2,1,0:T(8,128)}), f32[5,128,128]{2,1,0:T(8,128)}) %all-reduce.3.cloned.1.call-update) | async-done | bytes 327696 | tf_op jit(solution)/shard_map/psum | solution.py:240
  (175 shorter events, 235.8 us)
Async XLA Ops:
  7.2 15.2 %copy-start = (bf16[128,4]{0,1:T(4,128)(2,1)S(1)}, bf16[128,4]{0,1:T(4,128)(2,1)}, u32[]{:S(2)}) copy-start(bf16[128,4]{0,1:T(4,128)(2,1)} %param.13) | copy-start | bytes 3076
  8.4 1.4 copy-start.13
  11.7 46.9 %copy-start.6 = (bf16[24,48,128]{2,1,0:T(8,128)(2,1)}, bf16[24,48,128]{2,1,0:T(8,128)(2,1)S(1)}, u32[]{:S(2)}) copy-start(bf16[24,48,128]{2,1,0:T(8,128)(2,1)S(1)} %fusion.89) | copy-start | bytes 884740
  13.9 239.3 %all-to-all-start = ((bf16[24,48,256]{2,0,1:T(8,128)(2,1)}), bf16[24,48,256]{2,0,1:T(8,128)(2,1)S(1)}, u32[]{:S(2)}, u32[]{:S(2)}) async-start(bf16[24,48,256]{2,0,1:T(8,128)(2,1)} %copy.194), calls=%async_computation | async-start | bytes 1179648 | tf_op jit(solution)/shard_map/all_to_all | solution.py:57
  287.6 85.1 %all-to-all-start.1 = ((bf16[384,3,128]{2,1,0:T(4,128)(2,1)}), bf16[384,3,128]{2,1,0:T(4,128)(2,1)}, u32[]{:S(2)}, u32[]{:S(2)}) async-start(bf16[384,3,128]{2,1,0:T(4,128)(2,1)} %copy.209), calls=%async_computation.1 | async-start | bytes 786432 | tf_op jit(solution)/shard_map/all_to_all | solution.py:209
  299.8 1.4 copy-start.1
  312.6 3.7 copy-start.2
  316.3 1.4 copy-start.1
  329.8 3.7 copy-start.2
  333.5 1.4 copy-start.1
  347.0 3.7 copy-start.2
  372.7 42.0 %all-to-all-start.3 = ((f32[8,1,73728]{2,1,0:T(1,128)}), f32[8,1,73728]{2,1,0:T(1,128)S(1)}, u32[]{:S(2)}, u32[]{:S(2)}) async-start(f32[8,1,73728]{2,1,0:T(1,128)} %reshape.162), calls=%async_computation.3 | async-start | bytes 4718592 | tf_op jit(solution)/shard_map/all_to_all | solution.py:72
  390.1 3.3 copy-start.10
  392.4 4.3 copy-start.5
  414.7 29.9 %all-to-all-start.2 = ((f32[384,3,128]{2,1,0:T(4,128)}), f32[384,3,128]{2,1,0:T(4,128)}, u32[]{:S(2)}, u32[]{:S(2)}) async-start(f32[384,3,128]{2,1,0:T(4,128)} %copy.220), calls=%async_computation.2 | async-start | bytes 1572864 | tf_op jit(solution)/shard_map/all_to_all | solution.py:237
  443.1 9.0 %copy-start.11 = (bf16[384,3,128]{0,2,1:T(8,128)(2,1)S(1)}, bf16[384,3,128]{0,2,1:T(8,128)(2,1)}, u32[]{:S(2)}) copy-start(bf16[384,3,128]{0,2,1:T(8,128)(2,1)} %get-tuple-element.287) | copy-start | bytes 884740
  443.1 9.9 %copy-start.9 = (bf16[384,3,128]{0,2,1:T(8,128)(2,1)S(1)}, bf16[384,3,128]{0,2,1:T(8,128)(2,1)}, u32[]{:S(2)}) copy-start(bf16[384,3,128]{0,2,1:T(8,128)(2,1)} %copy-done.8) | copy-start | bytes 884740
  444.6 16.1 %all-to-all-start.4 = ((f32[16,1,4608]{2,1,0:T(1,128)}), f32[16,1,4608]{2,1,0:T(1,128)S(1)}, u32[]{:S(2)}, u32[]{:S(2)}) async-start(f32[16,1,4608]{2,1,0:T(1,128)} %reshape.164), calls=%async_computation.4 | async-start | bytes 589824 | tf_op jit(solution)/shard_map/all_to_all | solution.py:72
  451.8 149.5 %all-reduce.3.cloned.1.call-start = ((), (), s32[]{:S(2)}) async-start(), calls=%async_computation.5 | async-start | bytes 655360 | tf_op jit(solution)/shard_map/psum | solution.py:240
  455.7 6.8 %copy-start.7 = (bf16[24,48,128]{2,1,0:T(8,128)(2,1)S(1)}, bf16[24,48,128]{2,1,0:T(8,128)(2,1)}, u32[]{:S(2)}) copy-start(bf16[24,48,128]{2,1,0:T(8,128)(2,1)} %copy-done.6) | copy-start | bytes 884740
  455.7 7.0 %copy-start.4 = (bf16[24,48,128]{2,1,0:T(8,128)(2,1)S(1)}, bf16[24,48,128]{2,1,0:T(8,128)(2,1)}, u32[]{:S(2)}) copy-start(bf16[24,48,128]{2,1,0:T(8,128)(2,1)} %param.10) | copy-start | bytes 884740
  455.7 7.0 %copy-start.14 = (f32[24,48]{1,0:T(8,128)S(1)}, f32[24,48]{1,0:T(8,128)}, u32[]{:S(2)}) copy-start(f32[24,48]{1,0:T(8,128)} %copy-done.13) | copy-start | bytes 13828
  455.7 7.0 %copy-start.16 = (f32[24,48]{1,0:T(8,128)S(1)}, f32[24,48]{1,0:T(8,128)}, u32[]{:S(2)}) copy-start(f32[24,48]{1,0:T(8,128)} %copy-done.15) | copy-start | bytes 13828
  455.7 7.0 %copy-start.17 = (f32[128]{0:T(128)S(1)}, f32[128]{0:T(128)}, u32[]{:S(2)}) copy-start(f32[128]{0:T(128)} %param.11) | copy-start | bytes 1540
  (8 other events, 9.6 us)
Sparse Core Ops, SparseCore 0:
  458.0 143.3 all-reduce.2
where the time goes:
time: 618 us; the launch traced here: 610 us
  blocking collectives  283 us (46%)
  waiting for transfers between devices  93.2 us (15%)
  matrix products  69.9 us (11%)
  local copies, waits for them, and re-layouts  64.8 us (10%)
  starting transfers between devices  47 us (8%)
  other arithmetic  37.9 us (6%)
  between operations  14.7 us (2%)
    all_gather x25, blocking collectives, stacked_from(): parts = lax.all_gather(parts, axes[k], axis=0, tiled=True)  219 us
    psum x1, waiting for transfers between devices, shards(): lax.psum((parts, bias_weight_part, gain_partial_sum), ROW_COL)  72.3 us
    psum x1, blocking collectives, shards(): lax.psum((parts, bias_weight_part, gain_partial_sum), ROW_COL)  64 us
    unnamed x38, local copies, waits for them, and re-layouts  22.6 us
    all_to_all x2, waiting for transfers between devices, summed_on_arrival(): lax.all_to_all(parts, axis, split_axis=0, concat_axis=0, tiled=True)  20.9 us
    all_to_all x2, starting transfers between devices, summed_on_arrival(): lax.all_to_all(parts, axis, split_axis=0, concat_axis=0, tiled=True)  20.4 us
    dot_general x10, matrix products, dense(): jnp.einsum('abc,cd->abd', left, right, preferred_element_type=jnp.float32)  13.4 us
    add x3, other arithmetic, per_column(): total + dscores  12.6 us
  transfers between devices with their start and end apart: 6, of which 3 were waited for; matrix products, arithmetic and copies ran while one was open for 20% of the time, Pallas kernels for 0%

commit v1 on v0

v1 whole, which is shorter than its diff:
```python
import functools

import jax
import jax.numpy as jnp
from jax import lax
from jax.experimental import pallas as pl
from jax.experimental.pallas import tpu as pltpu
from jax.sharding import Mesh
from jax.sharding import PartitionSpec as P

ROW = ("row_0", "row_1", "row_2")
COL = ("col_0", "col_1")
ALL = ROW + COL
EPS = 1e-05
MASKED = -1000000000.0
CHUNK = 128
F32 = jnp.float32
BF16 = jnp.bfloat16


def nn(left, right):
    return lax.dot_general(left, right, (((1,), (0,)), ((), ())), preferred_element_type=F32)


def nt(left, right):
    return lax.dot_general(left, right, (((1,), (1,)), ((), ())), preferred_element_type=F32)


def turned(value):
    return jnp.transpose(value.astype(F32)).astype(value.dtype)


def exchange(value, axes):
    return lax.all_to_all(value, axes, split_axis=0, concat_axis=0, tiled=True)


def attention_kernel(
    heads, valid_ref, normed_ref, cot_ref, bias_ref, w_ref, wt_ref,
    out_ref, dbias_ref, grads_ref, total, ctx_t, dq_t, dk_acc, dv_acc,
):
    column = pl.program_id(0)
    columns = pl.num_programs(0)
    rows, channels = normed_ref.shape
    width = channels // heads
    scale = width ** (-0.5)
    normed = normed_ref[...]
    cot = cot_ref[...]

    @pl.when(column == 0)
    def _():
        total[...] = jnp.zeros_like(total)
        grads_ref[...] = jnp.zeros_like(grads_ref)

    query = nn(normed, w_ref[0]).astype(BF16)
    key = nn(normed, w_ref[1]).astype(BF16)
    value = nn(normed, w_ref[2]).astype(BF16)
    query_t = nt(wt_ref[0], normed).astype(BF16)
    key_t = nt(wt_ref[1], normed).astype(BF16)
    value_t = nt(wt_ref[2], normed).astype(BF16)
    gate_t = jax.nn.sigmoid(nt(wt_ref[3], normed))
    d_gated_t = nt(w_ref[4], cot)
    d_context_t = (d_gated_t * gate_t).astype(BF16)
    d_context = turned(d_context_t)
    keep = lax.broadcasted_iota(jnp.int32, (rows, CHUNK), 0) < valid_ref[0]
    lane = lax.broadcasted_iota(jnp.int32, (rows, channels), 1)
    dk_acc[...] = jnp.zeros_like(dk_acc)
    dv_acc[...] = jnp.zeros_like(dv_acc)
    for head in range(heads):
        mine = (lane >= head * width) & (lane < (head + 1) * width)
        zero = jnp.zeros((rows, channels), BF16)
        key_h = jnp.where(mine, key, zero)
        value_h = jnp.where(mine, value, zero)
        query_h = jnp.where(mine, query, zero)
        d_context_h = jnp.where(mine, d_context, zero)
        part = slice(head * width, (head + 1) * width)
        for at in range(0, rows, CHUNK):
            here = slice(at, at + CHUNK)
            scores = nn(key_h, query_t[:, here]) * scale + bias_ref[head, :, here]
            scores = jnp.where(keep, scores, MASKED)
            top = jnp.max(scores, axis=0, keepdims=True)
            grown = jnp.exp(scores - top)
            probs = grown * (1.0 / jnp.sum(grown, axis=0, keepdims=True))
            weights_b = probs.astype(BF16)
            ctx_t[part, here] = nn(value_t[part, :], weights_b).astype(BF16)
            d_probs = nn(value_h, d_context_t[:, here])
            delta = jnp.sum(probs * d_probs, axis=0, keepdims=True)
            d_scores = probs * (d_probs - delta)
            total[head, :, here] += d_scores
            d_scores_b = d_scores.astype(BF16)
            dq_t[part, here] = (nn(key_t[part, :], d_scores_b) * scale).astype(BF16)
            dk_acc[...] += nn(d_scores_b, query_h[here, :])
            dv_acc[...] += nn(weights_b, d_context_h[here, :])
    context_t = ctx_t[...].astype(F32)
    gated_t = (gate_t * context_t).astype(BF16)
    d_gate_t = (d_gated_t * context_t * gate_t * (1.0 - gate_t)).astype(BF16)
    gated = turned(gated_t)
    d_gate = turned(d_gate_t)
    d_query = turned(dq_t[...])
    d_key = (dk_acc[...] * scale).astype(BF16)
    d_value = dv_acc[...].astype(BF16)
    attended = nn(gated, w_ref[4]).astype(BF16)
    d_normed = nt(d_query, w_ref[0]) + nt(d_key, w_ref[1]) + nt(d_value, w_ref[2])
    d_normed = d_normed + nt(d_gate, w_ref[3])
    out_ref[:, pl.ds(pl.multiple_of(column * channels, channels), channels)] = attended
    second = pl.multiple_of((columns + column) * channels, channels)
    out_ref[:, pl.ds(second, channels)] = d_normed.astype(BF16)
    normed_t = turned(normed)
    grads_ref[0] += nn(normed_t, d_query)
    grads_ref[1] += nn(normed_t, d_key)
    grads_ref[2] += nn(normed_t, d_value)
    grads_ref[3] += nn(normed_t, d_gate)
    grads_ref[4] += nn(gated_t, cot)

    @pl.when(column == columns - 1)
    def _():
        dbias_ref[...] = total[...].astype(BF16)


def attend(valid_len, both, bias, projections, projections_t, columns):
    rows = both.shape[0]
    heads = bias.shape[0]
    channels = projections.shape[-1]
    whole3 = lambda j: (0, 0, 0)
    return pl.pallas_call(
        functools.partial(attention_kernel, heads),
        grid=(columns,),
        in_specs=[
            pl.BlockSpec(memory_space=pltpu.SMEM),
            pl.BlockSpec((rows, channels), lambda j: (0, j)),
            pl.BlockSpec((rows, channels), lambda j: (0, columns + j)),
            pl.BlockSpec(bias.shape, whole3),
            pl.BlockSpec(projections.shape, whole3),
            pl.BlockSpec(projections.shape, whole3),
        ],
        out_specs=[
            pl.BlockSpec((rows, 2 * columns * channels), lambda j: (0, 0)),
            pl.BlockSpec(bias.shape, whole3),
            pl.BlockSpec(projections.shape, whole3),
        ],
        out_shape=[
            jax.ShapeDtypeStruct((rows, 2 * columns * channels), BF16),
            jax.ShapeDtypeStruct(bias.shape, BF16),
            jax.ShapeDtypeStruct(projections.shape, F32),
        ],
        scratch_shapes=[
            pltpu.VMEM(bias.shape, F32),
            pltpu.VMEM((channels, rows), BF16),
            pltpu.VMEM((channels, rows), BF16),
            pltpu.VMEM((rows, channels), F32),
            pltpu.VMEM((rows, channels), F32),
        ],
        compiler_params=pltpu.CompilerParams(vmem_limit_bytes=56 << 20),
        name="attention",
    )(valid_len, both, both, bias, projections, projections_t)


def shards(pair, gain, projections, bias_weight, valid_len, out_cotangent):
    n_row = lax.axis_size(ROW)
    n_col = lax.axis_size(COL)
    n_all = n_row * n_col
    tile_rows, tile_cols, channels = pair.shape
    rows = tile_rows * n_row
    heads = bias_weight.shape[1]
    ncols = tile_cols // n_row
    pair_float = pair.astype(F32)
    average_value = jnp.mean(pair_float, axis=-1, keepdims=True)
    var = jnp.mean((pair_float - average_value) ** 2, axis=-1, keepdims=True)
    inverse_deviation = lax.rsqrt(var + EPS)
    centered_scaled = (pair_float - average_value) * inverse_deviation
    normalized_pair = (centered_scaled * gain).astype(BF16)
    bias_tile = jnp.einsum("abc,ch->hab", normalized_pair, bias_weight, preferred_element_type=F32)
    bias_tile = bias_tile.reshape(1, 1, heads * tile_rows * tile_cols)
    spread = jnp.broadcast_to(bias_tile, (n_all, 1, bias_tile.shape[-1]))
    grid = exchange(spread, ALL).reshape(n_row, n_col, heads, tile_rows, tile_cols)
    bias = jnp.transpose(grid, (2, 0, 3, 1, 4)).reshape(heads, rows, rows)

    def by_owner(tile):
        return jnp.moveaxis(tile.reshape(tile_rows, n_row, ncols * channels), 1, 0)

    both = jnp.concatenate([by_owner(normalized_pair), by_owner(out_cotangent)], axis=2)
    both = exchange(both, ROW).reshape(rows, 2 * ncols * channels)
    out, d_bias_part, grads = attend(
        valid_len, both, bias, projections, jnp.swapaxes(projections, 1, 2), ncols
    )
    part = d_bias_part.reshape(heads, n_row, tile_rows, n_col, tile_cols)
    part = jnp.transpose(part, (1, 3, 0, 2, 4)).reshape(n_all, heads * tile_rows * tile_cols)
    grads = grads.reshape(n_all, -1)
    share = grads.shape[1]
    coarse = grads.astype(BF16)
    fine = (grads - coarse.astype(F32)).astype(BF16)
    sent = jnp.concatenate([part, coarse, fine], axis=1)[:, None, :]
    summed = jnp.sum(exchange(sent, ALL).astype(F32), axis=(0, 1))
    at = heads * tile_rows * tile_cols
    d_bias = summed[:at].reshape(heads, tile_rows, tile_cols).astype(BF16)
    grad_share = summed[at : at + share] + summed[at + share :]

    back = exchange(out.reshape(n_row, tile_rows, 2 * ncols * channels), ROW)
    back = jnp.moveaxis(back.reshape(n_row, tile_rows, 2, ncols, channels), 0, 2)
    back = jnp.moveaxis(back, 1, 0).reshape(2, tile_rows, tile_cols, channels)
    attended = back[0]
    bias_term = jnp.einsum("hab,ch->abc", d_bias, bias_weight, preferred_element_type=F32)
    bias_weight_part = jnp.einsum("abc,hab->ch", normalized_pair, d_bias, preferred_element_type=F32)
    normalized_gradient = back[1].astype(F32) + bias_term
    gain_part = jnp.sum(normalized_gradient * centered_scaled, axis=(0, 1))
    last = jnp.concatenate([grad_share, bias_weight_part.reshape(-1), gain_part])
    everyone = exchange(jnp.broadcast_to(last[None, None], (n_all, 1, last.shape[0])), ALL)[:, 0]
    projection_grad = everyone[:, :share].reshape(projections.shape)
    small = jnp.sum(everyone[:, share:], axis=0)
    bias_weight_grad = small[: channels * heads].reshape(channels, heads)
    gain_gradient = small[channels * heads :]
    scaled_output = normalized_gradient * gain
    pair_gradient = inverse_deviation * (
        scaled_output
        - jnp.mean(scaled_output, axis=-1, keepdims=True)
        - centered_scaled * jnp.mean(scaled_output * centered_scaled, axis=-1, keepdims=True)
    )
    return (attended, pair_gradient, projection_grad, bias_weight_grad, gain_gradient)


def solution(mesh):
    torus = Mesh(mesh.devices.reshape(2, 4, 2, 2, 4), ALL)
    in_specs = (P(ROW, COL, None), P(), P(), P(), P(), P(ROW, COL, None))
    out_specs = (P(ROW, COL, None), P(ROW, COL, None), P(), P(), P())
    return jax.shard_map(
        shards, mesh=torus, in_specs=in_specs, out_specs=out_specs, check_vma=False
    )
```

time: 618 us -> 218 us (0.35); the launches traced: 610 us -> 216 us
  blocking collectives: 283 us -> 0 us
  matrix products: 69.9 us -> 3.63 us
  Pallas kernels: 0 us -> 26.9 us
  waiting for transfers between devices: 93.2 us -> 72.7 us
  other arithmetic: 37.9 us -> 19.7 us
  between operations: 14.7 us -> 1.61 us
  starting transfers between devices: 47 us -> 34.2 us
  local copies, waits for them, and re-layouts: 64.8 us -> 57.7 us
    all_gather x25 -> x0, blocking collectives: 219 us -> none  [stacked_from(): parts = lax.all_gather(parts, axes[k], axis=0, tiled=True)]
    psum x1 -> x0, waiting for transfers between devices: 72.3 us -> none  [shards(): lax.psum((parts, bias_weight_part, gain_partial_sum), ROW_COL)]
    psum x1 -> x0, blocking collectives: 64 us -> none  [shards(): lax.psum((parts, bias_weight_part, gain_partial_sum), ROW_COL)]
    dot_general x34 -> x1, matrix products: 57.8 us -> 1.89 us  [shards(): jnp.einsum('hab,ch->abc', d_bias, bias_weight, preferred_element_type=F32)]
    all_to_all x5, waiting for transfers between devices: 20.9 us -> 72.7 us  [exchange(): return lax.all_to_all(value, axes, split_axis=0, concat_axis=0, tiled=True)]
    pallas_call x0 -> x1, Pallas kernels: none -> 26.9 us  [attend(): pl.pallas_call(functools.partial(attention_kernel, heads), grid=(columns,...]
    reshape x8 -> x13, local copies, waits for them, and re-layouts: 7.48 us -> 29.1 us  [the longest x1 6.55 us: shards(): jnp.transpose(part, (1, 3, 0, 2, 4))]
    another operation x6 -> x0, local copies, waits for them, and re-layouts: 13.5 us -> none  [the longest x1 5.8 us: shards(): total.transpose(1, 0, 2, 3)]
  transfers between devices with their start and end apart: 6 -> 5, of which waited for: 3 -> 4; matrix products, arithmetic and copies ran while one was open for 20% -> 18% of each run, Pallas kernels for 0% -> 0%
where the time goes in v1:
time: 218 us; the launch traced here: 216 us
  waiting for transfers between devices  72.7 us (33%)
  local copies, waits for them, and re-layouts  57.7 us (26%)
  starting transfers between devices  34.2 us (16%)
  Pallas kernels  26.9 us (12%)
  other arithmetic  19.7 us (9%)
  matrix products  3.63 us (2%)
    all_to_all x5, waiting for transfers between devices, exchange(): return lax.all_to_all(value, axes, split_axis=0, concat_axis=0, tiled=True)  72.7 us
    all_to_all x5, starting transfers between devices, exchange(): return lax.all_to_all(value, axes, split_axis=0, concat_axis=0, tiled=True)  34.2 us
    pallas_call x1, Pallas kernels, attend(): pl.pallas_call(functools.partial(attention_kernel, heads), grid=(columns,...  26.9 us
    unnamed x20, local copies, waits for them, and re-layouts  13.3 us
    transpose x1, local copies, waits for them, and re-layouts, shards(): bias = jnp.transpose(grid, (2, 0, 3, 1, 4)).reshape(heads, rows, rows)  9.08 us
    all_to_all x1, other arithmetic, exchange(): return lax.all_to_all(value, axes, split_axis=0, concat_axis=0, tiled=True)  7.71 us
    reshape x1, local copies, waits for them, and re-layouts, shards(): jnp.transpose(part, (1, 3, 0, 2, 4))  6.55 us
    reshape x2, local copies, waits for them, and re-layouts, shards(): part = d_bias_part.reshape(heads, n_row, tile_rows, n_col, tile_cols)  6.47 us
  transfers between devices with their start and end apart: 5, of which 4 were waited for; matrix products, arithmetic and copies ran while one was open for 18% of the time, Pallas kernels for 0%

profile of v1, /device:TPU:1, one launch (start us, length us, event | category | flops | bytes accessed | tf_op | source)
XLA Modules:
  0.0 216.5 jit_solution(5739083523457251575)
XLA Ops:
  1.9 1.4 fusion.11
  5.1 2.6 %broadcast_in_dim.9 = f32[128,1,4608]{2,1,0:T(1,128)} broadcast(f32[4608]{0:T(1024)S(1)} %broadcast_in_dim.8), dimensions={2} | broadcast | bytes 2377728 | tf_op jit(solution)/shard_map/broadcast_in_dim | solution.py:173
  7.7 11.5 %all-to-all-start.1 = ((f32[128,1,4608]{2,1,0:T(1,128)}), f32[128,1,4608]{2,1,0:T(1,128)S(1)}, u32[]{:S(2)}, u32[]{:S(2)}) async-start(f32[128,1,4608]{2,1,0:T(1,128)} %broadcast_in_dim.9), calls=%async_computation.1 | async-start | bytes 4718592 | tf_op jit(solution)/shard_map/all_to_all | solution.py:34
  20.6 31.2 %all-to-all-done.1 = f32[128,1,4608]{2,1,0:T(1,128)S(1)} async-done(((f32[128,1,4608]{2,1,0:T(1,128)}), f32[128,1,4608]{2,1,0:T(1,128)S(1)}, u32[]{:S(2)}, u32[]{:S(2)}) %all-to-all-start.1) | async-done | bytes 2359328 | tf_op jit(solution)/shard_map/all_to_all | solution.py:34
  51.8 4.9 %all-to-all-start = ((bf16[16,24,768]{2,1,0:T(8,128)(2,1)}), bf16[16,24,768]{2,1,0:T(8,128)(2,1)S(1)}, u32[]{:S(2)}, u32[]{:S(2)}) async-start(bf16[16,24,768]{2,1,0:T(8,128)(2,1)} %pad_maximum_fusion), calls=%async_computation | async-start | bytes 1179648 | tf_op jit(solution)/shard_map/all_to_all | solution.py:34
  58.2 7.7 %reduce = f32[128,4608]{1,0:T(8,128)} reduce(f32[128,1,4608]{2,1,0:T(1,128)S(1)} %all-to-all-done.1, f32[]{:T(128)} %constant.12), dimensions={1}, to_apply=%all_to_all.16.reduce_sub_computation | reduce | bytes 4718596 | tf_op jit(solution)/shard_map/all_to_all | solution.py:34
  65.9 6.0 %reshape.97 = f32[16,8,4,24,48]{4,3,2,1,0:T(8,128)} reshape(f32[128,4608]{1,0:T(8,128)} %reduce) | data formatting | bytes 4718592 | tf_op jit(solution)/shard_map/reshape | solution.py:174
  71.8 9.1 %copy.47 = f32[4,16,24,8,48]{4,3,2,1,0:T(8,128)} copy(f32[4,16,24,8,48]{4,2,0,3,1:T(8,128)} %bitcast.38) | data formatting | bytes 4718592 | tf_op jit(solution)/shard_map/transpose | solution.py:175
  80.9 5.9 %reshape.98.bias_ref = f32[4,384,384]{2,1,0:T(8,128)} reshape(f32[4,16,24,8,48]{4,3,2,1,0:T(8,128)} %copy.47) | data formatting | bytes 4718592 | tf_op jit(solution)/shard_map/reshape | solution.py:175
  87.6 26.9 %attention.1 = (bf16[384,768]{1,0:T(8,128)(2,1)}, bf16[4,384,384]{2,1,0:T(8,128)(2,1)}, f32[5,128,128]{2,1,0:T(8,128)}) custom-call(s32[1]{0:T(128)S(6)} %copy.79.valid_ref, bf16[384,768]{1,0:T(8,128)(2,1)} %bitcast.40, bf16[384,768]{1,0:T(8,128)(2,1)} %bitcast.41, f32[4,384,384]{2,1,0:T(8,128)} %reshape.98.bias_ref, bf16[5,128,128]{2,1,0:T(8,128)(2,1)} %w_ref.1, ...), custom_call_target="tpu_custom_call" | custom-call | tf_op jit(solution)/shard_map/attention/pallas_call | solution.py:124
  115.7 4.2 %reshape.101 = bf16[4,16,24,8,48]{4,3,2,1,0:T(8,128)(2,1)S(1)} reshape(bf16[4,384,384]{2,1,0:T(8,128)(2,1)} %get-tuple-element.9) | data formatting | bytes 2359296 | tf_op jit(solution)/shard_map/reshape | solution.py:185
  119.9 2.3 %copy.75 = bf16[4,16,24,8,48]{4,2,0,3,1:T(8,128)(2,1)} copy(bf16[4,16,24,8,48]{4,3,2,1,0:T(8,128)(2,1)S(1)} %reshape.101) | data formatting | bytes 2359296 | tf_op jit(solution)/shard_map/reshape | solution.py:185
  122.1 6.6 %reshape.102 = bf16[128,4608]{1,0:T(8,128)(2,1)S(1)} reshape(bf16[16,8,4,24,48]{4,3,2,1,0:T(8,128)(2,1)} %bitcast.39) | data formatting | bytes 2359296 | tf_op jit(solution)/shard_map/reshape | solution.py:186
  128.7 7.3 %all-to-all-start.2 = ((bf16[16,24,768]{2,1,0:T(8,128)(2,1)}), bf16[16,24,768]{2,1,0:T(8,128)(2,1)}, u32[]{:S(2)}, u32[]{:S(2)}) async-start(bf16[16,24,768]{2,1,0:T(8,128)(2,1)} %bitcast.7), calls=%async_computation.2 | async-start | bytes 1179648 | tf_op jit(solution)/shard_map/all_to_all | solution.py:34
  136.6 1.8 reduce.1
  139.8 8.4 %all-to-all-done.2 = bf16[16,24,768]{2,1,0:T(8,128)(2,1)} async-done(((bf16[16,24,768]{2,1,0:T(8,128)(2,1)}), bf16[16,24,768]{2,1,0:T(8,128)(2,1)}, u32[]{:S(2)}, u32[]{:S(2)}) %all-to-all-start.2) | async-done | bytes 589856 | tf_op jit(solution)/shard_map/all_to_all | solution.py:34
  148.1 5.6 %all-to-all-start.3 = ((bf16[128,2,2944]{2,1,0:T(2,128)(2,1)}), bf16[128,2,2944]{2,1,0:T(2,128)(2,1)}, u32[]{:S(2)}, u32[]{:S(2)}) async-start(bf16[128,2,2944]{2,1,0:T(2,128)(2,1)} %reshape.111), calls=%async_computation.3 | async-start | bytes 3014656 | tf_op jit(solution)/shard_map/all_to_all | solution.py:34
  157.6 19.7 %all-to-all-done.3 = bf16[128,2,2944]{2,1,0:T(2,128)(2,1)} async-done(((bf16[128,2,2944]{2,1,0:T(2,128)(2,1)}), bf16[128,2,2944]{2,1,0:T(2,128)(2,1)}, u32[]{:S(2)}, u32[]{:S(2)}) %all-to-all-start.3) | async-done | bytes 1507360 | tf_op jit(solution)/shard_map/all_to_all | solution.py:34
  177.2 8.9 %reshape.112 = bf16[128,1,5888]{2,1,0:T(2,128)(2,1)S(1)} reshape(bf16[128,2,2944]{2,1,0:T(2,128)(2,1)} %all-to-all-done.3) | data formatting | bytes 3014656
  186.1 3.7 %convert_reduce_fusion = f32[5888]{0:T(1024)S(1)} fusion(bf16[128,1,5888]{2,1,0:T(2,128)(2,1)S(1)} %reshape.112), kind=kLoop, calls=%fused_computation.1 | loop fusion | flops 1501440 | bytes 1530880 | tf_op jit(solution)/shard_map/reduce_sum | solution.py:192
  191.3 1.9 fusion.10
  194.5 4.8 %all-to-all-start.4 = ((f32[128,1,1280]{2,1,0:T(1,128)}), f32[128,1,1280]{2,1,0:T(1,128)S(1)}, u32[]{:S(2)}, u32[]{:S(2)}) async-start(f32[128,1,1280]{2,1,0:T(1,128)} %broadcast_in_dim.11), calls=%async_computation.4 | async-start | bytes 1310720 | tf_op jit(solution)/shard_map/all_to_all | solution.py:34
  199.4 1.5 fusion.9
  200.9 13.4 %all-to-all-done.4 = f32[128,1,1280]{2,1,0:T(1,128)S(1)} async-done(((f32[128,1,1280]{2,1,0:T(1,128)}), f32[128,1,1280]{2,1,0:T(1,128)S(1)}, u32[]{:S(2)}, u32[]{:S(2)}) %all-to-all-start.4) | async-done | bytes 655392 | tf_op jit(solution)/shard_map/all_to_all | solution.py:34
  (54 shorter events, 17.7 us)
Async XLA Ops:
  0.6 4.0 %copy-start = (bf16[128,4]{0,1:T(4,128)(2,1)S(1)}, bf16[128,4]{0,1:T(4,128)(2,1)}, u32[]{:S(2)}) copy-start(bf16[128,4]{0,1:T(4,128)(2,1)} %param.9) | copy-start | bytes 3076
  4.6 14.6 %copy-start.3 = (bf16[24,48,128]{2,1,0:T(8,128)(2,1)}, bf16[24,48,128]{2,1,0:T(8,128)(2,1)S(1)}, u32[]{:S(2)}) copy-start(bf16[24,48,128]{2,1,0:T(8,128)(2,1)S(1)} %fusion.6) | copy-start | bytes 884740
  7.7 11.7 %copy-start.5 = (bf16[24,48,128]{2,1,0:T(8,128)(2,1)S(1)}, bf16[24,48,128]{2,1,0:T(8,128)(2,1)}, u32[]{:S(2)}) copy-start(bf16[24,48,128]{2,1,0:T(8,128)(2,1)} %param.11) | copy-start | bytes 884740
  7.7 44.0 %all-to-all-start.1 = ((f32[128,1,4608]{2,1,0:T(1,128)}), f32[128,1,4608]{2,1,0:T(1,128)S(1)}, u32[]{:S(2)}, u32[]{:S(2)}) async-start(f32[128,1,4608]{2,1,0:T(1,128)} %broadcast_in_dim.9), calls=%async_computation.1 | async-start | bytes 4718592 | tf_op jit(solution)/shard_map/all_to_all | solution.py:34
  19.2 37.5 %copy-start.4 = (bf16[5,128,128]{2,1,0:T(8,128)(2,1)S(1)}, bf16[5,128,128]{2,1,0:T(8,128)(2,1)}, u32[]{:S(2)}) copy-start(bf16[5,128,128]{2,1,0:T(8,128)(2,1)} %w_ref.1) | copy-start | bytes 491524
  51.8 35.0 %all-to-all-start = ((bf16[16,24,768]{2,1,0:T(8,128)(2,1)}), bf16[16,24,768]{2,1,0:T(8,128)(2,1)S(1)}, u32[]{:S(2)}, u32[]{:S(2)}) async-start(bf16[16,24,768]{2,1,0:T(8,128)(2,1)} %pad_maximum_fusion), calls=%async_computation | async-start | bytes 1179648 | tf_op jit(solution)/shard_map/all_to_all | solution.py:34
  86.8 0.8 copy-start.1
  128.7 19.4 %all-to-all-start.2 = ((bf16[16,24,768]{2,1,0:T(8,128)(2,1)}), bf16[16,24,768]{2,1,0:T(8,128)(2,1)}, u32[]{:S(2)}, u32[]{:S(2)}) async-start(bf16[16,24,768]{2,1,0:T(8,128)(2,1)} %bitcast.7), calls=%async_computation.2 | async-start | bytes 1179648 | tf_op jit(solution)/shard_map/all_to_all | solution.py:34
  148.1 29.1 %all-to-all-start.3 = ((bf16[128,2,2944]{2,1,0:T(2,128)(2,1)}), bf16[128,2,2944]{2,1,0:T(2,128)(2,1)}, u32[]{:S(2)}, u32[]{:S(2)}) async-start(bf16[128,2,2944]{2,1,0:T(2,128)(2,1)} %reshape.111), calls=%async_computation.3 | async-start | bytes 3014656 | tf_op jit(solution)/shard_map/all_to_all | solution.py:34
  186.1 5.2 %copy-start.2 = (bf16[24,48,128]{2,1,0:T(8,128)(2,1)S(1)}, bf16[24,48,128]{2,1,0:T(8,128)(2,1)}, u32[]{:S(2)}) copy-start(bf16[24,48,128]{2,1,0:T(8,128)(2,1)} %param.6) | copy-start | bytes 884740
  186.1 5.2 %copy-start.6 = (f32[128]{0:T(128)S(1)}, f32[128]{0:T(128)}, u32[]{:S(2)}) copy-start(f32[128]{0:T(128)} %param.7) | copy-start | bytes 1540
  194.5 19.8 %all-to-all-start.4 = ((f32[128,1,1280]{2,1,0:T(1,128)}), f32[128,1,1280]{2,1,0:T(1,128)S(1)}, u32[]{:S(2)}, u32[]{:S(2)}) async-start(f32[128,1,1280]{2,1,0:T(1,128)} %broadcast_in_dim.11), calls=%async_computation.4 | async-start | bytes 1310720 | tf_op jit(solution)/shard_map/all_to_all | solution.py:34

commit v2 on v1

v2 whole, which is shorter than its diff:
```python
import functools

import jax
import jax.numpy as jnp
from jax import lax
from jax.experimental import pallas as pl
from jax.experimental.pallas import tpu as pltpu
from jax.sharding import Mesh
from jax.sharding import PartitionSpec as P

ROW = ("row_0", "row_1", "row_2")
COL = ("col_0", "col_1")
ALL = ROW + COL
CORE = "row_2"
EPS = 1e-05
MASKED = -1000000000.0
PARTS = 4
F32 = jnp.float32
BF16 = jnp.bfloat16


def nn(left, right):
    return lax.dot_general(left, right, (((1,), (0,)), ((), ())), preferred_element_type=F32)


def nt(left, right):
    return lax.dot_general(left, right, (((1,), (1,)), ((), ())), preferred_element_type=F32)


def turned(value):
    return jnp.transpose(value.astype(F32)).astype(value.dtype)


def exchange(value, axes):
    return lax.all_to_all(value, axes, split_axis=0, concat_axis=0, tiled=True)


def call(kernel, out_shape, scratch, name, *operands):
    return pl.pallas_call(
        kernel,
        out_shape=out_shape,
        scratch_shapes=scratch,
        compiler_params=pltpu.CompilerParams(vmem_limit_bytes=56 << 20),
        name=name,
    )(*operands)


def coarse_fine(value):
    coarse = value.astype(BF16)
    return coarse, (value - coarse.astype(F32)).astype(BF16)


def normalize(pair_ref, gain_ref):
    rows, cols, channels = pair_ref.shape
    pair = pair_ref[...].astype(F32).reshape(rows * cols, channels)
    average = jnp.mean(pair, axis=-1, keepdims=True)
    var = jnp.mean((pair - average) ** 2, axis=-1, keepdims=True)
    inverse = lax.rsqrt(var + EPS)
    xhat = (pair - average) * inverse
    return xhat, inverse, (xhat * gain_ref[...]).astype(BF16)


def pack_kernel(pair_ref, cot_ref, gain_ref, bias_weight_ref, out_ref, normed_s, cot_s, bias_s):
    rows, cols, channels = pair_ref.shape
    owners = out_ref.shape[0]
    ncols = cols // owners
    heads = bias_weight_ref.shape[0]
    normed = normalize(pair_ref, gain_ref)[2]
    normed_s[...] = normed.astype(F32)
    cot_s[...] = cot_ref[...].astype(F32).reshape(rows * cols, channels)
    for a in range(rows):
        bias = nt(bias_weight_ref[...], normed[a * cols : (a + 1) * cols])
        bias_s[pl.ds(a, heads, stride=rows), :] = bias
    pad = jnp.zeros((rows, 256 - 4 * cols), BF16)
    for core in range(2):
        first = 2 * core * rows
        bias = jnp.concatenate([bias_s[first : first + rows], bias_s[first + rows : first + 2 * rows]], axis=1)
        bias = jnp.concatenate([*coarse_fine(bias), pad], axis=1)
        for owner in range(core, owners, 2):
            out_ref[owner, :, 2 * ncols * channels :] = bias
    for owner in range(owners):
        for k in range(ncols):
            column = pl.ds(owner * ncols + k, rows, stride=cols)
            at = k * channels
            out_ref[owner, :, at : at + channels] = normed_s[column, :].astype(BF16)
            at = (ncols + k) * channels
            out_ref[owner, :, at : at + channels] = cot_s[column, :].astype(BF16)


def bias_out_kernel(parts_ref, out_ref):
    rows = parts_ref.shape[0]
    width = out_ref.shape[2] // PARTS
    bias = parts_ref[:, :width].astype(F32) + parts_ref[:, width : 2 * width].astype(F32)
    high = rows // PARTS
    packed = jnp.concatenate([bias[k * high : (k + 1) * high] for k in range(PARTS)], axis=1)
    for c in range(out_ref.shape[0]):
        out_ref[c] = packed


def project_kernel(
    normed_ref, twin_normed_ref, cot_ref, twin_cot_ref, w_ref, wt_ref, w_out_ref,
    query_ref, key_ref, value_ref, d_context_ref,
    query_t_ref, key_t_ref, value_t_ref, d_context_t_ref, gate_t_ref, d_gated_t_ref,
):
    normed = jnp.concatenate([normed_ref[...], twin_normed_ref[...]], axis=1)
    cot = jnp.concatenate([cot_ref[...], twin_cot_ref[...]], axis=1)
    for m, ref, ref_t in ((0, query_ref, query_t_ref), (1, key_ref, key_t_ref), (2, value_ref, value_t_ref)):
        ref[0] = nn(normed, w_ref[m]).astype(BF16)
        ref_t[0] = nt(wt_ref[m], normed).astype(BF16)
    gate_t = jax.nn.sigmoid(nt(wt_ref[3], normed))
    d_gated_t = nt(w_out_ref[...], cot)
    d_context_t = (d_gated_t * gate_t).astype(BF16)
    gate_t_ref[0] = gate_t
    d_gated_t_ref[0] = d_gated_t
    d_context_t_ref[0] = d_context_t
    d_context_ref[0] = turned(d_context_t)


def project(both, twin, w, wt, w_out, columns):
    rows = both.shape[0]
    channels = w.shape[-1]
    normed = pl.BlockSpec((rows, channels), lambda j: (0, j))
    cot = pl.BlockSpec((rows, channels), lambda j: (0, columns + j))
    flat = pl.BlockSpec((1, rows, channels), lambda j: (j, 0, 0))
    flat_t = pl.BlockSpec((1, channels, rows), lambda j: (j, 0, 0))
    upright = jax.ShapeDtypeStruct((columns, rows, channels), BF16)
    lying = jax.ShapeDtypeStruct((columns, channels, rows), BF16)
    wide = jax.ShapeDtypeStruct((columns, channels, rows), F32)
    return pl.pallas_call(
        project_kernel,
        grid=(columns,),
        in_specs=[
            normed, normed, cot, cot,
            pl.BlockSpec(w.shape, lambda j: (0, 0, 0)),
            pl.BlockSpec(wt.shape, lambda j: (0, 0, 0)),
            pl.BlockSpec(w_out.shape, lambda j: (0, 0)),
        ],
        out_specs=[flat] * 4 + [flat_t] * 6,
        out_shape=[upright] * 4 + [lying] * 4 + [wide] * 2,
        compiler_params=pltpu.CompilerParams(vmem_limit_bytes=56 << 20),
        name="project",
    )(both, twin, both, twin, w, wt, w_out)


def attention_kernel(
    valid_ref, got_ref, normed_ref, twin_normed_ref, cot_ref, twin_cot_ref,
    query_ref, key_ref, value_ref, d_context_ref,
    query_t_ref, key_t_ref, value_t_ref, d_context_t_ref, gate_t_ref, d_gated_t_ref,
    acts_ref, sent_ref, bias_s, total, grads_s, ctx_t, dq_t, d_scores_s, weights_s, query_s, d_context_s,
):
    step = pl.program_id(0)
    steps = pl.num_programs(0)
    blocks, high, lanes = got_ref.shape
    rows, channels = normed_ref.shape
    slots = 4
    width = channels // slots
    half = channels // 2
    cols = rows // blocks
    scale = width ** (-0.5)

    @pl.when(step == 0)
    def _():
        for k in range(PARTS):
            for h in range(2):
                at = (2 * k + h) * cols
                pieces = [got_ref[c, :, at : at + cols] for c in range(blocks)]
                bias_s[h, k * high : (k + 1) * high, :] = jnp.concatenate(pieces, axis=1)
        total[...] = jnp.zeros_like(total)
        grads_s[...] = jnp.zeros_like(grads_s)

    query = query_ref[0]
    key = key_ref[0]
    value = value_ref[0]
    d_context = d_context_ref[0]
    lane = lax.broadcasted_iota(jnp.int32, (rows, channels), 1)
    keep = lax.broadcasted_iota(jnp.int32, (rows, rows), 0) < valid_ref[0]
    zero = jnp.zeros((rows, channels), BF16)
    for slot in range(slots):
        mine = (lane >= slot * width) & (lane < (slot + 1) * width)
        key_h = jnp.where(mine, key, zero)
        value_h = jnp.where(mine, value, zero)
        here = slice(slot * rows, (slot + 1) * rows)
        part = slice(slot * width, (slot + 1) * width)
        query_s[here, :] = jnp.where(mine, query, zero)
        d_context_s[here, :] = jnp.where(mine, d_context, zero)
        scores = nn(key_h, query_t_ref[0]) * scale + bias_s[slot % 2]
        scores = jnp.where(keep, scores, MASKED)
        top = jnp.max(scores, axis=0, keepdims=True)
        grown = jnp.exp(scores - top)
        probs = grown * (1.0 / jnp.sum(grown, axis=0, keepdims=True))
        weights_b = probs.astype(BF16)
        weights_s[:, here] = weights_b
        ctx_t[part, :] = nn(value_t_ref[0, part, :], weights_b).astype(BF16)
        d_probs = nn(value_h, d_context_t_ref[0])
        delta = jnp.sum(probs * d_probs, axis=0, keepdims=True)
        d_scores = probs * (d_probs - delta)
        total[slot % 2] += d_scores
        d_scores_b = d_scores.astype(BF16)
        d_scores_s[:, here] = d_scores_b
        dq_t[part, :] = (nn(key_t_ref[0, part, :], d_scores_b) * scale).astype(BF16)
    d_key = (nn(d_scores_s[...], query_s[...]) * scale).astype(BF16)
    d_value = nn(weights_s[...], d_context_s[...]).astype(BF16)
    gate_t = gate_t_ref[0]
    context_t = ctx_t[...].astype(F32)
    gated_t = (gate_t * context_t).astype(BF16)
    d_gate_t = (d_gated_t_ref[0] * context_t * gate_t * (1.0 - gate_t)).astype(BF16)
    acts = [turned(gated_t), turned(dq_t[...]), d_key, d_value, turned(d_gate_t)]
    for m in range(5):
        acts_ref[0, :, m * channels : (m + 1) * channels] = acts[m]
    right = jnp.concatenate(acts[1:], axis=1)
    own = nn(turned(normed_ref[...]), right)
    other = nn(turned(twin_normed_ref[...]), right)
    for m in range(4):
        at = slice(m * channels, (m + 1) * channels)
        grads_s[:channels, at] += jnp.where(lane[:channels] < half, own[:, at], other[:, at])
    last = nn(gated_t[:half], cot_ref[...]) + nn(gated_t[half:], twin_cot_ref[...])
    grads_s[channels:, :channels] += last

    @pl.when(step == steps - 1)
    def _():
        for c in range(blocks):
            pieces = [
                total[h, k * high : (k + 1) * high, c * cols : (c + 1) * cols]
                for k in range(PARTS)
                for h in range(2)
            ]
            sent_ref[c, :high, :] = jnp.concatenate(pieces, axis=1).astype(BF16)
        sums = []
        for m in range(4):
            at = slice(m * channels, (m + 1) * channels)
            both = grads_s[:channels, at]
            sums.append(both + pltpu.roll(both, half, 1))
        left = lane[:channels] < half
        grads = [
            jnp.where(left, sums[0], sums[1]),
            jnp.where(left, sums[2], sums[3]),
            grads_s[channels:, :channels],
        ]
        grads = jnp.concatenate(grads, axis=0)
        share = grads.shape[0] // blocks
        rest = sent_ref.shape[1] - high
        spare = jnp.zeros((3 * rest - share, channels), F32)
        for c in range(blocks):
            mine = jnp.concatenate([grads[c * share : (c + 1) * share], spare], axis=0)
            pieces = [mine[k * rest : (k + 1) * rest] for k in range(3)]
            sent_ref[c, high:, :] = jnp.concatenate(pieces, axis=1).astype(BF16)


def attend(valid_len, got, both, twin, inner, columns):
    rows = both.shape[0]
    channels = inner[0].shape[-1]
    blocks, high, lanes = got.shape
    normed = pl.BlockSpec((rows, channels), lambda j: (0, j))
    cot = pl.BlockSpec((rows, channels), lambda j: (0, columns + j))
    flat = pl.BlockSpec((1, rows, channels), lambda j: (j, 0, 0))
    flat_t = pl.BlockSpec((1, channels, rows), lambda j: (j, 0, 0))
    return pl.pallas_call(
        attention_kernel,
        grid=(columns,),
        in_specs=[
            pl.BlockSpec(memory_space=pltpu.SMEM),
            pl.BlockSpec(got.shape, lambda j: (0, 0, 0)),
            normed, normed, cot, cot,
        ]
        + [flat] * 4
        + [flat_t] * 6,
        out_specs=[
            pl.BlockSpec((1, rows, 5 * channels), lambda j: (j, 0, 0)),
            pl.BlockSpec((blocks, high + 16, lanes), lambda j: (0, 0, 0)),
        ],
        out_shape=[
            jax.ShapeDtypeStruct((columns, rows, 5 * channels), BF16),
            jax.ShapeDtypeStruct((blocks, high + 16, lanes), BF16),
        ],
        scratch_shapes=[
            pltpu.VMEM((2, rows, rows), F32),
            pltpu.VMEM((2, rows, rows), F32),
            pltpu.VMEM((channels + channels // 2, 4 * channels), F32),
            pltpu.VMEM((channels, rows), BF16),
            pltpu.VMEM((channels, rows), BF16),
            pltpu.VMEM((rows, 4 * rows), BF16),
            pltpu.VMEM((rows, 4 * rows), BF16),
            pltpu.VMEM((4 * rows, channels), BF16),
            pltpu.VMEM((4 * rows, channels), BF16),
        ],
        compiler_params=pltpu.CompilerParams(vmem_limit_bytes=56 << 20),
        name="attention",
    )(valid_len, got, both, twin, both, twin, *inner)


def merge_kernel(acts_ref, came_ref, w_ref, out_ref):
    column = pl.program_id(0)
    columns = pl.num_programs(0)
    channels = w_ref.shape[-1]
    parts = []
    for m in range(5):
        at = slice(m * channels, (m + 1) * channels)
        parts.append(nn(jnp.concatenate([acts_ref[0, :, at], came_ref[0, :, at]], axis=1), w_ref[m]))
    d_normed = parts[1] + parts[2] + parts[3] + parts[4]
    out_ref[:, pl.ds(pl.multiple_of(column * channels, channels), channels)] = parts[0].astype(BF16)
    second = pl.multiple_of((columns + column) * channels, channels)
    out_ref[:, pl.ds(second, channels)] = d_normed.astype(BF16)


def merge(acts, came, w):
    columns, rows, lanes = acts.shape
    channels = w.shape[-1]
    block = pl.BlockSpec((1, rows, lanes), lambda j: (j, 0, 0))
    return pl.pallas_call(
        merge_kernel,
        grid=(columns,),
        in_specs=[block, block, pl.BlockSpec(w.shape, lambda j: (0, 0, 0))],
        out_specs=pl.BlockSpec((rows, 2 * columns * channels), lambda j: (0, 0)),
        out_shape=jax.ShapeDtypeStruct((rows, 2 * columns * channels), BF16),
        compiler_params=pltpu.CompilerParams(vmem_limit_bytes=56 << 20),
        name="merge",
    )(acts, came, w)


def sum_kernel(got_ref, main_ref, out_ref):
    blocks, high, lanes = got_ref.shape
    owners, rows, wide = out_ref.shape
    main = main_ref.shape[1]
    part = lanes // PARTS
    rest = high - part
    total = got_ref[0].astype(F32)
    for c in range(1, blocks):
        total = total + got_ref[c].astype(F32)
    grads = jnp.concatenate([total[part:, k * 128 : (k + 1) * 128] for k in range(lanes // 128)], axis=0)
    share = 5
    pad = jnp.zeros((rows, 256 - 2 * part), BF16)
    gap = jnp.zeros((8 - share, 128), F32)
    for owner in range(owners):
        across, down = divmod(owner, part // rows)
        block = total[down * rows : (down + 1) * rows, across * part : (across + 1) * part]
        out_ref[owner, :, :main] = main_ref[owner * rows : (owner + 1) * rows, :]
        out_ref[owner, :, main : main + 256] = jnp.concatenate([*coarse_fine(block), pad], axis=1)
        mine = grads[owner // 2 * share : (owner // 2 + 1) * share]
        coarse = mine.astype(BF16).astype(F32)
        stack = jnp.concatenate([coarse, gap, mine - coarse, gap, jnp.zeros((8, 128), F32)], axis=0)
        out_ref[owner, :, main + 256 :] = stack.astype(BF16)


def finish_kernel(
    core_ref, got_ref, pair_ref, gain_ref, bias_weight_ref, repeated_ref,
    attended_ref, gradient_ref, last_ref, moved_s, d_normed_s, d_bias_s,
):
    owners, rows, wide = got_ref.shape
    cols, channels = pair_ref.shape[1:]
    heads = bias_weight_ref.shape[0]
    ncols = cols // owners
    main = 2 * ncols * channels
    xhat, inverse, normed = normalize(pair_ref, gain_ref)
    for owner in range(owners):
        for k in range(ncols):
            column = pl.ds(owner * ncols + k, rows, stride=cols)
            at = k * channels
            moved_s[column, :] = got_ref[owner, :, at : at + channels].astype(F32)
            at = (ncols + k) * channels
            d_normed_s[column, :] = got_ref[owner, :, at : at + channels].astype(F32)
    attended_ref[...] = moved_s[...].astype(BF16).reshape(attended_ref.shape)
    grads = [jnp.zeros((rows, 128), F32), jnp.zeros((rows, 128), F32)]
    for owner in range(owners):
        grads[owner % 2] = grads[owner % 2] + got_ref[owner, :, main + 256 :].astype(F32)
    grads = jnp.where(core_ref[0] == 0, grads[0], grads[1])
    for core in range(2):
        block = jnp.zeros((rows, 2 * cols), F32)
        for owner in range(core, owners, 2):
            block = block + got_ref[owner, :, main : main + 2 * cols].astype(F32)
            block = block + got_ref[owner, :, main + 2 * cols : main + 4 * cols].astype(F32)
        block = block.astype(BF16).astype(F32)
        for h in range(2):
            at = pl.ds(2 * core + h, rows, stride=heads)
            d_bias_s[at, :] = block[:, h * cols : (h + 1) * cols]
    d_bias_t = jnp.transpose(d_bias_s[...]).astype(BF16)
    row = lax.broadcasted_iota(jnp.int32, (rows * heads, channels), 0)
    weight_part = jnp.zeros((heads, channels), F32)
    for a in range(rows):
        here = slice(a * cols, (a + 1) * cols)
        mine = (row >= a * heads) & (row < (a + 1) * heads)
        weight = jnp.where(mine, repeated_ref[...], jnp.zeros((rows * heads, channels), BF16))
        d_normed_s[here, :] += nn(d_bias_t, weight)
        d_bias_a = d_bias_s[a * heads : (a + 1) * heads, :].astype(BF16)
        weight_part = weight_part + nn(d_bias_a, normed[here])
    d_normed = d_normed_s[...]
    gain_part = jnp.sum(d_normed * xhat, axis=0, keepdims=True)
    last = jnp.concatenate([grads[:5] + grads[8:13], weight_part, gain_part], axis=0)
    last_ref[...] = jnp.broadcast_to(last[None], last_ref.shape)
    scaled = d_normed * gain_ref[...]
    gradient = inverse * (
        scaled
        - jnp.mean(scaled, axis=-1, keepdims=True)
        - xhat * jnp.mean(scaled * xhat, axis=-1, keepdims=True)
    )
    gradient_ref[...] = gradient.reshape(gradient_ref.shape)


def shards(pair, gain, projections, bias_weight, valid_len, out_cotangent):
    n_row = lax.axis_size(ROW)
    n_col = lax.axis_size(COL)
    n_all = n_row * n_col
    tile_rows, tile_cols, channels = pair.shape
    rows = tile_rows * n_row
    heads = bias_weight.shape[1]
    ncols = tile_cols // n_row
    tile = tile_rows * tile_cols
    main = 2 * ncols * channels
    half = channels // 2
    shape = jax.ShapeDtypeStruct
    gain_row = gain[None, :]
    weight_t = bias_weight.T
    swap = [(0, 1), (1, 0)]
    core = lax.axis_index(CORE).astype(jnp.int32)
    repeated = jnp.tile(weight_t, (tile_rows, 1))
    halves = projections[:4].reshape(4, channels, 2, half)
    rows_out = projections[4].reshape(2, half, channels)
    own = lax.dynamic_index_in_dim(halves, core, 2, keepdims=False)
    other = lax.dynamic_index_in_dim(halves, 1 - core, 2, keepdims=False)
    own_out = lax.dynamic_index_in_dim(rows_out, core, 0, keepdims=False)
    other_out = lax.dynamic_index_in_dim(rows_out, 1 - core, 0, keepdims=False)
    zero = jnp.zeros_like(own)
    w = jnp.concatenate(
        [jnp.concatenate([own, zero], axis=2), jnp.concatenate([zero, own], axis=2)], axis=1
    )
    zero_out = jnp.zeros_like(own_out)
    w_out = jnp.concatenate(
        [jnp.concatenate([own_out, zero_out], axis=1), jnp.concatenate([zero_out, own_out], axis=1)],
        axis=0,
    )
    mine = jnp.concatenate([own_out[None], jnp.swapaxes(own, 1, 2)], axis=0)
    theirs = jnp.concatenate([other_out[None], jnp.swapaxes(other, 1, 2)], axis=0)
    gap = jnp.zeros((5, channels, channels), BF16)
    w_merge = jnp.concatenate([mine, gap, theirs], axis=1)

    packed = call(
        pack_kernel, shape((n_row, tile_rows, main + 256), BF16),
        [pltpu.VMEM((tile, channels), F32), pltpu.VMEM((tile, channels), F32),
         pltpu.VMEM((heads * tile_rows, tile_cols), F32)],
        "pack", pair, out_cotangent, gain_row, weight_t,
    )
    both = exchange(packed, ROW).reshape(rows, main + 256)
    high = rows // PARTS
    lanes = PARTS * 2 * tile_cols
    spread = pl.pallas_call(
        bias_out_kernel,
        grid=(1,),
        in_specs=[pl.BlockSpec((rows, 256), lambda i: (0, main // 256))],
        out_specs=pl.BlockSpec((n_col, high, lanes), lambda i: (0, 0, 0)),
        out_shape=shape((n_col, high, lanes), F32),
        name="bias_out",
    )(both)
    got = exchange(spread, COL)
    twin = lax.ppermute(both, CORE, swap)
    inner = project(both, twin, w, jnp.swapaxes(w, 1, 2), w_out, ncols)
    acts, sent = attend(valid_len, got, both, twin, inner, ncols)
    summed = exchange(sent, COL)
    out = merge(acts, lax.ppermute(acts, CORE, swap), w_merge)
    back = call(
        sum_kernel, shape((n_row, tile_rows, main + 384), BF16), [], "sum", summed, out
    )
    attended, pair_gradient, last = pl.pallas_call(
        finish_kernel,
        in_specs=[pl.BlockSpec(memory_space=pltpu.SMEM)] + [pl.BlockSpec(memory_space=pltpu.VMEM)] * 5,
        out_shape=[shape(pair.shape, BF16), shape(pair.shape, F32), shape((n_all, 10, channels), F32)],
        scratch_shapes=[
            pltpu.VMEM((tile, channels), F32), pltpu.VMEM((tile, channels), F32),
            pltpu.VMEM((heads * tile_rows, tile_cols), F32),
        ],
        compiler_params=pltpu.CompilerParams(vmem_limit_bytes=56 << 20),
        name="finish",
    )(core[None], exchange(back, ROW), pair, gain_row, weight_t, repeated)
    everyone = exchange(last, ALL)
    shares = everyone[:, :5].reshape(n_row // 2, 2, n_col, 5, channels)
    shares = jnp.transpose(shares, (1, 2, 0, 3, 4)).reshape(2, 5 * half, channels)
    inward = shares[:, : 2 * channels].reshape(2, 2, channels, 2, half)
    inward = jnp.transpose(inward, (1, 3, 2, 0, 4)).reshape(4, channels, channels)
    outward = shares[:, 2 * channels :].reshape(1, channels, channels)
    projection_grad = jnp.concatenate([inward, outward], axis=0)
    small = jnp.sum(everyone[:, 5:], axis=0)
    return (attended, pair_gradient, projection_grad, small[:4].T, small[4])


def solution(mesh):
    torus = Mesh(mesh.devices.reshape(2, 4, 2, 2, 4), ALL)
    in_specs = (P(ROW, COL, None), P(), P(), P(), P(), P(ROW, COL, None))
    out_specs = (P(ROW, COL, None), P(ROW, COL, None), P(), P(), P())
    return jax.shard_map(
        shards, mesh=torus, in_specs=in_specs, out_specs=out_specs, check_vma=False
    )
```

time: 218 us -> 140 us (0.64)
  blocking collectives: 0 us -> 66.9 us
  waiting for transfers between devices: 72.7 us -> 11 us
  local copies, waits for them, and re-layouts: 57.7 us -> 8.32 us
  starting transfers between devices: 34.2 us -> 11 us
  other arithmetic: 19.7 us -> 2.41 us
  Pallas kernels: 26.9 us -> 38.6 us
  matrix products: 3.63 us -> 0 us
    all_to_all x0 -> x3, blocking collectives: none -> 66.9 us  [exchange(): return lax.all_to_all(value, axes, split_axis=0, concat_axis=0, tiled=True)]
    all_to_all x5 -> x2, waiting for transfers between devices: 72.7 us -> 11 us  [exchange(): return lax.all_to_all(value, axes, split_axis=0, concat_axis=0, tiled=True)]
    reshape x13 -> x3, local copies, waits for them, and re-layouts: 29.1 us -> 0.48 us  [the longest x1 0.25 us: shards(): shares = everyone[:, :5].reshape(n_row // 2, 2, n_col, 5, channels)]
    all_to_all x5 -> x2, starting transfers between devices: 34.2 us -> 8.74 us  [exchange(): return lax.all_to_all(value, axes, split_axis=0, concat_axis=0, tiled=True)]
    pallas_call x1 -> x7, Pallas kernels: 26.9 us -> 38.6 us  [the longest x1 18.2 us: attend(): pl.pallas_call(attention_kernel, grid=(columns,), in_specs=[pl.BlockSpec(...]
    transpose x2 -> x3, local copies, waits for them, and re-layouts: 9.2 us -> 0.63 us  [the longest x1 0.58 us: shards(): return (attended, pair_gradient, projection_grad, small[:4].T, small[4])]
    unnamed x20 -> x14, local copies, waits for them, and re-layouts: 13.3 us -> 4.95 us
    all_to_all x1 -> x0, other arithmetic: 7.71 us -> none  [exchange(): return lax.all_to_all(value, axes, split_axis=0, concat_axis=0, tiled=True)]
  transfers between devices with their start and end apart: 5 -> 4, of which waited for: 4 -> 2; matrix products, arithmetic and copies ran while one was open for 18% -> 2% of each run, Pallas kernels for 0% -> 6%
where the time goes in v2:
time: 140 us
  blocking collectives  66.9 us (48%)
  Pallas kernels  38.6 us (28%)
  starting transfers between devices  11 us (8%)
  waiting for transfers between devices  11 us (8%)
  local copies, waits for them, and re-layouts  8.32 us (6%)
  other arithmetic  2.41 us (2%)
  between operations  1.43 us (1%)
    all_to_all x3, blocking collectives, exchange(): return lax.all_to_all(value, axes, split_axis=0, concat_axis=0, tiled=True)  66.9 us
    pallas_call x1, Pallas kernels, attend(): pl.pallas_call(attention_kernel, grid=(columns,), in_specs=[pl.BlockSpec(...  18.2 us
    all_to_all x2, waiting for transfers between devices, exchange(): return lax.all_to_all(value, axes, split_axis=0, concat_axis=0, tiled=True)  11 us
    all_to_all x2, starting transfers between devices, exchange(): return lax.all_to_all(value, axes, split_axis=0, concat_axis=0, tiled=True)  8.74 us
    pallas_call x2, Pallas kernels, call(): pl.pallas_call(kernel, out_shape=out_shape, scratch_shapes=scratch, compi...  5.27 us
    unnamed x14, local copies, waits for them, and re-layouts  4.95 us
    pallas_call x1, Pallas kernels, project(): pl.pallas_call(project_kernel, grid=(columns,), in_specs=[normed, normed,...  4.76 us
    pallas_call x1, Pallas kernels, merge(): pl.pallas_call(merge_kernel, grid=(columns,), in_specs=[block, block, pl....  4.13 us
  transfers between devices with their start and end apart: 4, of which 2 were waited for; matrix products, arithmetic and copies ran while one was open for 2% of the time, Pallas kernels for 6%

profile of v2, /device:TPU:1, one launch (start us, length us, event | category | flops | bytes accessed | tf_op | source)
XLA Modules:
  0.0 139.6 jit_solution(8262062813181811905)
XLA Ops:
  0.6 2.9 %pack.1 = bf16[16,24,1024]{2,1,0:T(8,128)(2,1)} custom-call(bf16[24,48,128]{2,1,0:T(8,128)(2,1)} %pair_ref.3, bf16[24,48,128]{2,1,0:T(8,128)(2,1)} %cot_ref.1, f32[1,128]{1,0:T(1,128)} %bitcast.51, bf16[4,128]{1,0:T(4,128)(2,1)} %bitcast.48), custom_call_target="tpu_custom_call" | custom-call | tf_op jit(solution)/shard_map/pack/pallas_call | solution.py:39
  3.5 22.8 %all_to_all.25 = bf16[16,24,1024]{2,1,0:T(8,128)(2,1)} all-to-all(bf16[16,24,1024]{2,1,0:T(8,128)(2,1)} %pack.1), channel_id=1, replica_groups=mesh['row_0'=2,'row_1'=4,'row_2'=2,'col_0'=2,'col_1'=4] {'row_0','row_1'..., dimensions={0} | all-to-all | bytes 1572864 | tf_op jit(solution)/shard_map/all_to_all | solution.py:35
  26.4 2.2 %bias_out.1 = f32[8,96,384]{2,1,0:T(8,128)} custom-call(bf16[384,1024]{1,0:T(8,128)(2,1)} %bitcast.32), custom_call_target="tpu_custom_call" | custom-call | tf_op jit(solution)/shard_map/bias_out/pallas_call | solution.py:444
  28.6 5.2 %all-to-all-start.1 = ((f32[8,96,384]{2,1,0:T(8,128)}), f32[8,96,384]{2,1,0:T(8,128)S(1)}, u32[]{:S(2)}, u32[]{:S(2)}) async-start(f32[8,96,384]{2,1,0:T(8,128)} %bias_out.1), calls=%async_computation.1 | async-start | bytes 2359296 | tf_op jit(solution)/shard_map/all_to_all | solution.py:35
  33.8 1.3 collective-permute-start
  35.3 0.8 fusion.6
  36.1 0.9 copy.22.w_ref
  38.2 0.9 copy-done.1
  39.1 4.8 %project.1 = (bf16[3,384,128]{2,1,0:T(8,128)(2,1)}, bf16[3,384,128]{2,1,0:T(8,128)(2,1)}, bf16[3,384,128]{2,1,0:T(8,128)(2,1)}, bf16[3,384,128]{2,1,0:T(8,128)(2...) custom-call(bf16[384,1024]{1,0:T(8,128)(2,1)} %bitcast.33, ...), custom_call_target="tpu_custom_call" | custom-call | tf_op jit(solution)/shard_map/project/pallas_call | solution.py:129
  43.9 6.2 %all-to-all-done.1.got_ref = f32[8,96,384]{2,1,0:T(8,128)S(1)} async-done(((f32[8,96,384]{2,1,0:T(8,128)}), f32[8,96,384]{2,1,0:T(8,128)S(1)}, u32[]{:S(2)}, u32[]{:S(2)}) %all-to-all-start.1) | async-done | bytes 1179680 | tf_op jit(solution)/shard_map/all_to_all | solution.py:35
  50.1 1.0 copy-done.2
  51.1 18.2 %attention.1 = (bf16[3,384,640]{2,1,0:T(8,128)(2,1)}, bf16[8,112,384]{2,1,0:T(8,128)(2,1)}) custom-call(s32[1]{0:T(128)S(6)} %copy.30.valid_ref, f32[8,96,384]{2,1,0:T(8,128)} %copy-done.2, bf16[384,1024]{1,0:T(8,128)(2,1)} %bitcast.35, bf16[384,1024]{1,0:T(8,128)(2,1)} %copy-done.1, bf16[384,1024]{1,0:T(8,128)(2,1)} %bitcast.36, ...), custom_call_target="tpu_custom_call" | custom-call | tf_op jit(solution)/shard_map/attention/pallas_call | solution.py:257
  69.2 0.9 collective-permute-start.1
  70.2 3.5 %all-to-all-start.2 = ((bf16[8,112,384]{2,1,0:T(8,128)(2,1)}), bf16[8,112,384]{2,1,0:T(8,128)(2,1)S(1)}, u32[]{:S(2)}, u32[]{:S(2)}) async-start(bf16[8,112,384]{2,1,0:T(8,128)(2,1)} %get-tuple-element.30), calls=%async_computation.2 | async-start | bytes 1376256 | tf_op jit(solution)/shard_map/all_to_all | solution.py:35
  73.8 0.8 maximum_maximum_fusion.w_ref
  74.7 1.1 copy-done.4
  75.8 4.1 %merge.1.main_ref = bf16[384,768]{1,0:T(8,128)(2,1)} custom-call(bf16[3,384,640]{2,1,0:T(8,128)(2,1)} %get-tuple-element.31.acts_ref, bf16[3,384,640]{2,1,0:T(8,128)(2,1)} %copy-done.4, bf16[5,256,128]{2,1,0:T(8,128)(2,1)} %maximum_maximum_fusion.w_ref), custom_call_target="tpu_custom_call" | custom-call | tf_op jit(solution)/shard_map/merge/pallas_call | solution.py:309
  79.9 4.8 %all-to-all-done.2.got_ref = bf16[8,112,384]{2,1,0:T(8,128)(2,1)S(1)} async-done(((bf16[8,112,384]{2,1,0:T(8,128)(2,1)}), bf16[8,112,384]{2,1,0:T(8,128)(2,1)S(1)}, u32[]{:S(2)}, u32[]{:S(2)}) %all-to-all-start.2) | async-done | bytes 688160 | tf_op jit(solution)/shard_map/all_to_all | solution.py:35
  84.7 0.9 copy-done.3
  85.6 2.4 %sum.1 = bf16[16,24,1152]{2,1,0:T(8,128)(2,1)} custom-call(bf16[8,112,384]{2,1,0:T(8,128)(2,1)} %copy-done.3, bf16[384,768]{1,0:T(8,128)(2,1)} %merge.1.main_ref), custom_call_target="tpu_custom_call" | custom-call | tf_op jit(solution)/shard_map/sum/pallas_call | solution.py:39
  88.0 20.1 %all_to_all.26.got_ref = bf16[16,24,1152]{2,1,0:T(8,128)(2,1)} all-to-all(bf16[16,24,1152]{2,1,0:T(8,128)(2,1)} %sum.1), channel_id=1, replica_groups=mesh['row_0'=2,'row_1'=4,'row_2'=2,'col_0'=2,'col_1'=4] {'row_0','row_1'..., dimensions={0} | all-to-all | bytes 1769472 | tf_op jit(solution)/shard_map/all_to_all | solution.py:35
  108.8 4.1 %finish.1 = (bf16[24,48,128]{2,1,0:T(8,128)(2,1)}, f32[24,48,128]{2,1,0:T(8,128)}, f32[128,10,128]{2,1,0:T(8,128)}) custom-call(s32[1]{0:T(128)} %bitcast.core_ref, bf16[16,24,1152]{2,1,0:T(8,128)(2,1)} %all_to_all.26.got_ref, bf16[24,48,128]{2,1,0:T(8,128)(2,1)} %pair_ref.3, f32[1,128]{1,0:T(1,128)} %bitcast.52, bf16[4,128]{1,0:T(4,128)(2,1)} %bitcast.49, ...), custom_call_target="tpu_custom_call" | custom-call | tf_op jit(solution)/shard_map/finish/pallas_call | solution.py:461
  112.9 23.9 %all_to_all.27 = f32[128,10,128]{2,1,0:T(8,128)S(1)} all-to-all(f32[128,10,128]{2,1,0:T(8,128)} %get-tuple-element.34), channel_id=1, replica_groups=mesh['row_0'=2,'row_1'=4,'row_2'=2,'col_0'=2,'col_1'=4] {'row_0','row_1'..., dimensions={0} | all-to-all | bytes 1310720 | tf_op jit(solution)/shard_map/all_to_all | solution.py:35
  138.7 0.9 copy.28
  (33 shorter events, 3.5 us)
Async XLA Ops:
  28.6 5.2 %copy-start = (bf16[16,24,1024]{2,1,0:T(8,128)(2,1)S(1)}, bf16[16,24,1024]{2,1,0:T(8,128)(2,1)}, u32[]{:S(2)}) copy-start(bf16[16,24,1024]{2,1,0:T(8,128)(2,1)} %all_to_all.25) | copy-start | bytes 2359300
  28.6 6.6 %slice-start = ((bf16[5,128,128]{2,1,0:T(8,128)(2,1)}), bf16[4,128,128]{2,1,0:T(8,128)(2,1)S(1)}, s32[]{:S(2)}) async-start(bf16[5,128,128]{2,1,0:T(8,128)(2,1)} %param.8), calls=%async_computation.5 | async-start | bytes 262144 | tf_op jit(solution)/shard_map/slice | solution.py:415
  28.6 21.5 %all-to-all-start.1 = ((f32[8,96,384]{2,1,0:T(8,128)}), f32[8,96,384]{2,1,0:T(8,128)S(1)}, u32[]{:S(2)}, u32[]{:S(2)}) async-start(f32[8,96,384]{2,1,0:T(8,128)} %bias_out.1), calls=%async_computation.1 | async-start | bytes 2359296 | tf_op jit(solution)/shard_map/all_to_all | solution.py:35
  33.8 3.8 %slice-start.1 = ((bf16[5,128,128]{2,1,0:T(8,128)(2,1)}), bf16[1,128,128]{2,1,0:T(8,128)(2,1)S(1)}, s32[]{:S(2)}) async-start(bf16[5,128,128]{2,1,0:T(8,128)(2,1)} %param.8), calls=%async_computation.6 | async-start | bytes 65536 | tf_op jit(solution)/shard_map/slice | solution.py:416
  33.8 4.5 %collective-permute-start = (bf16[384,1024]{1,0:T(8,128)(2,1)S(1)}, bf16[384,1024]{1,0:T(8,128)(2,1)S(1)}, u32[]{:S(2)}, u32[]{:S(2)}) collective-permute-start(bf16[384,1024]{1,0:T(8,128)(2,1)S(1)} %bitcast.37), channel_id=1, source_target_pairs={{0,8},{8,0},{1,9},{9,1},{2,10},{10,2},{3,11},{11,3},{4,12},{12,4},... | collective-permute-start | bytes 2359304 | tf_op jit(solution)/shard_map/ppermute | solution.py:453
  38.2 0.9 copy-start.1
  50.1 1.0 copy-start.2
  69.2 5.4 %collective-permute-start.1 = (bf16[3,384,640]{2,1,0:T(8,128)(2,1)}, bf16[3,384,640]{2,1,0:T(8,128)(2,1)S(1)}, u32[]{:S(2)}, u32[]{:S(2)}) collective-permute-start(bf16[3,384,640]{2,1,0:T(8,128)(2,1)} %get-tuple-element.31.acts_ref), channel_id=1, source_target_pairs={{0,8},{8,0},{1,9},{9,1},{2,10},{10,2},{3,11},{11,3},{4,12},{12,4},... | collective-permute-start | bytes 4423688 | tf_op jit(solution)/shard_map/ppermute | solution.py:457
  70.2 14.6 %all-to-all-start.2 = ((bf16[8,112,384]{2,1,0:T(8,128)(2,1)}), bf16[8,112,384]{2,1,0:T(8,128)(2,1)S(1)}, u32[]{:S(2)}, u32[]{:S(2)}) async-start(bf16[8,112,384]{2,1,0:T(8,128)(2,1)} %get-tuple-element.30), calls=%async_computation.2 | async-start | bytes 1376256 | tf_op jit(solution)/shard_map/all_to_all | solution.py:35
  74.7 1.1 copy-start.4
  79.9 28.2 %copy-start.5 = (bf16[128,4]{0,1:T(4,128)(2,1)S(1)}, bf16[128,4]{0,1:T(4,128)(2,1)}, u32[]{:S(2)}) copy-start(bf16[128,4]{0,1:T(4,128)(2,1)} %param.9) | copy-start | bytes 3076
  84.7 0.9 copy-start.3

commit v3 on v2

--- a/solution.py
+++ b/solution.py
@@ -14,6 +14,7 @@
 CORE = "row_2"
 EPS = 1e-05
 MASKED = -1000000000.0
+LOG2E = 1.4426950408889634
 PARTS = 4
 F32 = jnp.float32
 BF16 = jnp.bfloat16
@@ -146,7 +147,7 @@
     valid_ref, got_ref, normed_ref, twin_normed_ref, cot_ref, twin_cot_ref,
     query_ref, key_ref, value_ref, d_context_ref,
     query_t_ref, key_t_ref, value_t_ref, d_context_t_ref, gate_t_ref, d_gated_t_ref,
-    acts_ref, sent_ref, bias_s, total, grads_s, ctx_t, dq_t, d_scores_s, weights_s, query_s, d_context_s,
+    acts_ref, sent_ref, bias_s, total, grads_s, d_scores_s, weights_s, right_s,
 ):
     step = pl.program_id(0)
     steps = pl.num_programs(0)
@@ -164,57 +165,59 @@
             for h in range(2):
                 at = (2 * k + h) * cols
                 pieces = [got_ref[c, :, at : at + cols] for c in range(blocks)]
-                bias_s[h, k * high : (k + 1) * high, :] = jnp.concatenate(pieces, axis=1)
+                bias_s[h, k * high : (k + 1) * high, :] = jnp.concatenate(pieces, axis=1) * LOG2E
         total[...] = jnp.zeros_like(total)
         grads_s[...] = jnp.zeros_like(grads_s)
 
     query = query_ref[0]
-    key = key_ref[0]
-    value = value_ref[0]
     d_context = d_context_ref[0]
     lane = lax.broadcasted_iota(jnp.int32, (rows, channels), 1)
-    keep = lax.broadcasted_iota(jnp.int32, (rows, rows), 0) < valid_ref[0]
+    sure = rows // 2
+    keep = lax.broadcasted_iota(jnp.int32, (rows - sure, rows), 0) + sure < valid_ref[0]
     zero = jnp.zeros((rows, channels), BF16)
     for slot in range(slots):
         mine = (lane >= slot * width) & (lane < (slot + 1) * width)
-        key_h = jnp.where(mine, key, zero)
-        value_h = jnp.where(mine, value, zero)
         here = slice(slot * rows, (slot + 1) * rows)
         part = slice(slot * width, (slot + 1) * width)
-        query_s[here, :] = jnp.where(mine, query, zero)
-        d_context_s[here, :] = jnp.where(mine, d_context, zero)
-        scores = nn(key_h, query_t_ref[0]) * scale + bias_s[slot % 2]
-        scores = jnp.where(keep, scores, MASKED)
+        right_s[here, :channels] = jnp.where(mine, query, zero)
+        right_s[here, channels:] = jnp.where(mine, d_context, zero)
+        scores = nn(key_ref[0, :, part], query_t_ref[0, part]) * (scale * LOG2E) + bias_s[slot % 2]
+        masked = jnp.where(keep, scores[sure:], MASKED * LOG2E)
+        scores = jnp.concatenate([scores[:sure], masked], axis=0)
         top = jnp.max(scores, axis=0, keepdims=True)
-        grown = jnp.exp(scores - top)
-        probs = grown * (1.0 / jnp.sum(grown, axis=0, keepdims=True))
-        weights_b = probs.astype(BF16)
-        weights_s[:, here] = weights_b
-        ctx_t[part, :] = nn(value_t_ref[0, part, :], weights_b).astype(BF16)
-        d_probs = nn(value_h, d_context_t_ref[0])
-        delta = jnp.sum(probs * d_probs, axis=0, keepdims=True)
+        grown = jnp.exp2(scores - top)
+        inverse = 1.0 / jnp.sum(grown, axis=0, keepdims=True)
+        probs = grown * inverse
+        weights_s[:, here] = probs.astype(BF16)
+        d_probs = nn(value_ref[0, :, part], d_context_t_ref[0, part])
+        delta = jnp.sum(grown * d_probs, axis=0, keepdims=True) * inverse
         d_scores = probs * (d_probs - delta)
         total[slot % 2] += d_scores
-        d_scores_b = d_scores.astype(BF16)
-        d_scores_s[:, here] = d_scores_b
-        dq_t[part, :] = (nn(key_t_ref[0, part, :], d_scores_b) * scale).astype(BF16)
-    d_key = (nn(d_scores_s[...], query_s[...]) * scale).astype(BF16)
-    d_value = nn(weights_s[...], d_context_s[...]).astype(BF16)
+        d_scores_s[:, here] = d_scores.astype(BF16)
+    blocks_t = [
+        (nn(value_t_ref[0, s * width : (s + 1) * width], weights_s[:, s * rows : (s + 1) * rows]),
+         nn(key_t_ref[0, s * width : (s + 1) * width], d_scores_s[:, s * rows : (s + 1) * rows]))
+        for s in range(slots)
+    ]
+    context_t = jnp.concatenate([one for one, _ in blocks_t], axis=0).astype(BF16).astype(F32)
+    d_query_t = (jnp.concatenate([two for _, two in blocks_t], axis=0) * scale).astype(BF16)
+    d_key = (nn(d_scores_s[...], right_s[:, :channels]) * scale).astype(BF16)
+    d_value = nn(weights_s[...], right_s[:, channels:]).astype(BF16)
     gate_t = gate_t_ref[0]
-    context_t = ctx_t[...].astype(F32)
     gated_t = (gate_t * context_t).astype(BF16)
     d_gate_t = (d_gated_t_ref[0] * context_t * gate_t * (1.0 - gate_t)).astype(BF16)
-    acts = [turned(gated_t), turned(dq_t[...]), d_key, d_value, turned(d_gate_t)]
+    acts = [turned(gated_t), turned(d_query_t), d_key, d_value, turned(d_gate_t)]
     for m in range(5):
         acts_ref[0, :, m * channels : (m + 1) * channels] = acts[m]
-    right = jnp.concatenate(acts[1:], axis=1)
-    own = nn(turned(normed_ref[...]), right)
-    other = nn(turned(twin_normed_ref[...]), right)
+    left = jnp.concatenate([d_query_t, turned(d_key), turned(d_value), d_gate_t], axis=0)
+    normed = jnp.concatenate([normed_ref[...], twin_normed_ref[...]], axis=1)
+    products = nn(left, normed)
     for m in range(4):
-        at = slice(m * channels, (m + 1) * channels)
-        grads_s[:channels, at] += jnp.where(lane[:channels] < half, own[:, at], other[:, at])
+        near = products[m * channels : m * channels + half, :channels]
+        far = products[m * channels + half : (m + 1) * channels, channels:]
+        grads_s[m * half : (m + 1) * half, :] += near + far
     last = nn(gated_t[:half], cot_ref[...]) + nn(gated_t[half:], twin_cot_ref[...])
-    grads_s[channels:, :channels] += last
+    grads_s[4 * half :, :] += last
 
     @pl.when(step == steps - 1)
     def _():
@@ -225,18 +228,7 @@
                 for h in range(2)
             ]
             sent_ref[c, :high, :] = jnp.concatenate(pieces, axis=1).astype(BF16)
-        sums = []
-        for m in range(4):
-            at = slice(m * channels, (m + 1) * channels)
-            both = grads_s[:channels, at]
-            sums.append(both + pltpu.roll(both, half, 1))
-        left = lane[:channels] < half
-        grads = [
-            jnp.where(left, sums[0], sums[1]),
-            jnp.where(left, sums[2], sums[3]),
-            grads_s[channels:, :channels],
-        ]
-        grads = jnp.concatenate(grads, axis=0)
+        grads = grads_s[...]
         share = grads.shape[0] // blocks
         rest = sent_ref.shape[1] - high
         spare = jnp.zeros((3 * rest - share, channels), F32)
@@ -275,13 +267,10 @@
         scratch_shapes=[
             pltpu.VMEM((2, rows, rows), F32),
             pltpu.VMEM((2, rows, rows), F32),
-            pltpu.VMEM((channels + channels // 2, 4 * channels), F32),
-            pltpu.VMEM((channels, rows), BF16),
-            pltpu.VMEM((channels, rows), BF16),
+            pltpu.VMEM((5 * channels // 2, channels), F32),
             pltpu.VMEM((rows, 4 * rows), BF16),
             pltpu.VMEM((rows, 4 * rows), BF16),
-            pltpu.VMEM((4 * rows, channels), BF16),
-            pltpu.VMEM((4 * rows, channels), BF16),
+            pltpu.VMEM((4 * rows, 2 * channels), BF16),
         ],
         compiler_params=pltpu.CompilerParams(vmem_limit_bytes=56 << 20),
         name="attention",
@@ -311,7 +300,7 @@
         grid=(columns,),
         in_specs=[block, block, pl.BlockSpec(w.shape, lambda j: (0, 0, 0))],
         out_specs=pl.BlockSpec((rows, 2 * columns * channels), lambda j: (0, 0)),
-        out_shape=jax.ShapeDtypeStruct((rows, 2 * columns * channels), BF16),
+        out_shape=jax.ShapeDtypeStruct((rows, 2 * columns * channels + 256), BF16),
         compiler_params=pltpu.CompilerParams(vmem_limit_bytes=56 << 20),
         name="merge",
     )(acts, came, w)
@@ -320,30 +309,43 @@
 def sum_kernel(got_ref, main_ref, out_ref):
     blocks, high, lanes = got_ref.shape
     owners, rows, wide = out_ref.shape
-    main = main_ref.shape[1]
     part = lanes // PARTS
-    rest = high - part
     total = got_ref[0].astype(F32)
     for c in range(1, blocks):
         total = total + got_ref[c].astype(F32)
-    grads = jnp.concatenate([total[part:, k * 128 : (k + 1) * 128] for k in range(lanes // 128)], axis=0)
+    grads = jnp.concatenate([total[part:, k * 128 : (k + 1) * 128] for k in range(3)], axis=0)
     share = 5
-    pad = jnp.zeros((rows, 256 - 2 * part), BF16)
-    gap = jnp.zeros((8 - share, 128), F32)
+    gap = jnp.zeros((rows - 4 * share, 64), F32)
     for owner in range(owners):
         across, down = divmod(owner, part // rows)
         block = total[down * rows : (down + 1) * rows, across * part : (across + 1) * part]
-        out_ref[owner, :, :main] = main_ref[owner * rows : (owner + 1) * rows, :]
-        out_ref[owner, :, main : main + 256] = jnp.concatenate([*coarse_fine(block), pad], axis=1)
+        coarse = block.astype(BF16).astype(F32)
         mine = grads[owner // 2 * share : (owner // 2 + 1) * share]
-        coarse = mine.astype(BF16).astype(F32)
-        stack = jnp.concatenate([coarse, gap, mine - coarse, gap, jnp.zeros((8, 128), F32)], axis=0)
-        out_ref[owner, :, main + 256 :] = stack.astype(BF16)
+        near = mine.astype(BF16).astype(F32)
+        far = mine - near
+        stack = jnp.concatenate([near[:, :64], near[:, 64:], far[:, :64], far[:, 64:], gap], axis=0)
+        out_ref[owner] = jnp.concatenate([coarse, block - coarse, stack], axis=1).astype(BF16)
+
+
+def add_sums(got, main, n_row):
+    rows, wide = main.shape
+    blocked = main.reshape(n_row, rows // n_row, wide)
+    spec = pl.BlockSpec((n_row, rows // n_row, 256), lambda i: (0, 0, wide // 256 - 1))
+    return pl.pallas_call(
+        sum_kernel,
+        grid=(1,),
+        in_specs=[pl.BlockSpec(got.shape, lambda i: (0, 0, 0)), pl.BlockSpec(memory_space=pl.ANY)],
+        out_specs=spec,
+        out_shape=jax.ShapeDtypeStruct(blocked.shape, BF16),
+        input_output_aliases={1: 0},
+        compiler_params=pltpu.CompilerParams(vmem_limit_bytes=56 << 20),
+        name="sum",
+    )(got, blocked)
 
 
 def finish_kernel(
-    core_ref, got_ref, pair_ref, gain_ref, bias_weight_ref, repeated_ref,
-    attended_ref, gradient_ref, last_ref, moved_s, d_normed_s, d_bias_s,
+    core_ref, got_ref, pair_ref, gain_ref, bias_weight_ref,
+    d_normed_ref, last_ref, d_bias_s,
 ):
     owners, rows, wide = got_ref.shape
     cols, channels = pair_ref.shape[1:]
@@ -354,45 +356,72 @@
     for owner in range(owners):
         for k in range(ncols):
             column = pl.ds(owner * ncols + k, rows, stride=cols)
-            at = k * channels
-            moved_s[column, :] = got_ref[owner, :, at : at + channels].astype(F32)
             at = (ncols + k) * channels
-            d_normed_s[column, :] = got_ref[owner, :, at : at + channels].astype(F32)
-    attended_ref[...] = moved_s[...].astype(BF16).reshape(attended_ref.shape)
-    grads = [jnp.zeros((rows, 128), F32), jnp.zeros((rows, 128), F32)]
+            d_normed_ref[column, :] = got_ref[owner, :, at : at + channels].astype(F32)
+    sums = [jnp.zeros((rows, 256), F32), jnp.zeros((rows, 256), F32)]
     for owner in range(owners):
-        grads[owner % 2] = grads[owner % 2] + got_ref[owner, :, main + 256 :].astype(F32)
-    grads = jnp.where(core_ref[0] == 0, grads[0], grads[1])
+        sums[owner % 2] = sums[owner % 2] + got_ref[owner, :, main:].astype(F32)
     for core in range(2):
-        block = jnp.zeros((rows, 2 * cols), F32)
-        for owner in range(core, owners, 2):
-            block = block + got_ref[owner, :, main : main + 2 * cols].astype(F32)
-            block = block + got_ref[owner, :, main + 2 * cols : main + 4 * cols].astype(F32)
+        block = sums[core][:, : 2 * cols] + sums[core][:, 2 * cols : 4 * cols]
         block = block.astype(BF16).astype(F32)
         for h in range(2):
             at = pl.ds(2 * core + h, rows, stride=heads)
             d_bias_s[at, :] = block[:, h * cols : (h + 1) * cols]
+    grads = jnp.where(core_ref[0] == 0, sums[0], sums[1])[:, 4 * cols :]
+    grads = jnp.concatenate([grads[:5] + grads[10:15], grads[5:10] + grads[15:20]], axis=1)
     d_bias_t = jnp.transpose(d_bias_s[...]).astype(BF16)
     row = lax.broadcasted_iota(jnp.int32, (rows * heads, channels), 0)
+    repeated = jnp.concatenate([bias_weight_ref[...].astype(F32)] * rows, axis=0).astype(BF16)
     weight_part = jnp.zeros((heads, channels), F32)
     for a in range(rows):
         here = slice(a * cols, (a + 1) * cols)
         mine = (row >= a * heads) & (row < (a + 1) * heads)
-        weight = jnp.where(mine, repeated_ref[...], jnp.zeros((rows * heads, channels), BF16))
-        d_normed_s[here, :] += nn(d_bias_t, weight)
+        weight = jnp.where(mine, repeated, jnp.zeros((rows * heads, channels), BF16))
+        d_normed_ref[here, :] += nn(d_bias_t, weight)
         d_bias_a = d_bias_s[a * heads : (a + 1) * heads, :].astype(BF16)
         weight_part = weight_part + nn(d_bias_a, normed[here])
-    d_normed = d_normed_s[...]
-    gain_part = jnp.sum(d_normed * xhat, axis=0, keepdims=True)
-    last = jnp.concatenate([grads[:5] + grads[8:13], weight_part, gain_part], axis=0)
-    last_ref[...] = jnp.broadcast_to(last[None], last_ref.shape)
-    scaled = d_normed * gain_ref[...]
+    gain_part = jnp.sum(d_normed_ref[...] * xhat, axis=0, keepdims=True)
+    small = jnp.concatenate([weight_part, gain_part], axis=0)
+    for t in range(5):
+        pair = jnp.concatenate([grads[t : t + 1], small[t : t + 1]], axis=0)
+        last_ref[:, t] = jnp.broadcast_to(pair[None], (last_ref.shape[0], 2, channels))
+
+
+def output_kernel(got_ref, d_normed_ref, pair_ref, gain_ref, attended_ref, gradient_ref, moved_s):
+    owners, rows, wide = got_ref.shape
+    cols, channels = pair_ref.shape[1:]
+    ncols = cols // owners
+    xhat, inverse, normed = normalize(pair_ref, gain_ref)
+    for owner in range(owners):
+        for k in range(ncols):
+            column = pl.ds(owner * ncols + k, rows, stride=cols)
+            moved_s[column, :] = got_ref[owner, :, k * channels : (k + 1) * channels].astype(F32)
+    attended_ref[...] = moved_s[...].astype(BF16).reshape(attended_ref.shape)
+    scaled = d_normed_ref[...] * gain_ref[...]
     gradient = inverse * (
         scaled
         - jnp.mean(scaled, axis=-1, keepdims=True)
         - xhat * jnp.mean(scaled * xhat, axis=-1, keepdims=True)
     )
     gradient_ref[...] = gradient.reshape(gradient_ref.shape)
+
+
+def gather_kernel(n_row, n_col, got_ref, grad_ref, weight_ref, gain_ref, halves_s):
+    channels = got_ref.shape[-1]
+    share = got_ref.shape[1]
+    half = channels // 2
+    for r in range(n_row):
+        for c in range(n_col):
+            at = (c * (n_row // 2) + r // 2) * share
+            halves_s[r % 2, at : at + share, :] = got_ref[r * n_col + c, :, 0, :]
+    small = jnp.sum(got_ref[:, :, 1, :], axis=0)
+    heads = weight_ref.shape[0]
+    weight_ref[...] = small[:heads]
+    gain_ref[...] = small[heads : heads + 1]
+    for m in range(5):
+        both = [halves_s[core, m * half : (m + 1) * half, :] for core in range(2)]
+        both = jnp.concatenate(both, axis=0)
+        grad_ref[m] = jnp.transpose(both) if m < 4 else both
 
 
 def shards(pair, gain, projections, bias_weight, valid_len, out_cotangent):
@@ -411,7 +440,6 @@
     weight_t = bias_weight.T
     swap = [(0, 1), (1, 0)]
     core = lax.axis_index(CORE).astype(jnp.int32)
-    repeated = jnp.tile(weight_t, (tile_rows, 1))
     halves = projections[:4].reshape(4, channels, 2, half)
     rows_out = projections[4].reshape(2, half, channels)
     own = lax.dynamic_index_in_dim(halves, core, 2, keepdims=False)
@@ -455,29 +483,28 @@
     acts, sent = attend(valid_len, got, both, twin, inner, ncols)
     summed = exchange(sent, COL)
     out = merge(acts, lax.ppermute(acts, CORE, swap), w_merge)
-    back = call(
-        sum_kernel, shape((n_row, tile_rows, main + 384), BF16), [], "sum", summed, out
-    )
-    attended, pair_gradient, last = pl.pallas_call(
+    back = exchange(add_sums(summed, out, n_row), ROW)
+    smem = pl.BlockSpec(memory_space=pltpu.SMEM)
+    vmem = pl.BlockSpec(memory_space=pltpu.VMEM)
+    d_normed, last = pl.pallas_call(
         finish_kernel,
-        in_specs=[pl.BlockSpec(memory_space=pltpu.SMEM)] + [pl.BlockSpec(memory_space=pltpu.VMEM)] * 5,
-        out_shape=[shape(pair.shape, BF16), shape(pair.shape, F32), shape((n_all, 10, channels), F32)],
-        scratch_shapes=[
-            pltpu.VMEM((tile, channels), F32), pltpu.VMEM((tile, channels), F32),
-            pltpu.VMEM((heads * tile_rows, tile_cols), F32),
-        ],
+        in_specs=[smem] + [vmem] * 4,
+        out_shape=[shape((tile, channels), F32), shape((n_all, 5, 2, channels), F32)],
+        scratch_shapes=[pltpu.VMEM((heads * tile_rows, tile_cols), F32)],
         compiler_params=pltpu.CompilerParams(vmem_limit_bytes=56 << 20),
         name="finish",
-    )(core[None], exchange(back, ROW), pair, gain_row, weight_t, repeated)
+    )(core[None], back, pair, gain_row, weight_t)
     everyone = exchange(last, ALL)
-    shares = everyone[:, :5].reshape(n_row // 2, 2, n_col, 5, channels)
-    shares = jnp.transpose(shares, (1, 2, 0, 3, 4)).reshape(2, 5 * half, channels)
-    inward = shares[:, : 2 * channels].reshape(2, 2, channels, 2, half)
-    inward = jnp.transpose(inward, (1, 3, 2, 0, 4)).reshape(4, channels, channels)
-    outward = shares[:, 2 * channels :].reshape(1, channels, channels)
-    projection_grad = jnp.concatenate([inward, outward], axis=0)
-    small = jnp.sum(everyone[:, 5:], axis=0)
-    return (attended, pair_gradient, projection_grad, small[:4].T, small[4])
+    attended, pair_gradient = call(
+        output_kernel, [shape(pair.shape, BF16), shape(pair.shape, F32)],
+        [pltpu.VMEM((tile, channels), F32)], "output", back, d_normed, pair, gain_row,
+    )
+    projection_grad, bias_weight_grad, gain_gradient = call(
+        functools.partial(gather_kernel, n_row, n_col),
+        [shape(projections.shape, F32), shape((heads, channels), F32), shape((1, channels), F32)],
+        [pltpu.VMEM((2, 5 * half, channels), F32)], "gather", everyone,
+    )
+    return (attended, pair_gradient, projection_grad, bias_weight_grad.T, gain_gradient[0])
 
 
 def solution(mesh):

time: 140 us -> 130 us (0.929)
  blocking collectives: 66.9 us -> 42.1 us
  waiting for transfers between devices: 11 us -> 22.6 us
  starting transfers between devices: 11 us -> 15.7 us
  local copies, waits for them, and re-layouts: 8.32 us -> 5.84 us
    all_to_all x3 -> x2, blocking collectives: 66.9 us -> 42.1 us  [exchange(): return lax.all_to_all(value, axes, split_axis=0, concat_axis=0, tiled=True)]
    all_to_all x2 -> x3, waiting for transfers between devices: 11 us -> 22.6 us  [exchange(): return lax.all_to_all(value, axes, split_axis=0, concat_axis=0, tiled=True)]
    all_to_all x2 -> x3, starting transfers between devices: 8.74 us -> 13.4 us  [exchange(): return lax.all_to_all(value, axes, split_axis=0, concat_axis=0, tiled=True)]
    pallas_call x1, Pallas kernels: 18.2 us -> 14.2 us  [attend(): pl.pallas_call(attention_kernel, grid=(columns,), in_specs=[pl.BlockSpec(...]
    pallas_call x2 -> x3, Pallas kernels: 5.27 us -> 8.35 us  [call(): pl.pallas_call(kernel, out_shape=out_shape, scratch_shapes=scratch, compi...]
    pallas_call x1 -> x2, Pallas kernels: 4.08 us -> 5.53 us  [the longest x1 3.24 us: shards(): pl.pallas_call(finish_kernel, in_specs=[smem] + [vmem] * 4, out_shape=[sh...]
    unnamed x14 -> x13, local copies, waits for them, and re-layouts: 4.95 us -> 4.86 us
  transfers between devices with their start and end apart: 4 -> 5, of which waited for: 2 -> 3; matrix products, arithmetic and copies ran while one was open for 2% -> 3% of each run, Pallas kernels for 6% -> 9%
where the time goes in v3:
time: 130 us; the launch traced here: 129 us
  blocking collectives  42.1 us (32%)
  Pallas kernels  39.2 us (30%)
  waiting for transfers between devices  22.6 us (17%)
  starting transfers between devices  15.7 us (12%)
  local copies, waits for them, and re-layouts  5.84 us (4%)
  other arithmetic  2.22 us (2%)
  between operations  1.37 us (1%)
    all_to_all x2, blocking collectives, exchange(): return lax.all_to_all(value, axes, split_axis=0, concat_axis=0, tiled=True)  42.1 us
    all_to_all x3, waiting for transfers between devices, exchange(): return lax.all_to_all(value, axes, split_axis=0, concat_axis=0, tiled=True)  22.6 us
    pallas_call x1, Pallas kernels, attend(): pl.pallas_call(attention_kernel, grid=(columns,), in_specs=[pl.BlockSpec(...  14.2 us
    all_to_all x3, starting transfers between devices, exchange(): return lax.all_to_all(value, axes, split_axis=0, concat_axis=0, tiled=True)  13.4 us
    pallas_call x3, Pallas kernels, call(): pl.pallas_call(kernel, out_shape=out_shape, scratch_shapes=scratch, compi...  8.35 us
    unnamed x13, local copies, waits for them, and re-layouts  4.86 us
    pallas_call x1, Pallas kernels, project(): pl.pallas_call(project_kernel, grid=(columns,), in_specs=[normed, normed,...  4.75 us
    pallas_call x1, Pallas kernels, merge(): pl.pallas_call(merge_kernel, grid=(columns,), in_specs=[block, block, pl....  4.17 us
  transfers between devices with their start and end apart: 5, of which 3 were waited for; matrix products, arithmetic and copies ran while one was open for 3% of the time, Pallas kernels for 9%

profile of v3, /device:TPU:1, one launch (start us, length us, event | category | flops | bytes accessed | tf_op | source)
XLA Modules:
  0.0 129.1 jit_solution(4594077286523902170)
XLA Ops:
  0.6 2.9 %pack.1 = bf16[16,24,1024]{2,1,0:T(8,128)(2,1)} custom-call(bf16[24,48,128]{2,1,0:T(8,128)(2,1)} %pair_ref.5, bf16[24,48,128]{2,1,0:T(8,128)(2,1)} %cot_ref.1, f32[1,128]{1,0:T(1,128)} %bitcast.31, bf16[4,128]{1,0:T(4,128)(2,1)} %bitcast.34), custom_call_target="tpu_custom_call" | custom-call | tf_op jit(solution)/shard_map/pack/pallas_call | solution.py:40
  3.5 22.8 %all_to_all.25 = bf16[16,24,1024]{2,1,0:T(8,128)(2,1)} all-to-all(bf16[16,24,1024]{2,1,0:T(8,128)(2,1)} %pack.1), channel_id=1, replica_groups=mesh['row_0'=2,'row_1'=4,'row_2'=2,'col_0'=2,'col_1'=4] {'row_0','row_1'..., dimensions={0} | all-to-all | bytes 1572864 | tf_op jit(solution)/shard_map/all_to_all | solution.py:36
  26.3 2.2 %bias_out.1 = f32[8,96,384]{2,1,0:T(8,128)} custom-call(bf16[384,1024]{1,0:T(8,128)(2,1)} %bitcast.21), custom_call_target="tpu_custom_call" | custom-call | tf_op jit(solution)/shard_map/bias_out/pallas_call | solution.py:472
  28.5 5.2 %all-to-all-start.1 = ((f32[8,96,384]{2,1,0:T(8,128)}), f32[8,96,384]{2,1,0:T(8,128)S(1)}, u32[]{:S(2)}, u32[]{:S(2)}) async-start(f32[8,96,384]{2,1,0:T(8,128)} %bias_out.1), calls=%async_computation.1 | async-start | bytes 2359296 | tf_op jit(solution)/shard_map/all_to_all | solution.py:36
  33.8 1.3 %collective-permute-start = (bf16[384,1024]{1,0:T(8,128)(2,1)S(1)}, bf16[384,1024]{1,0:T(8,128)(2,1)S(1)}, u32[]{:S(2)}, u32[]{:S(2)}) collective-permute-start(bf16[384,1024]{1,0:T(8,128)(2,1)S(1)} %bitcast.26), channel_id=1, source_target_pairs={{0,8},{8,0},{1,9},{9,1},{2,10},{10,2},{3,11},{11,3},{4,12},{12,4},... | collective-permute-start | bytes 2359304 | tf_op jit(solution)/shard_map/ppermute | solution.py:481
  38.2 0.9 copy-done.1
  39.1 4.8 %project.1 = (bf16[3,384,128]{2,1,0:T(8,128)(2,1)}, bf16[3,384,128]{2,1,0:T(8,128)(2,1)}, bf16[3,384,128]{2,1,0:T(8,128)(2,1)}, bf16[3,384,128]{2,1,0:T(8,128)(2...) custom-call(bf16[384,1024]{1,0:T(8,128)(2,1)} %bitcast.22, ...), custom_call_target="tpu_custom_call" | custom-call | tf_op jit(solution)/shard_map/project/pallas_call | solution.py:130
  43.8 6.2 %all-to-all-done.1.got_ref = f32[8,96,384]{2,1,0:T(8,128)S(1)} async-done(((f32[8,96,384]{2,1,0:T(8,128)}), f32[8,96,384]{2,1,0:T(8,128)S(1)}, u32[]{:S(2)}, u32[]{:S(2)}) %all-to-all-start.1) | async-done | bytes 1179680 | tf_op jit(solution)/shard_map/all_to_all | solution.py:36
  50.0 1.0 copy-done.2
  51.1 14.2 %attention.1 = (bf16[3,384,640]{2,1,0:T(8,128)(2,1)}, bf16[8,112,384]{2,1,0:T(8,128)(2,1)}) custom-call(s32[1]{0:T(128)S(6)} %copy.19.valid_ref, f32[8,96,384]{2,1,0:T(8,128)} %copy-done.2, bf16[384,1024]{1,0:T(8,128)(2,1)} %bitcast.24, bf16[384,1024]{1,0:T(8,128)(2,1)} %copy-done.1, bf16[384,1024]{1,0:T(8,128)(2,1)} %bitcast.25, ...), custom_call_target="tpu_custom_call" | custom-call | tf_op jit(solution)/shard_map/attention/pallas_call | solution.py:249
  65.3 0.9 collective-permute-start.1
  66.2 3.5 %all-to-all-start.2 = ((bf16[8,112,384]{2,1,0:T(8,128)(2,1)}), bf16[8,112,384]{2,1,0:T(8,128)(2,1)S(1)}, u32[]{:S(2)}, u32[]{:S(2)}) async-start(bf16[8,112,384]{2,1,0:T(8,128)(2,1)} %get-tuple-element.34), calls=%async_computation.2 | async-start | bytes 1376256 | tf_op jit(solution)/shard_map/all_to_all | solution.py:36
  70.7 1.1 copy-done.5
  71.8 4.2 %merge.1 = bf16[384,1024]{1,0:T(8,128)(2,1)} custom-call(bf16[3,384,640]{2,1,0:T(8,128)(2,1)} %get-tuple-element.35.acts_ref, bf16[3,384,640]{2,1,0:T(8,128)(2,1)} %copy-done.5, bf16[5,256,128]{2,1,0:T(8,128)(2,1)} %maximum_maximum_fusion.w_ref), custom_call_target="tpu_custom_call" | custom-call | tf_op jit(solution)/shard_map/merge/pallas_call | solution.py:298
  76.0 4.8 %all-to-all-done.2.got_ref = bf16[8,112,384]{2,1,0:T(8,128)(2,1)S(1)} async-done(((bf16[8,112,384]{2,1,0:T(8,128)(2,1)}), bf16[8,112,384]{2,1,0:T(8,128)(2,1)S(1)}, u32[]{:S(2)}, u32[]{:S(2)}) %all-to-all-start.2) | async-done | bytes 688160 | tf_op jit(solution)/shard_map/all_to_all | solution.py:36
  80.8 0.9 copy-done.3
  81.7 2.3 %sum.1 = bf16[16,24,1024]{2,1,0:T(8,128)(2,1)} custom-call(bf16[8,112,384]{2,1,0:T(8,128)(2,1)} %copy-done.3, bf16[16,24,1024]{2,1,0:T(8,128)(2,1)} %bitcast.27), custom_call_target="tpu_custom_call", output_to_operand_aliasing={{}: (1, {})} | custom-call | tf_op jit(solution)/shard_map/sum/pallas_call | solution.py:334
  84.0 19.3 %all_to_all.26.got_ref = bf16[16,24,1024]{2,1,0:T(8,128)(2,1)} all-to-all(bf16[16,24,1024]{2,1,0:T(8,128)(2,1)} %sum.1), channel_id=1, replica_groups=mesh['row_0'=2,'row_1'=4,'row_2'=2,'col_0'=2,'col_1'=4] {'row_0','row_1'..., dimensions={0} | all-to-all | bytes 1572864 | tf_op jit(solution)/shard_map/all_to_all | solution.py:36
  103.2 3.2 %finish.1 = (f32[1152,128]{1,0:T(8,128)}, f32[128,5,2,128]{3,2,1,0:T(2,128)}) custom-call(s32[1]{0:T(128)} %bitcast.12.core_ref, bf16[16,24,1024]{2,1,0:T(8,128)(2,1)} %all_to_all.26.got_ref, bf16[24,48,128]{2,1,0:T(8,128)(2,1)} %pair_ref.5, f32[1,128]{1,0:T(1,128)} %bitcast.32, bf16[4,128]{1,0:T(4,128)(2,1)} %bitcast.35), custom_call_target="tpu_custom_call" | custom-call | tf_op jit(solution)/shard_map/finish/pallas_call | solution.py:489
  106.5 4.7 %all-to-all-start.4 = ((f32[128,5,2,128]{3,2,1,0:T(2,128)}), f32[128,5,2,128]{3,2,1,0:T(2,128)S(1)}, u32[]{:S(2)}, u32[]{:S(2)}) async-start(f32[128,5,2,128]{3,2,1,0:T(2,128)} %get-tuple-element.39), calls=%async_computation.4 | async-start | bytes 1310720 | tf_op jit(solution)/shard_map/all_to_all | solution.py:36
  111.2 3.2 %output.1 = (bf16[24,48,128]{2,1,0:T(8,128)(2,1)}, f32[24,48,128]{2,1,0:T(8,128)}) custom-call(bf16[16,24,1024]{2,1,0:T(8,128)(2,1)} %all_to_all.26.got_ref, f32[1152,128]{1,0:T(8,128)} %get-tuple-element.36.d_normed_ref, bf16[24,48,128]{2,1,0:T(8,128)(2,1)} %pair_ref.5, f32[1,128]{1,0:T(1,128)} %bitcast.33), custom_call_target="tpu_custom_call" | custom-call | tf_op jit(solution)/shard_map/output/pallas_call | solution.py:40
  114.4 11.6 %all-to-all-done.4.got_ref = f32[128,5,2,128]{3,2,1,0:T(2,128)S(1)} async-done(((f32[128,5,2,128]{3,2,1,0:T(2,128)}), f32[128,5,2,128]{3,2,1,0:T(2,128)S(1)}, u32[]{:S(2)}, u32[]{:S(2)}) %all-to-all-start.4) | async-done | bytes 655392 | tf_op jit(solution)/shard_map/all_to_all | solution.py:36
  126.0 0.9 copy-done.4
  126.9 2.2 %gather.1 = (f32[5,128,128]{2,1,0:T(8,128)}, f32[4,128]{1,0:T(4,128)}, f32[1,128]{1,0:T(1,128)}) custom-call(f32[128,5,2,128]{3,2,1,0:T(2,128)} %copy-done.4), custom_call_target="tpu_custom_call" | custom-call | tf_op jit(solution)/shard_map/gather/pallas_call | solution.py:40
  (22 shorter events, 3.3 us)
Async XLA Ops:
  28.5 5.2 %copy-start = (bf16[16,24,1024]{2,1,0:T(8,128)(2,1)S(1)}, bf16[16,24,1024]{2,1,0:T(8,128)(2,1)}, u32[]{:S(2)}) copy-start(bf16[16,24,1024]{2,1,0:T(8,128)(2,1)} %all_to_all.25) | copy-start | bytes 2359300
  28.5 6.6 %slice-start = ((bf16[5,128,128]{2,1,0:T(8,128)(2,1)}), bf16[4,128,128]{2,1,0:T(8,128)(2,1)S(1)}, s32[]{:S(2)}) async-start(bf16[5,128,128]{2,1,0:T(8,128)(2,1)} %param.8), calls=%async_computation.5 | async-start | bytes 262144 | tf_op jit(solution)/shard_map/slice | solution.py:443
  28.5 21.5 %all-to-all-start.1 = ((f32[8,96,384]{2,1,0:T(8,128)}), f32[8,96,384]{2,1,0:T(8,128)S(1)}, u32[]{:S(2)}, u32[]{:S(2)}) async-start(f32[8,96,384]{2,1,0:T(8,128)} %bias_out.1), calls=%async_computation.1 | async-start | bytes 2359296 | tf_op jit(solution)/shard_map/all_to_all | solution.py:36
  33.7 3.8 %slice-start.1 = ((bf16[5,128,128]{2,1,0:T(8,128)(2,1)}), bf16[1,128,128]{2,1,0:T(8,128)(2,1)S(1)}, s32[]{:S(2)}) async-start(bf16[5,128,128]{2,1,0:T(8,128)(2,1)} %param.8), calls=%async_computation.6 | async-start | bytes 65536 | tf_op jit(solution)/shard_map/slice | solution.py:444
  33.8 4.4 %collective-permute-start = (bf16[384,1024]{1,0:T(8,128)(2,1)S(1)}, bf16[384,1024]{1,0:T(8,128)(2,1)S(1)}, u32[]{:S(2)}, u32[]{:S(2)}) collective-permute-start(bf16[384,1024]{1,0:T(8,128)(2,1)S(1)} %bitcast.26), channel_id=1, source_target_pairs={{0,8},{8,0},{1,9},{9,1},{2,10},{10,2},{3,11},{11,3},{4,12},{12,4},... | collective-permute-start | bytes 2359304 | tf_op jit(solution)/shard_map/ppermute | solution.py:481
  38.2 0.9 copy-start.1
  50.0 1.0 copy-start.2
  65.3 5.4 %collective-permute-start.1 = (bf16[3,384,640]{2,1,0:T(8,128)(2,1)}, bf16[3,384,640]{2,1,0:T(8,128)(2,1)S(1)}, u32[]{:S(2)}, u32[]{:S(2)}) collective-permute-start(bf16[3,384,640]{2,1,0:T(8,128)(2,1)} %get-tuple-element.35.acts_ref), channel_id=1, source_target_pairs={{0,8},{8,0},{1,9},{9,1},{2,10},{10,2},{3,11},{11,3},{4,12},{12,4},... | collective-permute-start | bytes 4423688 | tf_op jit(solution)/shard_map/ppermute | solution.py:485
  66.2 14.6 %all-to-all-start.2 = ((bf16[8,112,384]{2,1,0:T(8,128)(2,1)}), bf16[8,112,384]{2,1,0:T(8,128)(2,1)S(1)}, u32[]{:S(2)}, u32[]{:S(2)}) async-start(bf16[8,112,384]{2,1,0:T(8,128)(2,1)} %get-tuple-element.34), calls=%async_computation.2 | async-start | bytes 1376256 | tf_op jit(solution)/shard_map/all_to_all | solution.py:36
  70.7 1.1 copy-start.5
  80.8 0.9 copy-start.3
  106.5 19.6 %all-to-all-start.4 = ((f32[128,5,2,128]{3,2,1,0:T(2,128)}), f32[128,5,2,128]{3,2,1,0:T(2,128)S(1)}, u32[]{:S(2)}, u32[]{:S(2)}) async-start(f32[128,5,2,128]{3,2,1,0:T(2,128)} %get-tuple-element.39), calls=%async_computation.4 | async-start | bytes 1310720 | tf_op jit(solution)/shard_map/all_to_all | solution.py:36
  126.0 0.9 copy-start.4

commit v4 on v3

--- a/solution.py
+++ b/solution.py
@@ -251,7 +251,7 @@
         grid=(columns,),
         in_specs=[
             pl.BlockSpec(memory_space=pltpu.SMEM),
-            pl.BlockSpec(got.shape, lambda j: (0, 0, 0)),
+            pl.BlockSpec(memory_space=pltpu.VMEM),
             normed, normed, cot, cot,
         ]
         + [flat] * 4
@@ -334,7 +334,7 @@
     return pl.pallas_call(
         sum_kernel,
         grid=(1,),
-        in_specs=[pl.BlockSpec(got.shape, lambda i: (0, 0, 0)), pl.BlockSpec(memory_space=pl.ANY)],
+        in_specs=[pl.BlockSpec(memory_space=pltpu.VMEM), pl.BlockSpec(memory_space=pl.ANY)],
         out_specs=spec,
         out_shape=jax.ShapeDtypeStruct(blocked.shape, BF16),
         input_output_aliases={1: 0},
@@ -477,13 +477,13 @@
         out_shape=shape((n_col, high, lanes), F32),
         name="bias_out",
     )(both)
-    got = exchange(spread, COL)
+    got = pltpu.with_memory_space_constraint(exchange(spread, COL), pltpu.VMEM)
     twin = lax.ppermute(both, CORE, swap)
     inner = project(both, twin, w, jnp.swapaxes(w, 1, 2), w_out, ncols)
     acts, sent = attend(valid_len, got, both, twin, inner, ncols)
-    summed = exchange(sent, COL)
+    summed = pltpu.with_memory_space_constraint(exchange(sent, COL), pltpu.VMEM)
     out = merge(acts, lax.ppermute(acts, CORE, swap), w_merge)
-    back = exchange(add_sums(summed, out, n_row), ROW)
+    back = pltpu.with_memory_space_constraint(exchange(add_sums(summed, out, n_row), ROW), pltpu.VMEM)
     smem = pl.BlockSpec(memory_space=pltpu.SMEM)
     vmem = pl.BlockSpec(memory_space=pltpu.VMEM)
     d_normed, last = pl.pallas_call(
@@ -494,16 +494,22 @@
         compiler_params=pltpu.CompilerParams(vmem_limit_bytes=56 << 20),
         name="finish",
     )(core[None], back, pair, gain_row, weight_t)
-    everyone = exchange(last, ALL)
-    attended, pair_gradient = call(
-        output_kernel, [shape(pair.shape, BF16), shape(pair.shape, F32)],
-        [pltpu.VMEM((tile, channels), F32)], "output", back, d_normed, pair, gain_row,
-    )
-    projection_grad, bias_weight_grad, gain_gradient = call(
+    everyone = pltpu.with_memory_space_constraint(exchange(last, ALL), pltpu.VMEM)
+    attended, pair_gradient = pl.pallas_call(
+        output_kernel,
+        in_specs=[vmem] * 4,
+        out_shape=[shape(pair.shape, BF16), shape(pair.shape, F32)],
+        scratch_shapes=[pltpu.VMEM((tile, channels), F32)],
+        compiler_params=pltpu.CompilerParams(vmem_limit_bytes=56 << 20),
+        name="output",
+    )(back, d_normed, pair, gain_row)
+    projection_grad, bias_weight_grad, gain_gradient = pl.pallas_call(
         functools.partial(gather_kernel, n_row, n_col),
-        [shape(projections.shape, F32), shape((heads, channels), F32), shape((1, channels), F32)],
-        [pltpu.VMEM((2, 5 * half, channels), F32)], "gather", everyone,
-    )
+        in_specs=[vmem],
+        out_shape=[shape(projections.shape, F32), shape((heads, channels), F32), shape((1, channels), F32)],
+        scratch_shapes=[pltpu.VMEM((2, 5 * half, channels), F32)],
+        name="gather",
+    )(everyone)
     return (attended, pair_gradient, projection_grad, bias_weight_grad.T, gain_gradient[0])
 
 

time: 130 us -> 124 us (0.954)
  Pallas kernels: 39.2 us -> 36.1 us
  local copies, waits for them, and re-layouts: 5.84 us -> 3.12 us
    pallas_call x3 -> x1, Pallas kernels: 8.35 us -> 2.9 us  [call(): pl.pallas_call(kernel, out_shape=out_shape, scratch_shapes=scratch, compi...]
    pallas_call x1 -> x3, Pallas kernels: 2.29 us -> 5.36 us  [the longest x1 3 us: shards(): pl.pallas_call(output_kernel, in_specs=[vmem] * 4, out_shape=[shape(pair....]
    unnamed x13 -> x7, local copies, waits for them, and re-layouts: 4.86 us -> 2.15 us
  transfers between devices with their start and end apart: 5 -> 5, of which waited for: 3 -> 3; matrix products, arithmetic and copies ran while one was open for 3% -> 3% of each run, Pallas kernels for 9% -> 10%
where the time goes in v4:
time: 124 us; the launch traced here: 123 us
  blocking collectives  41.8 us (34%)
  Pallas kernels  36.1 us (29%)
  waiting for transfers between devices  22.8 us (18%)
  starting transfers between devices  15.6 us (13%)
  local copies, waits for them, and re-layouts  3.12 us (3%)
  other arithmetic  2.23 us (2%)
  between operations  1.37 us (1%)
    all_to_all x2, blocking collectives, exchange(): return lax.all_to_all(value, axes, split_axis=0, concat_axis=0, tiled=True)  41.8 us
    all_to_all x3, waiting for transfers between devices, exchange(): return lax.all_to_all(value, axes, split_axis=0, concat_axis=0, tiled=True)  22.8 us
    pallas_call x1, Pallas kernels, attend(): pl.pallas_call(attention_kernel, grid=(columns,), in_specs=[pl.BlockSpec(...  13.8 us
    all_to_all x3, starting transfers between devices, exchange(): return lax.all_to_all(value, axes, split_axis=0, concat_axis=0, tiled=True)  13.3 us
    pallas_call x1, Pallas kernels, project(): pl.pallas_call(project_kernel, grid=(columns,), in_specs=[normed, normed,...  4.76 us
    pallas_call x1, Pallas kernels, merge(): pl.pallas_call(merge_kernel, grid=(columns,), in_specs=[block, block, pl....  4.17 us
    pallas_call x1, Pallas kernels, shards(): pl.pallas_call(output_kernel, in_specs=[vmem] * 4, out_shape=[shape(pair....  3 us
    pallas_call x1, Pallas kernels, shards(): pl.pallas_call(finish_kernel, in_specs=[smem] + [vmem] * 4, out_shape=[sh...  2.98 us
  transfers between devices with their start and end apart: 5, of which 3 were waited for; matrix products, arithmetic and copies ran while one was open for 3% of the time, Pallas kernels for 10%

profile of v4, /device:TPU:1, one launch (start us, length us, event | category | flops | bytes accessed | tf_op | source)
XLA Modules:
  0.0 123.0 jit_solution(3588750689491369732)
XLA Ops:
  0.6 2.9 %pack.1 = bf16[16,24,1024]{2,1,0:T(8,128)(2,1)} custom-call(bf16[24,48,128]{2,1,0:T(8,128)(2,1)} %pair_ref.5, bf16[24,48,128]{2,1,0:T(8,128)(2,1)} %cot_ref.1, f32[1,128]{1,0:T(1,128)} %bitcast.31, bf16[4,128]{1,0:T(4,128)(2,1)} %bitcast.34), custom_call_target="tpu_custom_call" | custom-call | tf_op jit(solution)/shard_map/pack/pallas_call | solution.py:40
  3.5 22.8 %all_to_all.25 = bf16[16,24,1024]{2,1,0:T(8,128)(2,1)} all-to-all(bf16[16,24,1024]{2,1,0:T(8,128)(2,1)} %pack.1), channel_id=1, replica_groups=mesh['row_0'=2,'row_1'=4,'row_2'=2,'col_0'=2,'col_1'=4] {'row_0','row_1'..., dimensions={0} | all-to-all | bytes 1572864 | tf_op jit(solution)/shard_map/all_to_all | solution.py:36
  26.4 2.2 %bias_out.1 = f32[8,96,384]{2,1,0:T(8,128)} custom-call(bf16[384,1024]{1,0:T(8,128)(2,1)} %bitcast.21), custom_call_target="tpu_custom_call" | custom-call | tf_op jit(solution)/shard_map/bias_out/pallas_call | solution.py:472
  28.6 5.2 %all-to-all-start.1 = ((f32[8,96,384]{2,1,0:T(8,128)}), f32[8,96,384]{2,1,0:T(8,128)S(1)}, u32[]{:S(2)}, u32[]{:S(2)}) async-start(f32[8,96,384]{2,1,0:T(8,128)} %bias_out.1), calls=%async_computation.1 | async-start | bytes 2359296 | tf_op jit(solution)/shard_map/all_to_all | solution.py:36
  33.8 1.3 %collective-permute-start = (bf16[384,1024]{1,0:T(8,128)(2,1)S(1)}, bf16[384,1024]{1,0:T(8,128)(2,1)S(1)}, u32[]{:S(2)}, u32[]{:S(2)}) collective-permute-start(bf16[384,1024]{1,0:T(8,128)(2,1)S(1)} %bitcast.26), channel_id=1, source_target_pairs={{0,8},{8,0},{1,9},{9,1},{2,10},{10,2},{3,11},{11,3},{4,12},{12,4},... | collective-permute-start | bytes 2359304 | tf_op jit(solution)/shard_map/ppermute | solution.py:481
  35.3 0.8 fusion.6
  36.0 0.8 copy.16.w_ref
  38.2 0.9 copy-done.1
  39.1 4.8 %project.1 = (bf16[3,384,128]{2,1,0:T(8,128)(2,1)}, bf16[3,384,128]{2,1,0:T(8,128)(2,1)}, bf16[3,384,128]{2,1,0:T(8,128)(2,1)}, bf16[3,384,128]{2,1,0:T(8,128)(2...) custom-call(bf16[384,1024]{1,0:T(8,128)(2,1)} %bitcast.22, ...), custom_call_target="tpu_custom_call" | custom-call | tf_op jit(solution)/shard_map/project/pallas_call | solution.py:130
  43.9 6.2 %all-to-all-done.1.got_ref = f32[8,96,384]{2,1,0:T(8,128)S(1)} async-done(((f32[8,96,384]{2,1,0:T(8,128)}), f32[8,96,384]{2,1,0:T(8,128)S(1)}, u32[]{:S(2)}, u32[]{:S(2)}) %all-to-all-start.1) | async-done | bytes 1179680 | tf_op jit(solution)/shard_map/all_to_all | solution.py:36
  50.1 13.8 %attention.1 = (bf16[3,384,640]{2,1,0:T(8,128)(2,1)}, bf16[8,112,384]{2,1,0:T(8,128)(2,1)}) custom-call(s32[1]{0:T(128)S(6)} %copy.19.valid_ref, f32[8,96,384]{2,1,0:T(8,128)S(1)} %all-to-all-done.1.got_ref, bf16[384,1024]{1,0:T(8,128)(2,1)} %bitcast.24, bf16[384,1024]{1,0:T(8,128)(2,1)} %copy-done.1, bf16[384,1024]{1,0:T(8,128)(2,1)} %bitcast.25, ...), custom_call_target="tpu_custom_call" | custom-call | tf_op jit(solution)/shard_map/attention/pallas_call | solution.py:249
  63.8 0.9 collective-permute-start.1
  64.8 3.5 %all-to-all-start.2 = ((bf16[8,112,384]{2,1,0:T(8,128)(2,1)}), bf16[8,112,384]{2,1,0:T(8,128)(2,1)S(1)}, u32[]{:S(2)}, u32[]{:S(2)}) async-start(bf16[8,112,384]{2,1,0:T(8,128)(2,1)} %get-tuple-element.34), calls=%async_computation.2 | async-start | bytes 1376256 | tf_op jit(solution)/shard_map/all_to_all | solution.py:36
  68.4 0.8 maximum_maximum_fusion.w_ref
  69.3 1.1 copy-done.2
  70.4 4.2 %merge.1 = bf16[384,1024]{1,0:T(8,128)(2,1)} custom-call(bf16[3,384,640]{2,1,0:T(8,128)(2,1)} %get-tuple-element.35.acts_ref, bf16[3,384,640]{2,1,0:T(8,128)(2,1)} %copy-done.2, bf16[5,256,128]{2,1,0:T(8,128)(2,1)} %maximum_maximum_fusion.w_ref), custom_call_target="tpu_custom_call" | custom-call | tf_op jit(solution)/shard_map/merge/pallas_call | solution.py:298
  74.6 4.8 %all-to-all-done.2.got_ref = bf16[8,112,384]{2,1,0:T(8,128)(2,1)S(1)} async-done(((bf16[8,112,384]{2,1,0:T(8,128)(2,1)}), bf16[8,112,384]{2,1,0:T(8,128)(2,1)S(1)}, u32[]{:S(2)}, u32[]{:S(2)}) %all-to-all-start.2) | async-done | bytes 688160 | tf_op jit(solution)/shard_map/all_to_all | solution.py:36
  79.3 1.2 sum.1
  80.5 19.0 %all_to_all.26.got_ref = bf16[16,24,1024]{2,1,0:T(8,128)(2,1)S(1)} all-to-all(bf16[16,24,1024]{2,1,0:T(8,128)(2,1)} %sum.1), channel_id=1, replica_groups=mesh['row_0'=2,'row_1'=4,'row_2'=2,'col_0'=2,'col_1'=4] {'row_0','row_1'..., dimensions={0} | all-to-all | bytes 1572864 | tf_op jit(solution)/shard_map/all_to_all | solution.py:36
  99.5 3.0 %finish.1 = (f32[1152,128]{1,0:T(8,128)}, f32[128,5,2,128]{3,2,1,0:T(2,128)}) custom-call(s32[1]{0:T(128)} %bitcast.12.core_ref, bf16[16,24,1024]{2,1,0:T(8,128)(2,1)S(1)} %all_to_all.26.got_ref, bf16[24,48,128]{2,1,0:T(8,128)(2,1)} %pair_ref.5, f32[1,128]{1,0:T(1,128)} %bitcast.32, bf16[4,128]{1,0:T(4,128)(2,1)} %bitcast.35), custom_call_target="tpu_custom_call" | custom-call | tf_op jit(solution)/shard_map/finish/pallas_call | solution.py:489
  102.5 4.5 %all-to-all-start.4 = ((f32[128,5,2,128]{3,2,1,0:T(2,128)}), f32[128,5,2,128]{3,2,1,0:T(2,128)S(1)}, u32[]{:S(2)}, u32[]{:S(2)}) async-start(f32[128,5,2,128]{3,2,1,0:T(2,128)} %get-tuple-element.39), calls=%async_computation.4 | async-start | bytes 1310720 | tf_op jit(solution)/shard_map/all_to_all | solution.py:36
  107.0 3.0 %output.1 = (bf16[24,48,128]{2,1,0:T(8,128)(2,1)}, f32[24,48,128]{2,1,0:T(8,128)}) custom-call(bf16[16,24,1024]{2,1,0:T(8,128)(2,1)S(1)} %all_to_all.26.got_ref, f32[1152,128]{1,0:T(8,128)} %get-tuple-element.36.d_normed_ref, bf16[24,48,128]{2,1,0:T(8,128)(2,1)} %pair_ref.5, f32[1,128]{1,0:T(1,128)} %bitcast.33), custom_call_target="tpu_custom_call" | custom-call | tf_op jit(solution)/shard_map/output/pallas_call | solution.py:498
  110.0 11.8 %all-to-all-done.4.got_ref = f32[128,5,2,128]{3,2,1,0:T(2,128)S(1)} async-done(((f32[128,5,2,128]{3,2,1,0:T(2,128)}), f32[128,5,2,128]{3,2,1,0:T(2,128)S(1)}, u32[]{:S(2)}, u32[]{:S(2)}) %all-to-all-start.4) | async-done | bytes 655392 | tf_op jit(solution)/shard_map/all_to_all | solution.py:36
  121.9 1.2 gather.1
  (16 shorter events, 0.9 us)
Async XLA Ops:
  28.6 5.2 %copy-start = (bf16[16,24,1024]{2,1,0:T(8,128)(2,1)S(1)}, bf16[16,24,1024]{2,1,0:T(8,128)(2,1)}, u32[]{:S(2)}) copy-start(bf16[16,24,1024]{2,1,0:T(8,128)(2,1)} %all_to_all.25) | copy-start | bytes 2359300
  28.6 6.6 %slice-start = ((bf16[5,128,128]{2,1,0:T(8,128)(2,1)}), bf16[4,128,128]{2,1,0:T(8,128)(2,1)S(1)}, s32[]{:S(2)}) async-start(bf16[5,128,128]{2,1,0:T(8,128)(2,1)} %param.8), calls=%async_computation.5 | async-start | bytes 262144 | tf_op jit(solution)/shard_map/slice | solution.py:443
  28.6 21.5 %all-to-all-start.1 = ((f32[8,96,384]{2,1,0:T(8,128)}), f32[8,96,384]{2,1,0:T(8,128)S(1)}, u32[]{:S(2)}, u32[]{:S(2)}) async-start(f32[8,96,384]{2,1,0:T(8,128)} %bias_out.1), calls=%async_computation.1 | async-start | bytes 2359296 | tf_op jit(solution)/shard_map/all_to_all | solution.py:36
  33.8 3.8 %slice-start.1 = ((bf16[5,128,128]{2,1,0:T(8,128)(2,1)}), bf16[1,128,128]{2,1,0:T(8,128)(2,1)S(1)}, s32[]{:S(2)}) async-start(bf16[5,128,128]{2,1,0:T(8,128)(2,1)} %param.8), calls=%async_computation.6 | async-start | bytes 65536 | tf_op jit(solution)/shard_map/slice | solution.py:444
  33.8 4.4 %collective-permute-start = (bf16[384,1024]{1,0:T(8,128)(2,1)S(1)}, bf16[384,1024]{1,0:T(8,128)(2,1)S(1)}, u32[]{:S(2)}, u32[]{:S(2)}) collective-permute-start(bf16[384,1024]{1,0:T(8,128)(2,1)S(1)} %bitcast.26), channel_id=1, source_target_pairs={{0,8},{8,0},{1,9},{9,1},{2,10},{10,2},{3,11},{11,3},{4,12},{12,4},... | collective-permute-start | bytes 2359304 | tf_op jit(solution)/shard_map/ppermute | solution.py:481
  38.2 0.9 copy-start.1
  63.8 5.4 %collective-permute-start.1 = (bf16[3,384,640]{2,1,0:T(8,128)(2,1)}, bf16[3,384,640]{2,1,0:T(8,128)(2,1)S(1)}, u32[]{:S(2)}, u32[]{:S(2)}) collective-permute-start(bf16[3,384,640]{2,1,0:T(8,128)(2,1)} %get-tuple-element.35.acts_ref), channel_id=1, source_target_pairs={{0,8},{8,0},{1,9},{9,1},{2,10},{10,2},{3,11},{11,3},{4,12},{12,4},... | collective-permute-start | bytes 4423688 | tf_op jit(solution)/shard_map/ppermute | solution.py:485
  64.8 14.6 %all-to-all-start.2 = ((bf16[8,112,384]{2,1,0:T(8,128)(2,1)}), bf16[8,112,384]{2,1,0:T(8,128)(2,1)S(1)}, u32[]{:S(2)}, u32[]{:S(2)}) async-start(bf16[8,112,384]{2,1,0:T(8,128)(2,1)} %get-tuple-element.34), calls=%async_computation.2 | async-start | bytes 1376256 | tf_op jit(solution)/shard_map/all_to_all | solution.py:36
  69.3 1.1 copy-start.2
  102.5 19.4 %all-to-all-start.4 = ((f32[128,5,2,128]{3,2,1,0:T(2,128)}), f32[128,5,2,128]{3,2,1,0:T(2,128)S(1)}, u32[]{:S(2)}, u32[]{:S(2)}) async-start(f32[128,5,2,128]{3,2,1,0:T(2,128)} %get-tuple-element.39), calls=%async_computation.4 | async-start | bytes 1310720 | tf_op jit(solution)/shard_map/all_to_all | solution.py:36

commit v5 on v4

--- a/solution.py
+++ b/solution.py
@@ -41,9 +41,24 @@
         kernel,
         out_shape=out_shape,
         scratch_shapes=scratch,
-        compiler_params=pltpu.CompilerParams(vmem_limit_bytes=56 << 20),
+        compiler_params=pltpu.CompilerParams(vmem_limit_bytes=24 << 20),
         name=name,
     )(*operands)
+
+
+def resident(value):
+    return pltpu.with_memory_space_constraint(value, pltpu.VMEM)
+
+
+def distant(value):
+    return pltpu.with_memory_space_constraint(value, pltpu.HBM)
+
+
+def fetched(sources, targets, sem):
+    copies = [pltpu.make_async_copy(a, b, sem.at[k]) for k, (a, b) in enumerate(zip(sources, targets))]
+    for copy in copies:
+        copy.start()
+    return copies
 
 
 def coarse_fine(value):
@@ -61,13 +76,22 @@
     return xhat, inverse, (xhat * gain_ref[...]).astype(BF16)
 
 
-def pack_kernel(pair_ref, cot_ref, gain_ref, bias_weight_ref, out_ref, normed_s, cot_s, bias_s):
+def pack_kernel(
+    pair_at, cot_at, gain_at, bias_weight_at,
+    out_ref, pair_ref, cot_ref, gain_ref, bias_weight_ref, sem, normed_s, cot_s, bias_s,
+):
+    copies = fetched(
+        (pair_at, gain_at, bias_weight_at, cot_at), (pair_ref, gain_ref, bias_weight_ref, cot_ref), sem
+    )
+    for copy in copies[:3]:
+        copy.wait()
     rows, cols, channels = pair_ref.shape
     owners = out_ref.shape[0]
     ncols = cols // owners
     heads = bias_weight_ref.shape[0]
     normed = normalize(pair_ref, gain_ref)[2]
     normed_s[...] = normed.astype(F32)
+    copies[3].wait()
     cot_s[...] = cot_ref[...].astype(F32).reshape(rows * cols, channels)
     for a in range(rows):
         bias = nt(bias_weight_ref[...], normed[a * cols : (a + 1) * cols])
@@ -88,10 +112,11 @@
             out_ref[owner, :, at : at + channels] = cot_s[column, :].astype(BF16)
 
 
-def bias_out_kernel(parts_ref, out_ref):
-    rows = parts_ref.shape[0]
+def bias_out_kernel(both_ref, out_ref):
+    rows, wide = both_ref.shape
     width = out_ref.shape[2] // PARTS
-    bias = parts_ref[:, :width].astype(F32) + parts_ref[:, width : 2 * width].astype(F32)
+    parts = both_ref[:, wide - 256 :].astype(F32)
+    bias = parts[:, :width] + parts[:, width : 2 * width]
     high = rows // PARTS
     packed = jnp.concatenate([bias[k * high : (k + 1) * high] for k in range(PARTS)], axis=1)
     for c in range(out_ref.shape[0]):
@@ -100,21 +125,31 @@
 
 def project_kernel(
     normed_ref, twin_normed_ref, cot_ref, twin_cot_ref, w_ref, wt_ref, w_out_ref,
-    query_ref, key_ref, value_ref, d_context_ref,
-    query_t_ref, key_t_ref, value_t_ref, d_context_t_ref, gate_t_ref, d_gated_t_ref,
+    upright_ref, lying_ref, gates_ref,
 ):
+    channels = w_ref.shape[-1]
     normed = jnp.concatenate([normed_ref[...], twin_normed_ref[...]], axis=1)
     cot = jnp.concatenate([cot_ref[...], twin_cot_ref[...]], axis=1)
-    for m, ref, ref_t in ((0, query_ref, query_t_ref), (1, key_ref, key_t_ref), (2, value_ref, value_t_ref)):
-        ref[0] = nn(normed, w_ref[m]).astype(BF16)
-        ref_t[0] = nt(wt_ref[m], normed).astype(BF16)
+    for m in range(3):
+        at = slice(m * channels, (m + 1) * channels)
+        upright_ref[0, :, at] = nn(normed, w_ref[m]).astype(BF16)
+        lying_ref[0, at, :] = nt(wt_ref[m], normed).astype(BF16)
     gate_t = jax.nn.sigmoid(nt(wt_ref[3], normed))
     d_gated_t = nt(w_out_ref[...], cot)
     d_context_t = (d_gated_t * gate_t).astype(BF16)
-    gate_t_ref[0] = gate_t
-    d_gated_t_ref[0] = d_gated_t
-    d_context_t_ref[0] = d_context_t
-    d_context_ref[0] = turned(d_context_t)
+    gates_ref[0, :channels, :] = gate_t
+    gates_ref[0, channels:, :] = d_gated_t
+    lying_ref[0, 3 * channels :, :] = d_context_t
+    upright_ref[0, :, 3 * channels : 4 * channels] = turned(d_context_t)
+    upright_ref[0, :, 4 * channels : 6 * channels] = normed
+    upright_ref[0, :, 6 * channels :] = cot
+
+
+def inner_specs(columns, rows, channels):
+    sizes = ((rows, 8 * channels, BF16), (4 * channels, rows, BF16), (2 * channels, rows, F32))
+    specs = [pl.BlockSpec((1, high, wide), lambda j: (j, 0, 0)) for high, wide, _ in sizes]
+    shapes = [jax.ShapeDtypeStruct((columns, high, wide), kind) for high, wide, kind in sizes]
+    return specs, shapes
 
 
 def project(both, twin, w, wt, w_out, columns):
@@ -122,11 +157,7 @@
     channels = w.shape[-1]
     normed = pl.BlockSpec((rows, channels), lambda j: (0, j))
     cot = pl.BlockSpec((rows, channels), lambda j: (0, columns + j))
-    flat = pl.BlockSpec((1, rows, channels), lambda j: (j, 0, 0))
-    flat_t = pl.BlockSpec((1, channels, rows), lambda j: (j, 0, 0))
-    upright = jax.ShapeDtypeStruct((columns, rows, channels), BF16)
-    lying = jax.ShapeDtypeStruct((columns, channels, rows), BF16)
-    wide = jax.ShapeDtypeStruct((columns, channels, rows), F32)
+    specs, shapes = inner_specs(columns, rows, channels)
     return pl.pallas_call(
         project_kernel,
         grid=(columns,),
@@ -136,31 +167,39 @@
             pl.BlockSpec(wt.shape, lambda j: (0, 0, 0)),
             pl.BlockSpec(w_out.shape, lambda j: (0, 0)),
         ],
-        out_specs=[flat] * 4 + [flat_t] * 6,
-        out_shape=[upright] * 4 + [lying] * 4 + [wide] * 2,
-        compiler_params=pltpu.CompilerParams(vmem_limit_bytes=56 << 20),
+        out_specs=specs,
+        out_shape=shapes,
+        compiler_params=pltpu.CompilerParams(vmem_limit_bytes=24 << 20),
         name="project",
     )(both, twin, both, twin, w, wt, w_out)
 
 
 def attention_kernel(
-    valid_ref, got_ref, normed_ref, twin_normed_ref, cot_ref, twin_cot_ref,
-    query_ref, key_ref, value_ref, d_context_ref,
-    query_t_ref, key_t_ref, value_t_ref, d_context_t_ref, gate_t_ref, d_gated_t_ref,
-    acts_ref, sent_ref, bias_s, total, grads_s, d_scores_s, weights_s, right_s,
+    valid_ref, got_ref, upright_at, lying_at, gates_at,
+    acts_ref, sent_ref, upright_ref, lying_ref, gates_ref, sem, bias_s, total, grads_s, d_scores_s, weights_s, right_s,
 ):
     step = pl.program_id(0)
     steps = pl.num_programs(0)
     blocks, high, lanes = got_ref.shape
-    rows, channels = normed_ref.shape
+    rows = lying_ref.shape[2]
+    channels = lying_ref.shape[1] // 4
     slots = 4
     width = channels // slots
     half = channels // 2
     cols = rows // blocks
     scale = width ** (-0.5)
 
+    sources = (upright_at, lying_at, gates_at)
+    targets = (upright_ref, lying_ref, gates_ref)
+
+    def block(m, j):
+        return pltpu.make_async_copy(sources[m].at[j], targets[m].at[j], sem.at[m, j])
+
     @pl.when(step == 0)
     def _():
+        for j in range(upright_ref.shape[0]):
+            for m in range(3):
+                block(m, j).start()
         for k in range(PARTS):
             for h in range(2):
                 at = (2 * k + h) * cols
@@ -169,8 +208,12 @@
         total[...] = jnp.zeros_like(total)
         grads_s[...] = jnp.zeros_like(grads_s)
 
-    query = query_ref[0]
-    d_context = d_context_ref[0]
+    for m in range(3):
+        block(m, step).wait()
+    query = upright_ref[step, :, :channels]
+    d_context = upright_ref[step, :, 3 * channels : 4 * channels]
+    key = upright_ref[step, :, channels : 2 * channels]
+    value = upright_ref[step, :, 2 * channels : 3 * channels]
     lane = lax.broadcasted_iota(jnp.int32, (rows, channels), 1)
     sure = rows // 2
     keep = lax.broadcasted_iota(jnp.int32, (rows - sure, rows), 0) + sure < valid_ref[0]
@@ -181,7 +224,7 @@
         part = slice(slot * width, (slot + 1) * width)
         right_s[here, :channels] = jnp.where(mine, query, zero)
         right_s[here, channels:] = jnp.where(mine, d_context, zero)
-        scores = nn(key_ref[0, :, part], query_t_ref[0, part]) * (scale * LOG2E) + bias_s[slot % 2]
+        scores = nn(key[:, part], lying_ref[step, part]) * (scale * LOG2E) + bias_s[slot % 2]
         masked = jnp.where(keep, scores[sure:], MASKED * LOG2E)
         scores = jnp.concatenate([scores[:sure], masked], axis=0)
         top = jnp.max(scores, axis=0, keepdims=True)
@@ -189,34 +232,34 @@
         inverse = 1.0 / jnp.sum(grown, axis=0, keepdims=True)
         probs = grown * inverse
         weights_s[:, here] = probs.astype(BF16)
-        d_probs = nn(value_ref[0, :, part], d_context_t_ref[0, part])
+        d_probs = nn(value[:, part], lying_ref[step, 3 * channels + slot * width : 3 * channels + (slot + 1) * width])
         delta = jnp.sum(grown * d_probs, axis=0, keepdims=True) * inverse
         d_scores = probs * (d_probs - delta)
         total[slot % 2] += d_scores
         d_scores_s[:, here] = d_scores.astype(BF16)
     blocks_t = [
-        (nn(value_t_ref[0, s * width : (s + 1) * width], weights_s[:, s * rows : (s + 1) * rows]),
-         nn(key_t_ref[0, s * width : (s + 1) * width], d_scores_s[:, s * rows : (s + 1) * rows]))
+        (nn(lying_ref[step, 2 * channels + s * width : 2 * channels + (s + 1) * width], weights_s[:, s * rows : (s + 1) * rows]),
+         nn(lying_ref[step, channels + s * width : channels + (s + 1) * width], d_scores_s[:, s * rows : (s + 1) * rows]))
         for s in range(slots)
     ]
     context_t = jnp.concatenate([one for one, _ in blocks_t], axis=0).astype(BF16).astype(F32)
     d_query_t = (jnp.concatenate([two for _, two in blocks_t], axis=0) * scale).astype(BF16)
     d_key = (nn(d_scores_s[...], right_s[:, :channels]) * scale).astype(BF16)
     d_value = nn(weights_s[...], right_s[:, channels:]).astype(BF16)
-    gate_t = gate_t_ref[0]
+    gate_t = gates_ref[step, :channels]
     gated_t = (gate_t * context_t).astype(BF16)
-    d_gate_t = (d_gated_t_ref[0] * context_t * gate_t * (1.0 - gate_t)).astype(BF16)
+    d_gate_t = (gates_ref[step, channels:] * context_t * gate_t * (1.0 - gate_t)).astype(BF16)
     acts = [turned(gated_t), turned(d_query_t), d_key, d_value, turned(d_gate_t)]
     for m in range(5):
         acts_ref[0, :, m * channels : (m + 1) * channels] = acts[m]
     left = jnp.concatenate([d_query_t, turned(d_key), turned(d_value), d_gate_t], axis=0)
-    normed = jnp.concatenate([normed_ref[...], twin_normed_ref[...]], axis=1)
-    products = nn(left, normed)
+    products = nn(left, upright_ref[step, :, 4 * channels : 6 * channels])
     for m in range(4):
         near = products[m * channels : m * channels + half, :channels]
         far = products[m * channels + half : (m + 1) * channels, channels:]
         grads_s[m * half : (m + 1) * half, :] += near + far
-    last = nn(gated_t[:half], cot_ref[...]) + nn(gated_t[half:], twin_cot_ref[...])
+    last = nn(gated_t[:half], upright_ref[step, :, 6 * channels : 7 * channels])
+    last = last + nn(gated_t[half:], upright_ref[step, :, 7 * channels :])
     grads_s[4 * half :, :] += last
 
     @pl.when(step == steps - 1)
@@ -238,24 +281,15 @@
             sent_ref[c, high:, :] = jnp.concatenate(pieces, axis=1).astype(BF16)
 
 
-def attend(valid_len, got, both, twin, inner, columns):
-    rows = both.shape[0]
-    channels = inner[0].shape[-1]
+def attend(valid_len, got, inner, columns):
+    rows = inner[1].shape[2]
+    channels = inner[1].shape[1] // 4
     blocks, high, lanes = got.shape
-    normed = pl.BlockSpec((rows, channels), lambda j: (0, j))
-    cot = pl.BlockSpec((rows, channels), lambda j: (0, columns + j))
-    flat = pl.BlockSpec((1, rows, channels), lambda j: (j, 0, 0))
-    flat_t = pl.BlockSpec((1, channels, rows), lambda j: (j, 0, 0))
     return pl.pallas_call(
         attention_kernel,
         grid=(columns,),
-        in_specs=[
-            pl.BlockSpec(memory_space=pltpu.SMEM),
-            pl.BlockSpec(memory_space=pltpu.VMEM),
-            normed, normed, cot, cot,
-        ]
-        + [flat] * 4
-        + [flat_t] * 6,
+        in_specs=[pl.BlockSpec(memory_space=pltpu.SMEM), pl.BlockSpec(memory_space=pltpu.VMEM)]
+        + [pl.BlockSpec(memory_space=pl.ANY)] * 3,
         out_specs=[
             pl.BlockSpec((1, rows, 5 * channels), lambda j: (j, 0, 0)),
             pl.BlockSpec((blocks, high + 16, lanes), lambda j: (0, 0, 0)),
@@ -265,6 +299,8 @@
             jax.ShapeDtypeStruct((blocks, high + 16, lanes), BF16),
         ],
         scratch_shapes=[
+            *[pltpu.VMEM(one.shape, one.dtype) for one in inner],
+            pltpu.SemaphoreType.DMA((3, columns)),
             pltpu.VMEM((2, rows, rows), F32),
             pltpu.VMEM((2, rows, rows), F32),
             pltpu.VMEM((5 * channels // 2, channels), F32),
@@ -272,9 +308,9 @@
             pltpu.VMEM((rows, 4 * rows), BF16),
             pltpu.VMEM((4 * rows, 2 * channels), BF16),
         ],
-        compiler_params=pltpu.CompilerParams(vmem_limit_bytes=56 << 20),
+        compiler_params=pltpu.CompilerParams(vmem_limit_bytes=24 << 20),
         name="attention",
-    )(valid_len, got, both, twin, both, twin, *inner)
+    )(valid_len, got, *[distant(one) for one in inner])
 
 
 def merge_kernel(acts_ref, came_ref, w_ref, out_ref):
@@ -301,7 +337,7 @@
         in_specs=[block, block, pl.BlockSpec(w.shape, lambda j: (0, 0, 0))],
         out_specs=pl.BlockSpec((rows, 2 * columns * channels), lambda j: (0, 0)),
         out_shape=jax.ShapeDtypeStruct((rows, 2 * columns * channels + 256), BF16),
-        compiler_params=pltpu.CompilerParams(vmem_limit_bytes=56 << 20),
+        compiler_params=pltpu.CompilerParams(vmem_limit_bytes=24 << 20),
         name="merge",
     )(acts, came, w)
 
@@ -338,21 +374,21 @@
         out_specs=spec,
         out_shape=jax.ShapeDtypeStruct(blocked.shape, BF16),
         input_output_aliases={1: 0},
-        compiler_params=pltpu.CompilerParams(vmem_limit_bytes=56 << 20),
+        compiler_params=pltpu.CompilerParams(vmem_limit_bytes=24 << 20),
         name="sum",
     )(got, blocked)
 
 
 def finish_kernel(
-    core_ref, got_ref, pair_ref, gain_ref, bias_weight_ref,
-    d_normed_ref, last_ref, d_bias_s,
+    core_ref, got_ref, pair_at, gain_at, bias_weight_at,
+    d_normed_ref, last_ref, pair_ref, gain_ref, bias_weight_ref, sem, d_bias_s,
 ):
+    copies = fetched((pair_at, gain_at, bias_weight_at), (pair_ref, gain_ref, bias_weight_ref), sem)
     owners, rows, wide = got_ref.shape
     cols, channels = pair_ref.shape[1:]
     heads = bias_weight_ref.shape[0]
     ncols = cols // owners
     main = 2 * ncols * channels
-    xhat, inverse, normed = normalize(pair_ref, gain_ref)
     for owner in range(owners):
         for k in range(ncols):
             column = pl.ds(owner * ncols + k, rows, stride=cols)
@@ -369,6 +405,9 @@
             d_bias_s[at, :] = block[:, h * cols : (h + 1) * cols]
     grads = jnp.where(core_ref[0] == 0, sums[0], sums[1])[:, 4 * cols :]
     grads = jnp.concatenate([grads[:5] + grads[10:15], grads[5:10] + grads[15:20]], axis=1)
+    for copy in copies:
+        copy.wait()
+    xhat, inverse, normed = normalize(pair_ref, gain_ref)
     d_bias_t = jnp.transpose(d_bias_s[...]).astype(BF16)
     row = lax.broadcasted_iota(jnp.int32, (rows * heads, channels), 0)
     repeated = jnp.concatenate([bias_weight_ref[...].astype(F32)] * rows, axis=0).astype(BF16)
@@ -460,38 +499,44 @@
     gap = jnp.zeros((5, channels, channels), BF16)
     w_merge = jnp.concatenate([mine, gap, theirs], axis=1)
 
-    packed = call(
-        pack_kernel, shape((n_row, tile_rows, main + 256), BF16),
-        [pltpu.VMEM((tile, channels), F32), pltpu.VMEM((tile, channels), F32),
-         pltpu.VMEM((heads * tile_rows, tile_cols), F32)],
-        "pack", pair, out_cotangent, gain_row, weight_t,
-    )
+    anywhere = pl.BlockSpec(memory_space=pl.ANY)
+    inputs = [pltpu.VMEM(pair.shape, BF16), pltpu.VMEM(gain_row.shape, F32), pltpu.VMEM(weight_t.shape, BF16)]
+    packed = pl.pallas_call(
+        pack_kernel,
+        in_specs=[anywhere] * 4,
+        out_shape=shape((n_row, tile_rows, main + 256), BF16),
+        scratch_shapes=[
+            inputs[0], *inputs, pltpu.SemaphoreType.DMA((4,)),
+            pltpu.VMEM((tile, channels), F32), pltpu.VMEM((tile, channels), F32),
+            pltpu.VMEM((heads * tile_rows, tile_cols), F32),
+        ],
+        compiler_params=pltpu.CompilerParams(vmem_limit_bytes=24 << 20),
+        name="pack",
+    )(distant(pair), distant(out_cotangent), distant(gain_row), distant(weight_t))
     both = exchange(packed, ROW).reshape(rows, main + 256)
     high = rows // PARTS
     lanes = PARTS * 2 * tile_cols
+    smem = pl.BlockSpec(memory_space=pltpu.SMEM)
+    vmem = pl.BlockSpec(memory_space=pltpu.VMEM)
     spread = pl.pallas_call(
         bias_out_kernel,
-        grid=(1,),
-        in_specs=[pl.BlockSpec((rows, 256), lambda i: (0, main // 256))],
-        out_specs=pl.BlockSpec((n_col, high, lanes), lambda i: (0, 0, 0)),
+        in_specs=[vmem],
         out_shape=shape((n_col, high, lanes), F32),
         name="bias_out",
-    )(both)
+    )(resident(both))
     got = pltpu.with_memory_space_constraint(exchange(spread, COL), pltpu.VMEM)
     twin = lax.ppermute(both, CORE, swap)
     inner = project(both, twin, w, jnp.swapaxes(w, 1, 2), w_out, ncols)
-    acts, sent = attend(valid_len, got, both, twin, inner, ncols)
+    acts, sent = attend(valid_len, got, inner, ncols)
     summed = pltpu.with_memory_space_constraint(exchange(sent, COL), pltpu.VMEM)
     out = merge(acts, lax.ppermute(acts, CORE, swap), w_merge)
     back = pltpu.with_memory_space_constraint(exchange(add_sums(summed, out, n_row), ROW), pltpu.VMEM)
-    smem = pl.BlockSpec(memory_space=pltpu.SMEM)
-    vmem = pl.BlockSpec(memory_space=pltpu.VMEM)
     d_normed, last = pl.pallas_call(
         finish_kernel,
-        in_specs=[smem] + [vmem] * 4,
+        in_specs=[smem, vmem] + [anywhere] * 3,
         out_shape=[shape((tile, channels), F32), shape((n_all, 5, 2, channels), F32)],
-        scratch_shapes=[pltpu.VMEM((heads * tile_rows, tile_cols), F32)],
-        compiler_params=pltpu.CompilerParams(vmem_limit_bytes=56 << 20),
+        scratch_shapes=[*inputs, pltpu.SemaphoreType.DMA((3,)), pltpu.VMEM((heads * tile_rows, tile_cols), F32)],
+        compiler_params=pltpu.CompilerParams(vmem_limit_bytes=24 << 20),
         name="finish",
     )(core[None], back, pair, gain_row, weight_t)
     everyone = pltpu.with_memory_space_constraint(exchange(last, ALL), pltpu.VMEM)
@@ -500,7 +545,7 @@
         in_specs=[vmem] * 4,
         out_shape=[shape(pair.shape, BF16), shape(pair.shape, F32)],
         scratch_shapes=[pltpu.VMEM((tile, channels), F32)],
-        compiler_params=pltpu.CompilerParams(vmem_limit_bytes=56 << 20),
+        compiler_params=pltpu.CompilerParams(vmem_limit_bytes=24 << 20),
         name="output",
     )(back, d_normed, pair, gain_row)
     projection_grad, bias_weight_grad, gain_gradient = pl.pallas_call(

time: 124 us -> 120 us (0.968)
  Pallas kernels: 36.1 us -> 27.8 us
  waiting for transfers between devices: 22.8 us -> 26.9 us
  local copies, waits for them, and re-layouts: 3.12 us -> 5.96 us
  other arithmetic: 2.23 us -> 0.17 us
    all_to_all x3, waiting for transfers between devices: 22.8 us -> 26.9 us  [exchange(): return lax.all_to_all(value, axes, split_axis=0, concat_axis=0, tiled=True)]
    pallas_call x1, Pallas kernels: 4.76 us -> 2.33 us  [project(): pl.pallas_call(project_kernel, grid=(columns,), in_specs=[normed, normed,...]
    pallas_call x3, Pallas kernels: 8.07 us -> 5.71 us  [the longest x1 2.22 us: shards(): pl.pallas_call(pack_kernel, in_specs=[anywhere] * 4, out_shape=shape((n_r...]
    unnamed x7 -> x19, local copies, waits for them, and re-layouts: 2.15 us -> 3.65 us
  transfers between devices with their start and end apart: 5 -> 5, of which waited for: 3 -> 3; matrix products, arithmetic and copies ran while one was open for 3% -> 2% of each run, Pallas kernels for 10% -> 6%
where the time goes in v5:
time: 120 us; the launch traced here: 119 us
  blocking collectives  41.4 us (34%)
  Pallas kernels  27.8 us (23%)
  waiting for transfers between devices  26.9 us (22%)
  starting transfers between devices  15.5 us (13%)
  local copies, waits for them, and re-layouts  5.96 us (5%)
  between operations  1.46 us (1%)
    all_to_all x2, blocking collectives, exchange(): return lax.all_to_all(value, axes, split_axis=0, concat_axis=0, tiled=True)  41.4 us
    all_to_all x3, waiting for transfers between devices, exchange(): return lax.all_to_all(value, axes, split_axis=0, concat_axis=0, tiled=True)  26.9 us
    all_to_all x3, starting transfers between devices, exchange(): return lax.all_to_all(value, axes, split_axis=0, concat_axis=0, tiled=True)  13.3 us
    pallas_call x1, Pallas kernels, attend(): pl.pallas_call(attention_kernel, grid=(columns,), in_specs=[pl.BlockSpec(...  13.2 us
    unnamed x19, local copies, waits for them, and re-layouts  3.65 us
    pallas_call x1, Pallas kernels, merge(): pl.pallas_call(merge_kernel, grid=(columns,), in_specs=[block, block, pl....  2.99 us
  transfers between devices with their start and end apart: 5, of which 3 were waited for; matrix products, arithmetic and copies ran while one was open for 2% of the time, Pallas kernels for 6%

profile of v5, /device:TPU:1, one launch (start us, length us, event | category | flops | bytes accessed | tf_op | source)
XLA Modules:
  0.0 119.2 jit_solution(14788668680010590889)
XLA Ops:
  0.6 2.2 %pack.1 = bf16[16,24,1024]{2,1,0:T(8,128)(2,1)S(1)} custom-call(bf16[24,48,128]{2,1,0:T(8,128)(2,1)} %pair_ref.1, bf16[24,48,128]{2,1,0:T(8,128)(2,1)} %cot_at.1, f32[1,128]{1,0:T(1,128)} %bitcast.26, bf16[4,128]{1,0:T(4,128)(2,1)} %bitcast.29), custom_call_target="tpu_custom_call" | custom-call | tf_op jit(solution)/shard_map/pack/pallas_call | solution.py:504
  2.9 22.5 %all_to_all.25 = bf16[16,24,1024]{2,1,0:T(8,128)(2,1)S(1)} all-to-all(bf16[16,24,1024]{2,1,0:T(8,128)(2,1)S(1)} %pack.1), channel_id=1, replica_groups=mesh['row_0'=2,'row_1'=4,'row_2'=2,'col_0'=2,'col_1'=4] {'row_0','row_1'..., dimensions={0} | all-to-all | bytes 1572864 | tf_op jit(solution)/shard_map/all_to_all | solution.py:36
  25.4 1.3 %bias_out.1 = f32[8,96,384]{2,1,0:T(8,128)} custom-call(bf16[384,1024]{1,0:T(8,128)(2,1)S(1)} %bitcast.21), custom_call_target="tpu_custom_call" | custom-call | tf_op jit(solution)/shard_map/bias_out/pallas_call | solution.py:521
  26.7 5.2 %all-to-all-start.1 = ((f32[8,96,384]{2,1,0:T(8,128)}), f32[8,96,384]{2,1,0:T(8,128)S(1)}, u32[]{:S(2)}, u32[]{:S(2)}) async-start(f32[8,96,384]{2,1,0:T(8,128)} %bias_out.1), calls=%async_computation.1 | async-start | bytes 2359296 | tf_op jit(solution)/shard_map/all_to_all | solution.py:36
  31.9 1.3 %collective-permute-start = (bf16[384,1024]{1,0:T(8,128)(2,1)S(1)}, bf16[384,1024]{1,0:T(8,128)(2,1)S(1)}, u32[]{:S(2)}, u32[]{:S(2)}) collective-permute-start(bf16[384,1024]{1,0:T(8,128)(2,1)S(1)} %bitcast.22), channel_id=1, source_target_pairs={{0,8},{8,0},{1,9},{9,1},{2,10},{10,2},{3,11},{11,3},{4,12},{12,4},... | collective-permute-start | bytes 2359304 | tf_op jit(solution)/shard_map/ppermute | solution.py:528
  33.1 0.6 slice.7
  33.9 0.7 dynamic-slice_bitcast_fusion.1
  35.5 0.7 constant_dynamic-slice_fusion
  36.2 2.3 %project.1 = (bf16[3,384,1024]{2,1,0:T(8,128)(2,1)S(1)}, bf16[3,512,384]{2,1,0:T(8,128)(2,1)S(1)}, f32[3,256,384]{2,1,0:T(8,128)S(1)}) custom-call(bf16[384,1024]{1,0:T(8,128)(2,1)S(1)} %bitcast.23, bf16[384,1024]{1,0:T(8,128)(2,1)S(1)} %collective-permute-done.twin_normed_ref.twin_cot_ref, bf16[384,1024]{1,0:T(8,128)(2,1)S(1)} %bitcast.24, ...), custom_call_target="tpu_custom_call" | custom-call | tf_op jit(solution)/shard_map/project/pallas_call | solution.py:161
  38.6 1.4 %copy-done.1 = bf16[3,384,1024]{2,1,0:T(8,128)(2,1)} copy-done((bf16[3,384,1024]{2,1,0:T(8,128)(2,1)}, bf16[3,384,1024]{2,1,0:T(8,128)(2,1)S(1)}, u32[]{:S(2)}) %copy-start.1) | copy-done | bytes 2359320
  40.0 1.0 copy-done.2
  41.0 1.0 copy-done.3
  42.1 6.1 %all-to-all-done.1.got_ref = f32[8,96,384]{2,1,0:T(8,128)S(1)} async-done(((f32[8,96,384]{2,1,0:T(8,128)}), f32[8,96,384]{2,1,0:T(8,128)S(1)}, u32[]{:S(2)}, u32[]{:S(2)}) %all-to-all-start.1) | async-done | bytes 1179680 | tf_op jit(solution)/shard_map/all_to_all | solution.py:36
  48.2 13.2 %attention.1 = (bf16[3,384,640]{2,1,0:T(8,128)(2,1)S(1)}, bf16[8,112,384]{2,1,0:T(8,128)(2,1)}) custom-call(s32[1]{0:T(128)S(6)} %copy.19.valid_ref, f32[8,96,384]{2,1,0:T(8,128)S(1)} %all-to-all-done.1.got_ref, bf16[3,384,1024]{2,1,0:T(8,128)(2,1)} %copy-done.1, bf16[3,512,384]{2,1,0:T(8,128)(2,1)} %copy-done.2, f32[3,256,384]{2,1,0:T(8,128)} %copy-done.3), custom_call_target="tpu_custom_call" | custom-call | tf_op jit(solution)/shard_map/attention/pallas_call | solution.py:288
  61.4 0.9 collective-permute-start.1
  62.4 3.5 %all-to-all-start.2 = ((bf16[8,112,384]{2,1,0:T(8,128)(2,1)}), bf16[8,112,384]{2,1,0:T(8,128)(2,1)S(1)}, u32[]{:S(2)}, u32[]{:S(2)}) async-start(bf16[8,112,384]{2,1,0:T(8,128)(2,1)} %get-tuple-element.20), calls=%async_computation.2 | async-start | bytes 1376256 | tf_op jit(solution)/shard_map/all_to_all | solution.py:36
  66.1 3.0 %merge.1 = bf16[384,1024]{1,0:T(8,128)(2,1)S(1)} custom-call(bf16[3,384,640]{2,1,0:T(8,128)(2,1)S(1)} %get-tuple-element.21.acts_ref, bf16[3,384,640]{2,1,0:T(8,128)(2,1)} %collective-permute-done.1.came_ref, bf16[5,256,128]{2,1,0:T(8,128)(2,1)S(1)} %maximum_maximum_fusion.w_ref), custom_call_target="tpu_custom_call" | custom-call | tf_op jit(solution)/shard_map/merge/pallas_call | solution.py:334
  69.1 7.8 %all-to-all-done.2.got_ref = bf16[8,112,384]{2,1,0:T(8,128)(2,1)S(1)} async-done(((bf16[8,112,384]{2,1,0:T(8,128)(2,1)}), bf16[8,112,384]{2,1,0:T(8,128)(2,1)S(1)}, u32[]{:S(2)}, u32[]{:S(2)}) %all-to-all-start.2) | async-done | bytes 688160 | tf_op jit(solution)/shard_map/all_to_all | solution.py:36
  77.5 18.9 %all_to_all.26.got_ref = bf16[16,24,1024]{2,1,0:T(8,128)(2,1)S(1)} all-to-all(bf16[16,24,1024]{2,1,0:T(8,128)(2,1)S(1)} %sum.1), channel_id=1, replica_groups=mesh['row_0'=2,'row_1'=4,'row_2'=2,'col_0'=2,'col_1'=4] {'row_0','row_1'..., dimensions={0} | all-to-all | bytes 1572864 | tf_op jit(solution)/shard_map/all_to_all | solution.py:36
  96.4 2.2 %finish.1 = (f32[1152,128]{1,0:T(8,128)S(1)}, f32[128,5,2,128]{3,2,1,0:T(2,128)}) custom-call(s32[1]{0:T(128)} %bitcast.12.core_ref, bf16[16,24,1024]{2,1,0:T(8,128)(2,1)S(1)} %all_to_all.26.got_ref, bf16[24,48,128]{2,1,0:T(8,128)(2,1)S(1)} %copy-done, f32[1,128]{1,0:T(1,128)S(1)} %bitcast.27, bf16[4,128]{1,0:T(4,128)(2,1)S(1)} %bitcast.30), custom_call_target="tpu_custom_call" | custom-call | tf_op jit(solution)/shard_map/finish/pallas_call | solution.py:534
  98.6 4.6 %all-to-all-start.4 = ((f32[128,5,2,128]{3,2,1,0:T(2,128)}), f32[128,5,2,128]{3,2,1,0:T(2,128)S(1)}, u32[]{:S(2)}, u32[]{:S(2)}) async-start(f32[128,5,2,128]{3,2,1,0:T(2,128)} %get-tuple-element.25), calls=%async_computation.4 | async-start | bytes 1310720 | tf_op jit(solution)/shard_map/all_to_all | solution.py:36
  103.1 1.8 %output.1 = (bf16[24,48,128]{2,1,0:T(8,128)(2,1)}, f32[24,48,128]{2,1,0:T(8,128)}) custom-call(bf16[16,24,1024]{2,1,0:T(8,128)(2,1)S(1)} %all_to_all.26.got_ref, f32[1152,128]{1,0:T(8,128)S(1)} %get-tuple-element.22.d_normed_ref, bf16[24,48,128]{2,1,0:T(8,128)(2,1)S(1)} %copy-done, f32[1,128]{1,0:T(1,128)S(1)} %bitcast.28), custom_call_target="tpu_custom_call" | custom-call | tf_op jit(solution)/shard_map/output/pallas_call | solution.py:543
  105.0 13.0 %all-to-all-done.4.got_ref = f32[128,5,2,128]{3,2,1,0:T(2,128)S(1)} async-done(((f32[128,5,2,128]{3,2,1,0:T(2,128)}), f32[128,5,2,128]{3,2,1,0:T(2,128)S(1)}, u32[]{:S(2)}, u32[]{:S(2)}) %all-to-all-start.4) | async-done | bytes 655392 | tf_op jit(solution)/shard_map/all_to_all | solution.py:36
  118.0 1.2 gather.1
  (27 shorter events, 1.1 us)
Async XLA Ops:
  26.7 6.5 %copy-start.6 = (bf16[5,128,128]{2,1,0:T(8,128)(2,1)S(1)}, bf16[5,128,128]{2,1,0:T(8,128)(2,1)}, u32[]{:S(2)}) copy-start(bf16[5,128,128]{2,1,0:T(8,128)(2,1)} %param.8) | copy-start | bytes 491524
  26.7 7.1 %slice-start = ((bf16[5,128,128]{2,1,0:T(8,128)(2,1)}), bf16[4,128,128]{2,1,0:T(8,128)(2,1)S(1)}, s32[]{:S(2)}) async-start(bf16[5,128,128]{2,1,0:T(8,128)(2,1)} %param.8), calls=%async_computation.5 | async-start | bytes 262144 | tf_op jit(solution)/shard_map/slice | solution.py:482
  26.7 21.5 %all-to-all-start.1 = ((f32[8,96,384]{2,1,0:T(8,128)}), f32[8,96,384]{2,1,0:T(8,128)S(1)}, u32[]{:S(2)}, u32[]{:S(2)}) async-start(f32[8,96,384]{2,1,0:T(8,128)} %bias_out.1), calls=%async_computation.1 | async-start | bytes 2359296 | tf_op jit(solution)/shard_map/all_to_all | solution.py:36
  31.9 4.4 %collective-permute-start = (bf16[384,1024]{1,0:T(8,128)(2,1)S(1)}, bf16[384,1024]{1,0:T(8,128)(2,1)S(1)}, u32[]{:S(2)}, u32[]{:S(2)}) collective-permute-start(bf16[384,1024]{1,0:T(8,128)(2,1)S(1)} %bitcast.22), channel_id=1, source_target_pairs={{0,8},{8,0},{1,9},{9,1},{2,10},{10,2},{3,11},{11,3},{4,12},{12,4},... | collective-permute-start | bytes 2359304 | tf_op jit(solution)/shard_map/ppermute | solution.py:528
  38.6 1.4 %copy-start.1 = (bf16[3,384,1024]{2,1,0:T(8,128)(2,1)}, bf16[3,384,1024]{2,1,0:T(8,128)(2,1)S(1)}, u32[]{:S(2)}) copy-start(bf16[3,384,1024]{2,1,0:T(8,128)(2,1)S(1)} %get-tuple-element.17.upright_at) | copy-start | bytes 7077892
  40.0 1.0 copy-start.2
  41.0 1.0 copy-start.3
  61.4 4.6 %copy-start.7 = (bf16[4,64,128]{2,1,0:T(8,128)(2,1)S(1)}, bf16[4,64,128]{2,1,0:T(8,128)(2,1)}, u32[]{:S(2)}) copy-start(bf16[4,64,128]{2,1,0:T(8,128)(2,1)} %get-tuple-element.29) | copy-start | bytes 196612
  61.4 4.6 %copy-start.8 = (bf16[4,64,128]{2,1,0:T(8,128)(2,1)S(1)}, bf16[4,64,128]{2,1,0:T(8,128)(2,1)}, u32[]{:S(2)}) copy-start(bf16[4,64,128]{2,1,0:T(8,128)(2,1)} %get-tuple-element.30) | copy-start | bytes 196612
  61.4 4.7 %collective-permute-start.1 = (bf16[3,384,640]{2,1,0:T(8,128)(2,1)S(1)}, bf16[3,384,640]{2,1,0:T(8,128)(2,1)}, u32[]{:S(2)}, u32[]{:S(2)}) collective-permute-start(bf16[3,384,640]{2,1,0:T(8,128)(2,1)S(1)} %get-tuple-element.21.acts_ref), channel_id=1, source_target_pairs={{0,8},{8,0},{1,9},{9,1},{2,10},{10,2},{3,11},{11,3},{4,12},{12,4},... | collective-permute-start | bytes 4423688 | tf_op jit(solution)/shard_map/ppermute | solution.py:532
  62.4 14.6 %all-to-all-start.2 = ((bf16[8,112,384]{2,1,0:T(8,128)(2,1)}), bf16[8,112,384]{2,1,0:T(8,128)(2,1)S(1)}, u32[]{:S(2)}, u32[]{:S(2)}) async-start(bf16[8,112,384]{2,1,0:T(8,128)(2,1)} %get-tuple-element.20), calls=%async_computation.2 | async-start | bytes 1376256 | tf_op jit(solution)/shard_map/all_to_all | solution.py:36
  77.4 18.9 %copy-start = (bf16[24,48,128]{2,1,0:T(8,128)(2,1)S(1)}, bf16[24,48,128]{2,1,0:T(8,128)(2,1)}, u32[]{:S(2)}) copy-start(bf16[24,48,128]{2,1,0:T(8,128)(2,1)} %pair_ref.1) | copy-start | bytes 884740
  77.4 18.9 %copy-start.4 = (f32[128]{0:T(128)S(1)}, f32[128]{0:T(128)}, u32[]{:S(2)}) copy-start(f32[128]{0:T(128)} %param.7) | copy-start | bytes 1540
  77.5 18.9 %copy-start.5 = (bf16[128,4]{0,1:T(4,128)(2,1)S(1)}, bf16[128,4]{0,1:T(4,128)(2,1)}, u32[]{:S(2)}) copy-start(bf16[128,4]{0,1:T(4,128)(2,1)} %param.9) | copy-start | bytes 3076
  98.6 19.4 %all-to-all-start.4 = ((f32[128,5,2,128]{3,2,1,0:T(2,128)}), f32[128,5,2,128]{3,2,1,0:T(2,128)S(1)}, u32[]{:S(2)}, u32[]{:S(2)}) async-start(f32[128,5,2,128]{3,2,1,0:T(2,128)} %get-tuple-element.25), calls=%async_computation.4 | async-start | bytes 1310720 | tf_op jit(solution)/shard_map/all_to_all | solution.py:36

commit v6 on v5

--- a/solution.py
+++ b/solution.py
@@ -210,57 +210,68 @@
 
     for m in range(3):
         block(m, step).wait()
-    query = upright_ref[step, :, :channels]
-    d_context = upright_ref[step, :, 3 * channels : 4 * channels]
-    key = upright_ref[step, :, channels : 2 * channels]
-    value = upright_ref[step, :, 2 * channels : 3 * channels]
-    lane = lax.broadcasted_iota(jnp.int32, (rows, channels), 1)
-    sure = rows // 2
-    keep = lax.broadcasted_iota(jnp.int32, (rows - sure, rows), 0) + sure < valid_ref[0]
-    zero = jnp.zeros((rows, channels), BF16)
-    for slot in range(slots):
-        mine = (lane >= slot * width) & (lane < (slot + 1) * width)
-        here = slice(slot * rows, (slot + 1) * rows)
-        part = slice(slot * width, (slot + 1) * width)
-        right_s[here, :channels] = jnp.where(mine, query, zero)
-        right_s[here, channels:] = jnp.where(mine, d_context, zero)
-        scores = nn(key[:, part], lying_ref[step, part]) * (scale * LOG2E) + bias_s[slot % 2]
-        masked = jnp.where(keep, scores[sure:], MASKED * LOG2E)
-        scores = jnp.concatenate([scores[:sure], masked], axis=0)
-        top = jnp.max(scores, axis=0, keepdims=True)
-        grown = jnp.exp2(scores - top)
-        inverse = 1.0 / jnp.sum(grown, axis=0, keepdims=True)
-        probs = grown * inverse
-        weights_s[:, here] = probs.astype(BF16)
-        d_probs = nn(value[:, part], lying_ref[step, 3 * channels + slot * width : 3 * channels + (slot + 1) * width])
-        delta = jnp.sum(grown * d_probs, axis=0, keepdims=True) * inverse
-        d_scores = probs * (d_probs - delta)
-        total[slot % 2] += d_scores
-        d_scores_s[:, here] = d_scores.astype(BF16)
-    blocks_t = [
-        (nn(lying_ref[step, 2 * channels + s * width : 2 * channels + (s + 1) * width], weights_s[:, s * rows : (s + 1) * rows]),
-         nn(lying_ref[step, channels + s * width : channels + (s + 1) * width], d_scores_s[:, s * rows : (s + 1) * rows]))
-        for s in range(slots)
-    ]
-    context_t = jnp.concatenate([one for one, _ in blocks_t], axis=0).astype(BF16).astype(F32)
-    d_query_t = (jnp.concatenate([two for _, two in blocks_t], axis=0) * scale).astype(BF16)
-    d_key = (nn(d_scores_s[...], right_s[:, :channels]) * scale).astype(BF16)
-    d_value = nn(weights_s[...], right_s[:, channels:]).astype(BF16)
-    gate_t = gates_ref[step, :channels]
-    gated_t = (gate_t * context_t).astype(BF16)
-    d_gate_t = (gates_ref[step, channels:] * context_t * gate_t * (1.0 - gate_t)).astype(BF16)
-    acts = [turned(gated_t), turned(d_query_t), d_key, d_value, turned(d_gate_t)]
-    for m in range(5):
-        acts_ref[0, :, m * channels : (m + 1) * channels] = acts[m]
-    left = jnp.concatenate([d_query_t, turned(d_key), turned(d_value), d_gate_t], axis=0)
-    products = nn(left, upright_ref[step, :, 4 * channels : 6 * channels])
-    for m in range(4):
-        near = products[m * channels : m * channels + half, :channels]
-        far = products[m * channels + half : (m + 1) * channels, channels:]
-        grads_s[m * half : (m + 1) * half, :] += near + far
-    last = nn(gated_t[:half], upright_ref[step, :, 6 * channels : 7 * channels])
-    last = last + nn(gated_t[half:], upright_ref[step, :, 7 * channels :])
-    grads_s[4 * half :, :] += last
+    def attend_keys(limit):
+        query = upright_ref[step, :, :channels]
+        d_context = upright_ref[step, :, 3 * channels : 4 * channels]
+        key = upright_ref[step, :limit, channels : 2 * channels]
+        value = upright_ref[step, :limit, 2 * channels : 3 * channels]
+        lane = lax.broadcasted_iota(jnp.int32, (rows, channels), 1)
+        sure = rows // 2
+        keep = lax.broadcasted_iota(jnp.int32, (limit - sure, rows), 0) + sure < valid_ref[0]
+        zero = jnp.zeros((rows, channels), BF16)
+        for slot in range(slots):
+            mine = (lane >= slot * width) & (lane < (slot + 1) * width)
+            here = slice(slot * rows, (slot + 1) * rows)
+            part = slice(slot * width, (slot + 1) * width)
+            right_s[here, :channels] = jnp.where(mine, query, zero)
+            right_s[here, channels:] = jnp.where(mine, d_context, zero)
+            scores = nn(key[:, part], lying_ref[step, part]) * (scale * LOG2E) + bias_s[slot % 2, :limit]
+            masked = jnp.where(keep, scores[sure:], MASKED * LOG2E)
+            scores = jnp.concatenate([scores[:sure], masked], axis=0)
+            top = jnp.max(scores, axis=0, keepdims=True)
+            grown = jnp.exp2(scores - top)
+            inverse = 1.0 / jnp.sum(grown, axis=0, keepdims=True)
+            probs = grown * inverse
+            weights_s[:limit, here] = probs.astype(BF16)
+            d_probs = nn(value[:, part], lying_ref[step, 3 * channels + slot * width : 3 * channels + (slot + 1) * width])
+            delta = jnp.sum(grown * d_probs, axis=0, keepdims=True) * inverse
+            d_scores = probs * (d_probs - delta)
+            total[slot % 2, :limit] += d_scores
+            d_scores_s[:limit, here] = d_scores.astype(BF16)
+        blocks_t = [
+            (nn(lying_ref[step, 2 * channels + s * width : 2 * channels + (s + 1) * width, :limit], weights_s[:limit, s * rows : (s + 1) * rows]),
+             nn(lying_ref[step, channels + s * width : channels + (s + 1) * width, :limit], d_scores_s[:limit, s * rows : (s + 1) * rows]))
+            for s in range(slots)
+        ]
+        context_t = jnp.concatenate([one for one, _ in blocks_t], axis=0).astype(BF16).astype(F32)
+        d_query_t = (jnp.concatenate([two for _, two in blocks_t], axis=0) * scale).astype(BF16)
+        d_key = (nn(d_scores_s[:limit], right_s[:, :channels]) * scale).astype(BF16)
+        d_value = nn(weights_s[:limit], right_s[:, channels:]).astype(BF16)
+        if limit < rows:
+            rest = jnp.zeros((rows - limit, channels), BF16)
+            d_key = jnp.concatenate([d_key, rest], axis=0)
+            d_value = jnp.concatenate([d_value, rest], axis=0)
+        gate_t = gates_ref[step, :channels]
+        gated_t = (gate_t * context_t).astype(BF16)
+        d_gate_t = (gates_ref[step, channels:] * context_t * gate_t * (1.0 - gate_t)).astype(BF16)
+        acts = [turned(gated_t), turned(d_query_t), d_key, d_value, turned(d_gate_t)]
+        for m in range(5):
+            acts_ref[0, :, m * channels : (m + 1) * channels] = acts[m]
+        left = jnp.concatenate([d_query_t, turned(d_key), turned(d_value), d_gate_t], axis=0)
+        products = nn(left, upright_ref[step, :, 4 * channels : 6 * channels])
+        for m in range(4):
+            near = products[m * channels : m * channels + half, :channels]
+            far = products[m * channels + half : (m + 1) * channels, channels:]
+            grads_s[m * half : (m + 1) * half, :] += near + far
+        last = nn(gated_t[:half], upright_ref[step, :, 6 * channels : 7 * channels])
+        last = last + nn(gated_t[half:], upright_ref[step, :, 7 * channels :])
+        grads_s[4 * half :, :] += last
+
+    below = 0
+    for limit in (2 * rows // 3, 5 * rows // 6, rows):
+        fits = (valid_ref[0] > below) & (valid_ref[0] <= limit)
+        pl.when(fits)(functools.partial(attend_keys, limit))
+        below = limit
 
     @pl.when(step == steps - 1)
     def _():

time: 120 us -> 118 us (0.983)
  Pallas kernels: 27.8 us -> 26.4 us
    pallas_call x1, Pallas kernels: 13.2 us -> 11.8 us  [attend(): pl.pallas_call(attention_kernel, grid=(columns,), in_specs=[pl.BlockSpec(...]
where the time goes in v6:
time: 118 us
  blocking collectives  41.4 us (35%)
  waiting for transfers between devices  26.9 us (23%)
  Pallas kernels  26.4 us (22%)
  starting transfers between devices  15.6 us (13%)
  local copies, waits for them, and re-layouts  5.96 us (5%)
  between operations  1.46 us (1%)
    all_to_all x2, blocking collectives, exchange(): return lax.all_to_all(value, axes, split_axis=0, concat_axis=0, tiled=True)  41.4 us
    all_to_all x3, waiting for transfers between devices, exchange(): return lax.all_to_all(value, axes, split_axis=0, concat_axis=0, tiled=True)  26.9 us
    all_to_all x3, starting transfers between devices, exchange(): return lax.all_to_all(value, axes, split_axis=0, concat_axis=0, tiled=True)  13.3 us
    pallas_call x1, Pallas kernels, attend(): pl.pallas_call(attention_kernel, grid=(columns,), in_specs=[pl.BlockSpec(...  11.8 us
    unnamed x19, local copies, waits for them, and re-layouts  3.65 us
    pallas_call x1, Pallas kernels, merge(): pl.pallas_call(merge_kernel, grid=(columns,), in_specs=[block, block, pl....  2.99 us
  transfers between devices with their start and end apart: 5, of which 3 were waited for; matrix products, arithmetic and copies ran while one was open for 2% of the time, Pallas kernels for 6%

profile of v6, /device:TPU:1, one launch (start us, length us, event | category | flops | bytes accessed | tf_op | source)
XLA Modules:
  0.0 117.9 jit_solution(16804314334977685242)
XLA Ops:
  0.6 2.2 %pack.1 = bf16[16,24,1024]{2,1,0:T(8,128)(2,1)S(1)} custom-call(bf16[24,48,128]{2,1,0:T(8,128)(2,1)} %pair_ref.1, bf16[24,48,128]{2,1,0:T(8,128)(2,1)} %cot_at.1, f32[1,128]{1,0:T(1,128)} %bitcast.26, bf16[4,128]{1,0:T(4,128)(2,1)} %bitcast.29), custom_call_target="tpu_custom_call" | custom-call | tf_op jit(solution)/shard_map/pack/pallas_call | solution.py:515
  2.9 22.5 %all_to_all.25 = bf16[16,24,1024]{2,1,0:T(8,128)(2,1)S(1)} all-to-all(bf16[16,24,1024]{2,1,0:T(8,128)(2,1)S(1)} %pack.1), channel_id=1, replica_groups=mesh['row_0'=2,'row_1'=4,'row_2'=2,'col_0'=2,'col_1'=4] {'row_0','row_1'..., dimensions={0} | all-to-all | bytes 1572864 | tf_op jit(solution)/shard_map/all_to_all | solution.py:36
  25.4 1.3 %bias_out.1 = f32[8,96,384]{2,1,0:T(8,128)} custom-call(bf16[384,1024]{1,0:T(8,128)(2,1)S(1)} %bitcast.21), custom_call_target="tpu_custom_call" | custom-call | tf_op jit(solution)/shard_map/bias_out/pallas_call | solution.py:532
  26.7 5.2 %all-to-all-start.1 = ((f32[8,96,384]{2,1,0:T(8,128)}), f32[8,96,384]{2,1,0:T(8,128)S(1)}, u32[]{:S(2)}, u32[]{:S(2)}) async-start(f32[8,96,384]{2,1,0:T(8,128)} %bias_out.1), calls=%async_computation.1 | async-start | bytes 2359296 | tf_op jit(solution)/shard_map/all_to_all | solution.py:36
  31.9 1.3 %collective-permute-start = (bf16[384,1024]{1,0:T(8,128)(2,1)S(1)}, bf16[384,1024]{1,0:T(8,128)(2,1)S(1)}, u32[]{:S(2)}, u32[]{:S(2)}) collective-permute-start(bf16[384,1024]{1,0:T(8,128)(2,1)S(1)} %bitcast.22), channel_id=1, source_target_pairs={{0,8},{8,0},{1,9},{9,1},{2,10},{10,2},{3,11},{11,3},{4,12},{12,4},... | collective-permute-start | bytes 2359304 | tf_op jit(solution)/shard_map/ppermute | solution.py:539
  33.1 0.6 slice.7
  33.9 0.7 dynamic-slice_bitcast_fusion.1
  35.5 0.7 constant_dynamic-slice_fusion
  36.2 2.3 %project.1 = (bf16[3,384,1024]{2,1,0:T(8,128)(2,1)S(1)}, bf16[3,512,384]{2,1,0:T(8,128)(2,1)S(1)}, f32[3,256,384]{2,1,0:T(8,128)S(1)}) custom-call(bf16[384,1024]{1,0:T(8,128)(2,1)S(1)} %bitcast.23, bf16[384,1024]{1,0:T(8,128)(2,1)S(1)} %collective-permute-done.twin_normed_ref.twin_cot_ref, bf16[384,1024]{1,0:T(8,128)(2,1)S(1)} %bitcast.24, ...), custom_call_target="tpu_custom_call" | custom-call | tf_op jit(solution)/shard_map/project/pallas_call | solution.py:161
  38.6 1.4 %copy-done.1 = bf16[3,384,1024]{2,1,0:T(8,128)(2,1)} copy-done((bf16[3,384,1024]{2,1,0:T(8,128)(2,1)}, bf16[3,384,1024]{2,1,0:T(8,128)(2,1)S(1)}, u32[]{:S(2)}) %copy-start.1) | copy-done | bytes 2359320
  40.0 1.0 copy-done.2
  41.0 1.0 copy-done.3
  42.1 6.1 %all-to-all-done.1.got_ref = f32[8,96,384]{2,1,0:T(8,128)S(1)} async-done(((f32[8,96,384]{2,1,0:T(8,128)}), f32[8,96,384]{2,1,0:T(8,128)S(1)}, u32[]{:S(2)}, u32[]{:S(2)}) %all-to-all-start.1) | async-done | bytes 1179680 | tf_op jit(solution)/shard_map/all_to_all | solution.py:36
  48.2 11.8 %attention.1 = (bf16[3,384,640]{2,1,0:T(8,128)(2,1)S(1)}, bf16[8,112,384]{2,1,0:T(8,128)(2,1)}) custom-call(s32[1]{0:T(128)S(6)} %copy.19.valid_ref, f32[8,96,384]{2,1,0:T(8,128)S(1)} %all-to-all-done.1.got_ref, bf16[3,384,1024]{2,1,0:T(8,128)(2,1)} %copy-done.1, bf16[3,512,384]{2,1,0:T(8,128)(2,1)} %copy-done.2, f32[3,256,384]{2,1,0:T(8,128)} %copy-done.3), custom_call_target="tpu_custom_call" | custom-call | tf_op jit(solution)/shard_map/attention/pallas_call | solution.py:299
  60.0 1.1 collective-permute-start.1
  61.1 3.5 %all-to-all-start.2 = ((bf16[8,112,384]{2,1,0:T(8,128)(2,1)}), bf16[8,112,384]{2,1,0:T(8,128)(2,1)S(1)}, u32[]{:S(2)}, u32[]{:S(2)}) async-start(bf16[8,112,384]{2,1,0:T(8,128)(2,1)} %get-tuple-element.20), calls=%async_computation.2 | async-start | bytes 1376256 | tf_op jit(solution)/shard_map/all_to_all | solution.py:36
  64.9 3.0 %merge.1 = bf16[384,1024]{1,0:T(8,128)(2,1)S(1)} custom-call(bf16[3,384,640]{2,1,0:T(8,128)(2,1)S(1)} %get-tuple-element.21.acts_ref, bf16[3,384,640]{2,1,0:T(8,128)(2,1)} %collective-permute-done.1.came_ref, bf16[5,256,128]{2,1,0:T(8,128)(2,1)S(1)} %maximum_maximum_fusion.w_ref), custom_call_target="tpu_custom_call" | custom-call | tf_op jit(solution)/shard_map/merge/pallas_call | solution.py:345
  67.9 7.8 %all-to-all-done.2.got_ref = bf16[8,112,384]{2,1,0:T(8,128)(2,1)S(1)} async-done(((bf16[8,112,384]{2,1,0:T(8,128)(2,1)}), bf16[8,112,384]{2,1,0:T(8,128)(2,1)S(1)}, u32[]{:S(2)}, u32[]{:S(2)}) %all-to-all-start.2) | async-done | bytes 688160 | tf_op jit(solution)/shard_map/all_to_all | solution.py:36
  76.2 18.9 %all_to_all.26.got_ref = bf16[16,24,1024]{2,1,0:T(8,128)(2,1)S(1)} all-to-all(bf16[16,24,1024]{2,1,0:T(8,128)(2,1)S(1)} %sum.1), channel_id=1, replica_groups=mesh['row_0'=2,'row_1'=4,'row_2'=2,'col_0'=2,'col_1'=4] {'row_0','row_1'..., dimensions={0} | all-to-all | bytes 1572864 | tf_op jit(solution)/shard_map/all_to_all | solution.py:36
  95.1 2.2 %finish.1 = (f32[1152,128]{1,0:T(8,128)S(1)}, f32[128,5,2,128]{3,2,1,0:T(2,128)}) custom-call(s32[1]{0:T(128)} %bitcast.12.core_ref, bf16[16,24,1024]{2,1,0:T(8,128)(2,1)S(1)} %all_to_all.26.got_ref, bf16[24,48,128]{2,1,0:T(8,128)(2,1)S(1)} %copy-done, f32[1,128]{1,0:T(1,128)S(1)} %bitcast.27, bf16[4,128]{1,0:T(4,128)(2,1)S(1)} %bitcast.30), custom_call_target="tpu_custom_call" | custom-call | tf_op jit(solution)/shard_map/finish/pallas_call | solution.py:545
  97.4 4.6 %all-to-all-start.4 = ((f32[128,5,2,128]{3,2,1,0:T(2,128)}), f32[128,5,2,128]{3,2,1,0:T(2,128)S(1)}, u32[]{:S(2)}, u32[]{:S(2)}) async-start(f32[128,5,2,128]{3,2,1,0:T(2,128)} %get-tuple-element.25), calls=%async_computation.4 | async-start | bytes 1310720 | tf_op jit(solution)/shard_map/all_to_all | solution.py:36
  101.9 1.8 %output.1 = (bf16[24,48,128]{2,1,0:T(8,128)(2,1)}, f32[24,48,128]{2,1,0:T(8,128)}) custom-call(bf16[16,24,1024]{2,1,0:T(8,128)(2,1)S(1)} %all_to_all.26.got_ref, f32[1152,128]{1,0:T(8,128)S(1)} %get-tuple-element.22.d_normed_ref, bf16[24,48,128]{2,1,0:T(8,128)(2,1)S(1)} %copy-done, f32[1,128]{1,0:T(1,128)S(1)} %bitcast.28), custom_call_target="tpu_custom_call" | custom-call | tf_op jit(solution)/shard_map/output/pallas_call | solution.py:554
  103.8 13.0 %all-to-all-done.4.got_ref = f32[128,5,2,128]{3,2,1,0:T(2,128)S(1)} async-done(((f32[128,5,2,128]{3,2,1,0:T(2,128)}), f32[128,5,2,128]{3,2,1,0:T(2,128)S(1)}, u32[]{:S(2)}, u32[]{:S(2)}) %all-to-all-start.4) | async-done | bytes 655392 | tf_op jit(solution)/shard_map/all_to_all | solution.py:36
  116.8 1.2 gather.1
  (27 shorter events, 1.1 us)
Async XLA Ops:
  26.7 6.5 %copy-start.6 = (bf16[5,128,128]{2,1,0:T(8,128)(2,1)S(1)}, bf16[5,128,128]{2,1,0:T(8,128)(2,1)}, u32[]{:S(2)}) copy-start(bf16[5,128,128]{2,1,0:T(8,128)(2,1)} %param.8) | copy-start | bytes 491524
  26.7 7.1 %slice-start = ((bf16[5,128,128]{2,1,0:T(8,128)(2,1)}), bf16[4,128,128]{2,1,0:T(8,128)(2,1)S(1)}, s32[]{:S(2)}) async-start(bf16[5,128,128]{2,1,0:T(8,128)(2,1)} %param.8), calls=%async_computation.5 | async-start | bytes 262144 | tf_op jit(solution)/shard_map/slice | solution.py:493
  26.7 21.5 %all-to-all-start.1 = ((f32[8,96,384]{2,1,0:T(8,128)}), f32[8,96,384]{2,1,0:T(8,128)S(1)}, u32[]{:S(2)}, u32[]{:S(2)}) async-start(f32[8,96,384]{2,1,0:T(8,128)} %bias_out.1), calls=%async_computation.1 | async-start | bytes 2359296 | tf_op jit(solution)/shard_map/all_to_all | solution.py:36
  31.9 4.4 %collective-permute-start = (bf16[384,1024]{1,0:T(8,128)(2,1)S(1)}, bf16[384,1024]{1,0:T(8,128)(2,1)S(1)}, u32[]{:S(2)}, u32[]{:S(2)}) collective-permute-start(bf16[384,1024]{1,0:T(8,128)(2,1)S(1)} %bitcast.22), channel_id=1, source_target_pairs={{0,8},{8,0},{1,9},{9,1},{2,10},{10,2},{3,11},{11,3},{4,12},{12,4},... | collective-permute-start | bytes 2359304 | tf_op jit(solution)/shard_map/ppermute | solution.py:539
  38.6 1.4 %copy-start.1 = (bf16[3,384,1024]{2,1,0:T(8,128)(2,1)}, bf16[3,384,1024]{2,1,0:T(8,128)(2,1)S(1)}, u32[]{:S(2)}) copy-start(bf16[3,384,1024]{2,1,0:T(8,128)(2,1)S(1)} %get-tuple-element.17.upright_at) | copy-start | bytes 7077892
  40.0 1.0 copy-start.2
  41.0 1.0 copy-start.3
  60.0 4.8 %copy-start.7 = (bf16[4,64,128]{2,1,0:T(8,128)(2,1)S(1)}, bf16[4,64,128]{2,1,0:T(8,128)(2,1)}, u32[]{:S(2)}) copy-start(bf16[4,64,128]{2,1,0:T(8,128)(2,1)} %get-tuple-element.29) | copy-start | bytes 196612
  60.0 4.7 %copy-start.8 = (bf16[4,64,128]{2,1,0:T(8,128)(2,1)S(1)}, bf16[4,64,128]{2,1,0:T(8,128)(2,1)}, u32[]{:S(2)}) copy-start(bf16[4,64,128]{2,1,0:T(8,128)(2,1)} %get-tuple-element.30) | copy-start | bytes 196612
  60.0 4.9 %collective-permute-start.1 = (bf16[3,384,640]{2,1,0:T(8,128)(2,1)S(1)}, bf16[3,384,640]{2,1,0:T(8,128)(2,1)}, u32[]{:S(2)}, u32[]{:S(2)}) collective-permute-start(bf16[3,384,640]{2,1,0:T(8,128)(2,1)S(1)} %get-tuple-element.21.acts_ref), channel_id=1, source_target_pairs={{0,8},{8,0},{1,9},{9,1},{2,10},{10,2},{3,11},{11,3},{4,12},{12,4},... | collective-permute-start | bytes 4423688 | tf_op jit(solution)/shard_map/ppermute | solution.py:543
  61.1 14.5 %all-to-all-start.2 = ((bf16[8,112,384]{2,1,0:T(8,128)(2,1)}), bf16[8,112,384]{2,1,0:T(8,128)(2,1)S(1)}, u32[]{:S(2)}, u32[]{:S(2)}) async-start(bf16[8,112,384]{2,1,0:T(8,128)(2,1)} %get-tuple-element.20), calls=%async_computation.2 | async-start | bytes 1376256 | tf_op jit(solution)/shard_map/all_to_all | solution.py:36
  76.2 18.9 %copy-start = (bf16[24,48,128]{2,1,0:T(8,128)(2,1)S(1)}, bf16[24,48,128]{2,1,0:T(8,128)(2,1)}, u32[]{:S(2)}) copy-start(bf16[24,48,128]{2,1,0:T(8,128)(2,1)} %pair_ref.1) | copy-start | bytes 884740
  76.2 18.9 %copy-start.4 = (f32[128]{0:T(128)S(1)}, f32[128]{0:T(128)}, u32[]{:S(2)}) copy-start(f32[128]{0:T(128)} %param.7) | copy-start | bytes 1540
  76.2 18.9 %copy-start.5 = (bf16[128,4]{0,1:T(4,128)(2,1)S(1)}, bf16[128,4]{0,1:T(4,128)(2,1)}, u32[]{:S(2)}) copy-start(bf16[128,4]{0,1:T(4,128)(2,1)} %param.9) | copy-start | bytes 3076
  97.4 19.4 %all-to-all-start.4 = ((f32[128,5,2,128]{3,2,1,0:T(2,128)}), f32[128,5,2,128]{3,2,1,0:T(2,128)S(1)}, u32[]{:S(2)}, u32[]{:S(2)}) async-start(f32[128,5,2,128]{3,2,1,0:T(2,128)} %get-tuple-element.25), calls=%async_computation.4 | async-start | bytes 1310720 | tf_op jit(solution)/shard_map/all_to_all | solution.py:36

commit v7 on v6

--- a/solution.py
+++ b/solution.py
@@ -96,11 +96,13 @@
     for a in range(rows):
         bias = nt(bias_weight_ref[...], normed[a * cols : (a + 1) * cols])
         bias_s[pl.ds(a, heads, stride=rows), :] = bias
-    pad = jnp.zeros((rows, 256 - 4 * cols), BF16)
+    pad = jnp.zeros((rows, 384 - 6 * cols), BF16)
     for core in range(2):
         first = 2 * core * rows
         bias = jnp.concatenate([bias_s[first : first + rows], bias_s[first + rows : first + 2 * rows]], axis=1)
-        bias = jnp.concatenate([*coarse_fine(bias), pad], axis=1)
+        coarse, fine = coarse_fine(bias)
+        finest = (bias - coarse.astype(F32) - fine.astype(F32)).astype(BF16)
+        bias = jnp.concatenate([coarse, fine, finest, pad], axis=1)
         for owner in range(core, owners, 2):
             out_ref[owner, :, 2 * ncols * channels :] = bias
     for owner in range(owners):
@@ -115,8 +117,8 @@
 def bias_out_kernel(both_ref, out_ref):
     rows, wide = both_ref.shape
     width = out_ref.shape[2] // PARTS
-    parts = both_ref[:, wide - 256 :].astype(F32)
-    bias = parts[:, :width] + parts[:, width : 2 * width]
+    parts = both_ref[:, wide - 384 :].astype(F32)
+    bias = parts[:, :width] + (parts[:, width : 2 * width] + parts[:, 2 * width : 3 * width])
     high = rows // PARTS
     packed = jnp.concatenate([bias[k * high : (k + 1) * high] for k in range(PARTS)], axis=1)
     for c in range(out_ref.shape[0]):
@@ -515,7 +517,7 @@
     packed = pl.pallas_call(
         pack_kernel,
         in_specs=[anywhere] * 4,
-        out_shape=shape((n_row, tile_rows, main + 256), BF16),
+        out_shape=shape((n_row, tile_rows, main + 384), BF16),
         scratch_shapes=[
             inputs[0], *inputs, pltpu.SemaphoreType.DMA((4,)),
             pltpu.VMEM((tile, channels), F32), pltpu.VMEM((tile, channels), F32),
@@ -524,7 +526,7 @@
         compiler_params=pltpu.CompilerParams(vmem_limit_bytes=24 << 20),
         name="pack",
     )(distant(pair), distant(out_cotangent), distant(gain_row), distant(weight_t))
-    both = exchange(packed, ROW).reshape(rows, main + 256)
+    both = exchange(packed, ROW).reshape(rows, main + 384)
     high = rows // PARTS
     lanes = PARTS * 2 * tile_cols
     smem = pl.BlockSpec(memory_space=pltpu.SMEM)

time: 118 us -> 119 us (level)
    unnamed x19 -> x17, local copies, waits for them, and re-layouts: 3.65 us -> 3.64 us
where the time goes in v7:
time: 119 us
  blocking collectives  42.4 us (36%)
  waiting for transfers between devices  26.4 us (22%)
  Pallas kernels  26.3 us (22%)
  starting transfers between devices  15.8 us (13%)
  local copies, waits for them, and re-layouts  5.55 us (5%)
  between operations  1.48 us (1%)
    all_to_all x2, blocking collectives, exchange(): return lax.all_to_all(value, axes, split_axis=0, concat_axis=0, tiled=True)  42.4 us
    all_to_all x3, waiting for transfers between devices, exchange(): return lax.all_to_all(value, axes, split_axis=0, concat_axis=0, tiled=True)  26.4 us
    all_to_all x3, starting transfers between devices, exchange(): return lax.all_to_all(value, axes, split_axis=0, concat_axis=0, tiled=True)  13.3 us
    pallas_call x1, Pallas kernels, attend(): pl.pallas_call(attention_kernel, grid=(columns,), in_specs=[pl.BlockSpec(...  11.8 us
    unnamed x17, local copies, waits for them, and re-layouts  3.64 us
    pallas_call x1, Pallas kernels, merge(): pl.pallas_call(merge_kernel, grid=(columns,), in_specs=[block, block, pl....  2.99 us
  transfers between devices with their start and end apart: 5, of which 3 were waited for; matrix products, arithmetic and copies ran while one was open for 2% of the time, Pallas kernels for 6%

profile of v7, /device:TPU:1, one launch (start us, length us, event | category | flops | bytes accessed | tf_op | source)
XLA Modules:
  0.0 118.9 jit_solution(9610367563843472096)
XLA Ops:
  0.6 2.2 %pack.1 = bf16[16,24,1152]{2,1,0:T(8,128)(2,1)S(1)} custom-call(bf16[24,48,128]{2,1,0:T(8,128)(2,1)} %pair_ref.1, bf16[24,48,128]{2,1,0:T(8,128)(2,1)} %cot_at.1, f32[1,128]{1,0:T(1,128)} %bitcast.26, bf16[4,128]{1,0:T(4,128)(2,1)} %bitcast.29), custom_call_target="tpu_custom_call" | custom-call | tf_op jit(solution)/shard_map/pack/pallas_call | solution.py:517
  2.9 23.4 %all_to_all.25 = bf16[16,24,1152]{2,1,0:T(8,128)(2,1)S(1)} all-to-all(bf16[16,24,1152]{2,1,0:T(8,128)(2,1)S(1)} %pack.1), channel_id=1, replica_groups=mesh['row_0'=2,'row_1'=4,'row_2'=2,'col_0'=2,'col_1'=4] {'row_0','row_1'..., dimensions={0} | all-to-all | bytes 1769472 | tf_op jit(solution)/shard_map/all_to_all | solution.py:36
  26.3 1.4 %bias_out.1 = f32[8,96,384]{2,1,0:T(8,128)} custom-call(bf16[384,1152]{1,0:T(8,128)(2,1)S(1)} %bitcast.21), custom_call_target="tpu_custom_call" | custom-call | tf_op jit(solution)/shard_map/bias_out/pallas_call | solution.py:534
  27.6 5.2 %all-to-all-start.1 = ((f32[8,96,384]{2,1,0:T(8,128)}), f32[8,96,384]{2,1,0:T(8,128)S(1)}, u32[]{:S(2)}, u32[]{:S(2)}) async-start(f32[8,96,384]{2,1,0:T(8,128)} %bias_out.1), calls=%async_computation.1 | async-start | bytes 2359296 | tf_op jit(solution)/shard_map/all_to_all | solution.py:36
  32.8 1.5 %collective-permute-start = (bf16[384,1152]{1,0:T(8,128)(2,1)S(1)}, bf16[384,1152]{1,0:T(8,128)(2,1)S(1)}, u32[]{:S(2)}, u32[]{:S(2)}) collective-permute-start(bf16[384,1152]{1,0:T(8,128)(2,1)S(1)} %bitcast.22), channel_id=1, source_target_pairs={{0,8},{8,0},{1,9},{9,1},{2,10},{10,2},{3,11},{11,3},{4,12},{12,4},... | collective-permute-start | bytes 2654216 | tf_op jit(solution)/shard_map/ppermute | solution.py:541
  34.5 0.7 dynamic-slice_bitcast_fusion.1
  35.2 0.7 fusion.6
  35.9 1.1 copy.16.w_ref
  37.8 2.2 %project.1 = (bf16[3,384,1024]{2,1,0:T(8,128)(2,1)S(1)}, bf16[3,512,384]{2,1,0:T(8,128)(2,1)S(1)}, f32[3,256,384]{2,1,0:T(8,128)S(1)}) custom-call(bf16[384,1152]{1,0:T(8,128)(2,1)S(1)} %bitcast.23, bf16[384,1152]{1,0:T(8,128)(2,1)S(1)} %collective-permute-done.twin_normed_ref.twin_cot_ref, bf16[384,1152]{1,0:T(8,128)(2,1)S(1)} %bitcast.24, ...), custom_call_target="tpu_custom_call" | custom-call | tf_op jit(solution)/shard_map/project/pallas_call | solution.py:163
  40.0 1.4 %copy-done.1 = bf16[3,384,1024]{2,1,0:T(8,128)(2,1)} copy-done((bf16[3,384,1024]{2,1,0:T(8,128)(2,1)}, bf16[3,384,1024]{2,1,0:T(8,128)(2,1)S(1)}, u32[]{:S(2)}) %copy-start.1) | copy-done | bytes 2359320
  41.5 1.0 copy-done.2
  42.5 1.0 copy-done.3
  43.5 5.6 %all-to-all-done.1.got_ref = f32[8,96,384]{2,1,0:T(8,128)S(1)} async-done(((f32[8,96,384]{2,1,0:T(8,128)}), f32[8,96,384]{2,1,0:T(8,128)S(1)}, u32[]{:S(2)}, u32[]{:S(2)}) %all-to-all-start.1) | async-done | bytes 1179680 | tf_op jit(solution)/shard_map/all_to_all | solution.py:36
  49.1 11.8 %attention.1 = (bf16[3,384,640]{2,1,0:T(8,128)(2,1)S(1)}, bf16[8,112,384]{2,1,0:T(8,128)(2,1)}) custom-call(s32[1]{0:T(128)S(6)} %copy.19.valid_ref, f32[8,96,384]{2,1,0:T(8,128)S(1)} %all-to-all-done.1.got_ref, bf16[3,384,1024]{2,1,0:T(8,128)(2,1)} %copy-done.1, bf16[3,512,384]{2,1,0:T(8,128)(2,1)} %copy-done.2, f32[3,256,384]{2,1,0:T(8,128)} %copy-done.3), custom_call_target="tpu_custom_call" | custom-call | tf_op jit(solution)/shard_map/attention/pallas_call | solution.py:301
  61.0 1.0 collective-permute-start.1
  61.9 3.5 %all-to-all-start.2 = ((bf16[8,112,384]{2,1,0:T(8,128)(2,1)}), bf16[8,112,384]{2,1,0:T(8,128)(2,1)S(1)}, u32[]{:S(2)}, u32[]{:S(2)}) async-start(bf16[8,112,384]{2,1,0:T(8,128)(2,1)} %get-tuple-element.20), calls=%async_computation.2 | async-start | bytes 1376256 | tf_op jit(solution)/shard_map/all_to_all | solution.py:36
  65.7 3.0 %merge.1 = bf16[384,1024]{1,0:T(8,128)(2,1)S(1)} custom-call(bf16[3,384,640]{2,1,0:T(8,128)(2,1)S(1)} %get-tuple-element.21.acts_ref, bf16[3,384,640]{2,1,0:T(8,128)(2,1)} %collective-permute-done.1.came_ref, bf16[5,256,128]{2,1,0:T(8,128)(2,1)S(1)} %maximum_maximum_fusion.w_ref), custom_call_target="tpu_custom_call" | custom-call | tf_op jit(solution)/shard_map/merge/pallas_call | solution.py:347
  68.7 7.8 %all-to-all-done.2.got_ref = bf16[8,112,384]{2,1,0:T(8,128)(2,1)S(1)} async-done(((bf16[8,112,384]{2,1,0:T(8,128)(2,1)}), bf16[8,112,384]{2,1,0:T(8,128)(2,1)S(1)}, u32[]{:S(2)}, u32[]{:S(2)}) %all-to-all-start.2) | async-done | bytes 688160 | tf_op jit(solution)/shard_map/all_to_all | solution.py:36
  77.0 19.0 %all_to_all.26.got_ref = bf16[16,24,1024]{2,1,0:T(8,128)(2,1)S(1)} all-to-all(bf16[16,24,1024]{2,1,0:T(8,128)(2,1)S(1)} %sum.1), channel_id=1, replica_groups=mesh['row_0'=2,'row_1'=4,'row_2'=2,'col_0'=2,'col_1'=4] {'row_0','row_1'..., dimensions={0} | all-to-all | bytes 1572864 | tf_op jit(solution)/shard_map/all_to_all | solution.py:36
  96.1 2.2 %finish.1 = (f32[1152,128]{1,0:T(8,128)S(1)}, f32[128,5,2,128]{3,2,1,0:T(2,128)}) custom-call(s32[1]{0:T(128)} %bitcast.12.core_ref, bf16[16,24,1024]{2,1,0:T(8,128)(2,1)S(1)} %all_to_all.26.got_ref, bf16[24,48,128]{2,1,0:T(8,128)(2,1)S(1)} %copy-done, f32[1,128]{1,0:T(1,128)S(1)} %bitcast.27, bf16[4,128]{1,0:T(4,128)(2,1)S(1)} %bitcast.30), custom_call_target="tpu_custom_call" | custom-call | tf_op jit(solution)/shard_map/finish/pallas_call | solution.py:547
  98.3 4.6 %all-to-all-start.4 = ((f32[128,5,2,128]{3,2,1,0:T(2,128)}), f32[128,5,2,128]{3,2,1,0:T(2,128)S(1)}, u32[]{:S(2)}, u32[]{:S(2)}) async-start(f32[128,5,2,128]{3,2,1,0:T(2,128)} %get-tuple-element.25), calls=%async_computation.4 | async-start | bytes 1310720 | tf_op jit(solution)/shard_map/all_to_all | solution.py:36
  102.9 1.8 %output.1 = (bf16[24,48,128]{2,1,0:T(8,128)(2,1)}, f32[24,48,128]{2,1,0:T(8,128)}) custom-call(bf16[16,24,1024]{2,1,0:T(8,128)(2,1)S(1)} %all_to_all.26.got_ref, f32[1152,128]{1,0:T(8,128)S(1)} %get-tuple-element.22.d_normed_ref, bf16[24,48,128]{2,1,0:T(8,128)(2,1)S(1)} %copy-done, f32[1,128]{1,0:T(1,128)S(1)} %bitcast.28), custom_call_target="tpu_custom_call" | custom-call | tf_op jit(solution)/shard_map/output/pallas_call | solution.py:556
  104.7 13.0 %all-to-all-done.4.got_ref = f32[128,5,2,128]{3,2,1,0:T(2,128)S(1)} async-done(((f32[128,5,2,128]{3,2,1,0:T(2,128)}), f32[128,5,2,128]{3,2,1,0:T(2,128)S(1)}, u32[]{:S(2)}, u32[]{:S(2)}) %all-to-all-start.4) | async-done | bytes 655392 | tf_op jit(solution)/shard_map/all_to_all | solution.py:36
  117.7 1.2 gather.1
  (26 shorter events, 0.9 us)
Async XLA Ops:
  27.6 6.7 %slice-start = ((bf16[5,128,128]{2,1,0:T(8,128)(2,1)}), bf16[4,128,128]{2,1,0:T(8,128)(2,1)S(1)}, s32[]{:S(2)}) async-start(bf16[5,128,128]{2,1,0:T(8,128)(2,1)} %param.8), calls=%async_computation.5 | async-start | bytes 262144 | tf_op jit(solution)/shard_map/slice | solution.py:495
  27.6 21.5 %all-to-all-start.1 = ((f32[8,96,384]{2,1,0:T(8,128)}), f32[8,96,384]{2,1,0:T(8,128)S(1)}, u32[]{:S(2)}, u32[]{:S(2)}) async-start(f32[8,96,384]{2,1,0:T(8,128)} %bias_out.1), calls=%async_computation.1 | async-start | bytes 2359296 | tf_op jit(solution)/shard_map/all_to_all | solution.py:36
  32.8 4.9 %slice-start.1 = ((bf16[5,128,128]{2,1,0:T(8,128)(2,1)}), bf16[1,128,128]{2,1,0:T(8,128)(2,1)S(1)}, s32[]{:S(2)}) async-start(bf16[5,128,128]{2,1,0:T(8,128)(2,1)} %param.8), calls=%async_computation.6 | async-start | bytes 65536 | tf_op jit(solution)/shard_map/slice | solution.py:496
  32.8 4.9 %collective-permute-start = (bf16[384,1152]{1,0:T(8,128)(2,1)S(1)}, bf16[384,1152]{1,0:T(8,128)(2,1)S(1)}, u32[]{:S(2)}, u32[]{:S(2)}) collective-permute-start(bf16[384,1152]{1,0:T(8,128)(2,1)S(1)} %bitcast.22), channel_id=1, source_target_pairs={{0,8},{8,0},{1,9},{9,1},{2,10},{10,2},{3,11},{11,3},{4,12},{12,4},... | collective-permute-start | bytes 2654216 | tf_op jit(solution)/shard_map/ppermute | solution.py:541
  40.0 1.4 %copy-start.1 = (bf16[3,384,1024]{2,1,0:T(8,128)(2,1)}, bf16[3,384,1024]{2,1,0:T(8,128)(2,1)S(1)}, u32[]{:S(2)}) copy-start(bf16[3,384,1024]{2,1,0:T(8,128)(2,1)S(1)} %get-tuple-element.17.upright_at) | copy-start | bytes 7077892
  41.5 1.0 copy-start.2
  42.5 1.0 copy-start.3
  60.9 4.6 %copy-start.6 = (bf16[4,64,128]{2,1,0:T(8,128)(2,1)S(1)}, bf16[4,64,128]{2,1,0:T(8,128)(2,1)}, u32[]{:S(2)}) copy-start(bf16[4,64,128]{2,1,0:T(8,128)(2,1)} %get-tuple-element.29) | copy-start | bytes 196612
  61.0 4.6 %copy-start.7 = (bf16[4,64,128]{2,1,0:T(8,128)(2,1)S(1)}, bf16[4,64,128]{2,1,0:T(8,128)(2,1)}, u32[]{:S(2)}) copy-start(bf16[4,64,128]{2,1,0:T(8,128)(2,1)} %get-tuple-element.30) | copy-start | bytes 196612
  61.0 4.7 %collective-permute-start.1 = (bf16[3,384,640]{2,1,0:T(8,128)(2,1)S(1)}, bf16[3,384,640]{2,1,0:T(8,128)(2,1)}, u32[]{:S(2)}, u32[]{:S(2)}) collective-permute-start(bf16[3,384,640]{2,1,0:T(8,128)(2,1)S(1)} %get-tuple-element.21.acts_ref), channel_id=1, source_target_pairs={{0,8},{8,0},{1,9},{9,1},{2,10},{10,2},{3,11},{11,3},{4,12},{12,4},... | collective-permute-start | bytes 4423688 | tf_op jit(solution)/shard_map/ppermute | solution.py:545
  61.9 14.6 %all-to-all-start.2 = ((bf16[8,112,384]{2,1,0:T(8,128)(2,1)}), bf16[8,112,384]{2,1,0:T(8,128)(2,1)S(1)}, u32[]{:S(2)}, u32[]{:S(2)}) async-start(bf16[8,112,384]{2,1,0:T(8,128)(2,1)} %get-tuple-element.20), calls=%async_computation.2 | async-start | bytes 1376256 | tf_op jit(solution)/shard_map/all_to_all | solution.py:36
  77.0 19.1 %copy-start = (bf16[24,48,128]{2,1,0:T(8,128)(2,1)S(1)}, bf16[24,48,128]{2,1,0:T(8,128)(2,1)}, u32[]{:S(2)}) copy-start(bf16[24,48,128]{2,1,0:T(8,128)(2,1)} %pair_ref.1) | copy-start | bytes 884740
  77.0 19.1 %copy-start.4 = (f32[128]{0:T(128)S(1)}, f32[128]{0:T(128)}, u32[]{:S(2)}) copy-start(f32[128]{0:T(128)} %param.7) | copy-start | bytes 1540
  77.0 19.1 %copy-start.5 = (bf16[128,4]{0,1:T(4,128)(2,1)S(1)}, bf16[128,4]{0,1:T(4,128)(2,1)}, u32[]{:S(2)}) copy-start(bf16[128,4]{0,1:T(4,128)(2,1)} %param.9) | copy-start | bytes 3076
  98.3 19.4 %all-to-all-start.4 = ((f32[128,5,2,128]{3,2,1,0:T(2,128)}), f32[128,5,2,128]{3,2,1,0:T(2,128)S(1)}, u32[]{:S(2)}, u32[]{:S(2)}) async-start(f32[128,5,2,128]{3,2,1,0:T(2,128)} %get-tuple-element.25), calls=%async_computation.4 | async-start | bytes 1310720 | tf_op jit(solution)/shard_map/all_to_all | solution.py:36

commit v8 on v7

--- a/solution.py
+++ b/solution.py
@@ -535,6 +535,7 @@
         bias_out_kernel,
         in_specs=[vmem],
         out_shape=shape((n_col, high, lanes), F32),
+        compiler_params=pltpu.CompilerParams(vmem_limit_bytes=24 << 20),
         name="bias_out",
     )(resident(both))
     got = pltpu.with_memory_space_constraint(exchange(spread, COL), pltpu.VMEM)
@@ -566,6 +567,7 @@
         in_specs=[vmem],
         out_shape=[shape(projections.shape, F32), shape((heads, channels), F32), shape((1, channels), F32)],
         scratch_shapes=[pltpu.VMEM((2, 5 * half, channels), F32)],
+        compiler_params=pltpu.CompilerParams(vmem_limit_bytes=24 << 20),
         name="gather",
     )(everyone)
     return (attended, pair_gradient, projection_grad, bias_weight_grad.T, gain_gradient[0])

time: 119 us -> 120 us (level); the launches traced: 119 us -> 118 us
  no operation moved by 1% of the time
where the time goes in v8:
time: 120 us; the launch traced here: 118 us
  blocking collectives  42.5 us (35%)
  waiting for transfers between devices  26.4 us (22%)
  Pallas kernels  25.2 us (21%)
  starting transfers between devices  15.8 us (13%)
  local copies, waits for them, and re-layouts  5.55 us (5%)
  between operations  1.48 us (1%)
    all_to_all x2, blocking collectives, exchange(): return lax.all_to_all(value, axes, split_axis=0, concat_axis=0, tiled=True)  42.5 us
    all_to_all x3, waiting for transfers between devices, exchange(): return lax.all_to_all(value, axes, split_axis=0, concat_axis=0, tiled=True)  26.4 us
    all_to_all x3, starting transfers between devices, exchange(): return lax.all_to_all(value, axes, split_axis=0, concat_axis=0, tiled=True)  13.3 us
    pallas_call x1, Pallas kernels, attend(): pl.pallas_call(attention_kernel, grid=(columns,), in_specs=[pl.BlockSpec(...  10.7 us
    unnamed x17, local copies, waits for them, and re-layouts  3.64 us
    pallas_call x1, Pallas kernels, merge(): pl.pallas_call(merge_kernel, grid=(columns,), in_specs=[block, block, pl....  2.99 us
  transfers between devices with their start and end apart: 5, of which 3 were waited for; matrix products, arithmetic and copies ran while one was open for 2% of the time, Pallas kernels for 6%

profile of v8, /device:TPU:1, one launch (start us, length us, event | category | flops | bytes accessed | tf_op | source)
XLA Modules:
  0.0 117.8 jit_solution(9610367563843472096)
XLA Ops:
  0.6 2.2 %pack.1 = bf16[16,24,1152]{2,1,0:T(8,128)(2,1)S(1)} custom-call(bf16[24,48,128]{2,1,0:T(8,128)(2,1)} %pair_ref.1, bf16[24,48,128]{2,1,0:T(8,128)(2,1)} %cot_at.1, f32[1,128]{1,0:T(1,128)} %bitcast.26, bf16[4,128]{1,0:T(4,128)(2,1)} %bitcast.29), custom_call_target="tpu_custom_call" | custom-call | tf_op jit(solution)/shard_map/pack/pallas_call | solution.py:517
  2.9 23.4 %all_to_all.25 = bf16[16,24,1152]{2,1,0:T(8,128)(2,1)S(1)} all-to-all(bf16[16,24,1152]{2,1,0:T(8,128)(2,1)S(1)} %pack.1), channel_id=1, replica_groups=mesh['row_0'=2,'row_1'=4,'row_2'=2,'col_0'=2,'col_1'=4] {'row_0','row_1'..., dimensions={0} | all-to-all | bytes 1769472 | tf_op jit(solution)/shard_map/all_to_all | solution.py:36
  26.3 1.4 %bias_out.1 = f32[8,96,384]{2,1,0:T(8,128)} custom-call(bf16[384,1152]{1,0:T(8,128)(2,1)S(1)} %bitcast.21), custom_call_target="tpu_custom_call" | custom-call | tf_op jit(solution)/shard_map/bias_out/pallas_call | solution.py:534
  27.6 5.2 %all-to-all-start.1 = ((f32[8,96,384]{2,1,0:T(8,128)}), f32[8,96,384]{2,1,0:T(8,128)S(1)}, u32[]{:S(2)}, u32[]{:S(2)}) async-start(f32[8,96,384]{2,1,0:T(8,128)} %bias_out.1), calls=%async_computation.1 | async-start | bytes 2359296 | tf_op jit(solution)/shard_map/all_to_all | solution.py:36
  32.8 1.5 %collective-permute-start = (bf16[384,1152]{1,0:T(8,128)(2,1)S(1)}, bf16[384,1152]{1,0:T(8,128)(2,1)S(1)}, u32[]{:S(2)}, u32[]{:S(2)}) collective-permute-start(bf16[384,1152]{1,0:T(8,128)(2,1)S(1)} %bitcast.22), channel_id=1, source_target_pairs={{0,8},{8,0},{1,9},{9,1},{2,10},{10,2},{3,11},{11,3},{4,12},{12,4},... | collective-permute-start | bytes 2654216 | tf_op jit(solution)/shard_map/ppermute | solution.py:542
  34.5 0.7 dynamic-slice_bitcast_fusion.1
  35.2 0.7 fusion.6
  35.9 1.1 copy.16.w_ref
  37.8 2.2 %project.1 = (bf16[3,384,1024]{2,1,0:T(8,128)(2,1)S(1)}, bf16[3,512,384]{2,1,0:T(8,128)(2,1)S(1)}, f32[3,256,384]{2,1,0:T(8,128)S(1)}) custom-call(bf16[384,1152]{1,0:T(8,128)(2,1)S(1)} %bitcast.23, bf16[384,1152]{1,0:T(8,128)(2,1)S(1)} %collective-permute-done.twin_normed_ref.twin_cot_ref, bf16[384,1152]{1,0:T(8,128)(2,1)S(1)} %bitcast.24, ...), custom_call_target="tpu_custom_call" | custom-call | tf_op jit(solution)/shard_map/project/pallas_call | solution.py:163
  40.0 1.4 %copy-done.1 = bf16[3,384,1024]{2,1,0:T(8,128)(2,1)} copy-done((bf16[3,384,1024]{2,1,0:T(8,128)(2,1)}, bf16[3,384,1024]{2,1,0:T(8,128)(2,1)S(1)}, u32[]{:S(2)}) %copy-start.1) | copy-done | bytes 2359320
  41.5 1.0 copy-done.2
  42.5 1.0 copy-done.3
  43.5 5.6 %all-to-all-done.1.got_ref = f32[8,96,384]{2,1,0:T(8,128)S(1)} async-done(((f32[8,96,384]{2,1,0:T(8,128)}), f32[8,96,384]{2,1,0:T(8,128)S(1)}, u32[]{:S(2)}, u32[]{:S(2)}) %all-to-all-start.1) | async-done | bytes 1179680 | tf_op jit(solution)/shard_map/all_to_all | solution.py:36
  49.1 10.7 %attention.1 = (bf16[3,384,640]{2,1,0:T(8,128)(2,1)S(1)}, bf16[8,112,384]{2,1,0:T(8,128)(2,1)}) custom-call(s32[1]{0:T(128)S(6)} %copy.19.valid_ref, f32[8,96,384]{2,1,0:T(8,128)S(1)} %all-to-all-done.1.got_ref, bf16[3,384,1024]{2,1,0:T(8,128)(2,1)} %copy-done.1, bf16[3,512,384]{2,1,0:T(8,128)(2,1)} %copy-done.2, f32[3,256,384]{2,1,0:T(8,128)} %copy-done.3), custom_call_target="tpu_custom_call" | custom-call | tf_op jit(solution)/shard_map/attention/pallas_call | solution.py:301
  59.8 0.9 collective-permute-start.1
  60.8 3.5 %all-to-all-start.2 = ((bf16[8,112,384]{2,1,0:T(8,128)(2,1)}), bf16[8,112,384]{2,1,0:T(8,128)(2,1)S(1)}, u32[]{:S(2)}, u32[]{:S(2)}) async-start(bf16[8,112,384]{2,1,0:T(8,128)(2,1)} %get-tuple-element.20), calls=%async_computation.2 | async-start | bytes 1376256 | tf_op jit(solution)/shard_map/all_to_all | solution.py:36
  64.6 3.0 %merge.1 = bf16[384,1024]{1,0:T(8,128)(2,1)S(1)} custom-call(bf16[3,384,640]{2,1,0:T(8,128)(2,1)S(1)} %get-tuple-element.21.acts_ref, bf16[3,384,640]{2,1,0:T(8,128)(2,1)} %collective-permute-done.1.came_ref, bf16[5,256,128]{2,1,0:T(8,128)(2,1)S(1)} %maximum_maximum_fusion.w_ref), custom_call_target="tpu_custom_call" | custom-call | tf_op jit(solution)/shard_map/merge/pallas_call | solution.py:347
  67.6 7.8 %all-to-all-done.2.got_ref = bf16[8,112,384]{2,1,0:T(8,128)(2,1)S(1)} async-done(((bf16[8,112,384]{2,1,0:T(8,128)(2,1)}), bf16[8,112,384]{2,1,0:T(8,128)(2,1)S(1)}, u32[]{:S(2)}, u32[]{:S(2)}) %all-to-all-start.2) | async-done | bytes 688160 | tf_op jit(solution)/shard_map/all_to_all | solution.py:36
  75.9 19.1 %all_to_all.26.got_ref = bf16[16,24,1024]{2,1,0:T(8,128)(2,1)S(1)} all-to-all(bf16[16,24,1024]{2,1,0:T(8,128)(2,1)S(1)} %sum.1), channel_id=1, replica_groups=mesh['row_0'=2,'row_1'=4,'row_2'=2,'col_0'=2,'col_1'=4] {'row_0','row_1'..., dimensions={0} | all-to-all | bytes 1572864 | tf_op jit(solution)/shard_map/all_to_all | solution.py:36
  95.0 2.2 %finish.1 = (f32[1152,128]{1,0:T(8,128)S(1)}, f32[128,5,2,128]{3,2,1,0:T(2,128)}) custom-call(s32[1]{0:T(128)} %bitcast.12.core_ref, bf16[16,24,1024]{2,1,0:T(8,128)(2,1)S(1)} %all_to_all.26.got_ref, bf16[24,48,128]{2,1,0:T(8,128)(2,1)S(1)} %copy-done, f32[1,128]{1,0:T(1,128)S(1)} %bitcast.27, bf16[4,128]{1,0:T(4,128)(2,1)S(1)} %bitcast.30), custom_call_target="tpu_custom_call" | custom-call | tf_op jit(solution)/shard_map/finish/pallas_call | solution.py:548
  97.2 4.6 %all-to-all-start.4 = ((f32[128,5,2,128]{3,2,1,0:T(2,128)}), f32[128,5,2,128]{3,2,1,0:T(2,128)S(1)}, u32[]{:S(2)}, u32[]{:S(2)}) async-start(f32[128,5,2,128]{3,2,1,0:T(2,128)} %get-tuple-element.25), calls=%async_computation.4 | async-start | bytes 1310720 | tf_op jit(solution)/shard_map/all_to_all | solution.py:36
  101.7 1.8 %output.1 = (bf16[24,48,128]{2,1,0:T(8,128)(2,1)}, f32[24,48,128]{2,1,0:T(8,128)}) custom-call(bf16[16,24,1024]{2,1,0:T(8,128)(2,1)S(1)} %all_to_all.26.got_ref, f32[1152,128]{1,0:T(8,128)S(1)} %get-tuple-element.22.d_normed_ref, bf16[24,48,128]{2,1,0:T(8,128)(2,1)S(1)} %copy-done, f32[1,128]{1,0:T(1,128)S(1)} %bitcast.28), custom_call_target="tpu_custom_call" | custom-call | tf_op jit(solution)/shard_map/output/pallas_call | solution.py:557
  103.6 13.0 %all-to-all-done.4.got_ref = f32[128,5,2,128]{3,2,1,0:T(2,128)S(1)} async-done(((f32[128,5,2,128]{3,2,1,0:T(2,128)}), f32[128,5,2,128]{3,2,1,0:T(2,128)S(1)}, u32[]{:S(2)}, u32[]{:S(2)}) %all-to-all-start.4) | async-done | bytes 655392 | tf_op jit(solution)/shard_map/all_to_all | solution.py:36
  116.6 1.2 gather.1
  (26 shorter events, 0.9 us)
Async XLA Ops:
  27.6 6.7 %slice-start = ((bf16[5,128,128]{2,1,0:T(8,128)(2,1)}), bf16[4,128,128]{2,1,0:T(8,128)(2,1)S(1)}, s32[]{:S(2)}) async-start(bf16[5,128,128]{2,1,0:T(8,128)(2,1)} %param.8), calls=%async_computation.5 | async-start | bytes 262144 | tf_op jit(solution)/shard_map/slice | solution.py:495
  27.6 21.5 %all-to-all-start.1 = ((f32[8,96,384]{2,1,0:T(8,128)}), f32[8,96,384]{2,1,0:T(8,128)S(1)}, u32[]{:S(2)}, u32[]{:S(2)}) async-start(f32[8,96,384]{2,1,0:T(8,128)} %bias_out.1), calls=%async_computation.1 | async-start | bytes 2359296 | tf_op jit(solution)/shard_map/all_to_all | solution.py:36
  32.8 4.9 %slice-start.1 = ((bf16[5,128,128]{2,1,0:T(8,128)(2,1)}), bf16[1,128,128]{2,1,0:T(8,128)(2,1)S(1)}, s32[]{:S(2)}) async-start(bf16[5,128,128]{2,1,0:T(8,128)(2,1)} %param.8), calls=%async_computation.6 | async-start | bytes 65536 | tf_op jit(solution)/shard_map/slice | solution.py:496
  32.8 4.9 %collective-permute-start = (bf16[384,1152]{1,0:T(8,128)(2,1)S(1)}, bf16[384,1152]{1,0:T(8,128)(2,1)S(1)}, u32[]{:S(2)}, u32[]{:S(2)}) collective-permute-start(bf16[384,1152]{1,0:T(8,128)(2,1)S(1)} %bitcast.22), channel_id=1, source_target_pairs={{0,8},{8,0},{1,9},{9,1},{2,10},{10,2},{3,11},{11,3},{4,12},{12,4},... | collective-permute-start | bytes 2654216 | tf_op jit(solution)/shard_map/ppermute | solution.py:542
  40.0 1.4 %copy-start.1 = (bf16[3,384,1024]{2,1,0:T(8,128)(2,1)}, bf16[3,384,1024]{2,1,0:T(8,128)(2,1)S(1)}, u32[]{:S(2)}) copy-start(bf16[3,384,1024]{2,1,0:T(8,128)(2,1)S(1)} %get-tuple-element.17.upright_at) | copy-start | bytes 7077892
  41.5 1.0 copy-start.2
  42.5 1.0 copy-start.3
  59.8 4.6 %copy-start.6 = (bf16[4,64,128]{2,1,0:T(8,128)(2,1)S(1)}, bf16[4,64,128]{2,1,0:T(8,128)(2,1)}, u32[]{:S(2)}) copy-start(bf16[4,64,128]{2,1,0:T(8,128)(2,1)} %get-tuple-element.29) | copy-start | bytes 196612
  59.8 4.6 %copy-start.7 = (bf16[4,64,128]{2,1,0:T(8,128)(2,1)S(1)}, bf16[4,64,128]{2,1,0:T(8,128)(2,1)}, u32[]{:S(2)}) copy-start(bf16[4,64,128]{2,1,0:T(8,128)(2,1)} %get-tuple-element.30) | copy-start | bytes 196612
  59.8 4.7 %collective-permute-start.1 = (bf16[3,384,640]{2,1,0:T(8,128)(2,1)S(1)}, bf16[3,384,640]{2,1,0:T(8,128)(2,1)}, u32[]{:S(2)}, u32[]{:S(2)}) collective-permute-start(bf16[3,384,640]{2,1,0:T(8,128)(2,1)S(1)} %get-tuple-element.21.acts_ref), channel_id=1, source_target_pairs={{0,8},{8,0},{1,9},{9,1},{2,10},{10,2},{3,11},{11,3},{4,12},{12,4},... | collective-permute-start | bytes 4423688 | tf_op jit(solution)/shard_map/ppermute | solution.py:546
  60.8 14.6 %all-to-all-start.2 = ((bf16[8,112,384]{2,1,0:T(8,128)(2,1)}), bf16[8,112,384]{2,1,0:T(8,128)(2,1)S(1)}, u32[]{:S(2)}, u32[]{:S(2)}) async-start(bf16[8,112,384]{2,1,0:T(8,128)(2,1)} %get-tuple-element.20), calls=%async_computation.2 | async-start | bytes 1376256 | tf_op jit(solution)/shard_map/all_to_all | solution.py:36
  75.9 19.1 %copy-start = (bf16[24,48,128]{2,1,0:T(8,128)(2,1)S(1)}, bf16[24,48,128]{2,1,0:T(8,128)(2,1)}, u32[]{:S(2)}) copy-start(bf16[24,48,128]{2,1,0:T(8,128)(2,1)} %pair_ref.1) | copy-start | bytes 884740
  75.9 19.1 %copy-start.4 = (f32[128]{0:T(128)S(1)}, f32[128]{0:T(128)}, u32[]{:S(2)}) copy-start(f32[128]{0:T(128)} %param.7) | copy-start | bytes 1540
  75.9 19.1 %copy-start.5 = (bf16[128,4]{0,1:T(4,128)(2,1)S(1)}, bf16[128,4]{0,1:T(4,128)(2,1)}, u32[]{:S(2)}) copy-start(bf16[128,4]{0,1:T(4,128)(2,1)} %param.9) | copy-start | bytes 3076
  97.2 19.4 %all-to-all-start.4 = ((f32[128,5,2,128]{3,2,1,0:T(2,128)}), f32[128,5,2,128]{3,2,1,0:T(2,128)S(1)}, u32[]{:S(2)}, u32[]{:S(2)}) async-start(f32[128,5,2,128]{3,2,1,0:T(2,128)} %get-tuple-element.25), calls=%async_computation.4 | async-start | bytes 1310720 | tf_op jit(solution)/shard_map/all_to_all | solution.py:36
